TPU v7x, 32 devices: a whole 2x2x4 slice. The times are simulated.
32 devices in a mesh: dp: 4 (over y, x), expert: 8 (over z, core).
Axes of the slice: x: 2, y: 2, z: 4, core: 2. Of those that a mesh axis runs over, the one named last changes fastest.
Arguments:
- conv_cache: float32 [128, 3, 16384], P('dp', None, 'expert'), may hold values from -6 to 6
- state_cache: float32 [128, 16, 16384], P('dp', None, 'expert'), may hold values from -6 to 6
- send_slot: int32 [4, 4, 8], replicated, may hold values from 0 to 31, as said below
- recv_row: int32 [4, 4, 8], P('dp'), may hold values from 0 to 31, as said below
- prefix_length: int32 [128], P('dp'), may hold values from 1 to 4
- x_input: bfloat16 [2, 128, 16384], P(None, 'dp', 'expert'), may hold values from -6 to 6
- z_input: bfloat16 [2, 128, 16384], P(None, 'dp', 'expert'), may hold values from -6 to 6
- dt_input: bfloat16 [2, 128, 16384], P(None, 'dp', 'expert'), may hold values from -6 to 6
- b_input: float32 [2, 128, 16], P(None, 'dp'), may hold values from -6 to 6
- c_input: float32 [2, 128, 16], P(None, 'dp'), may hold values from -4 to 4
- conv_weight: float32 [4, 16384], P(None, 'expert'), may hold values from -3 to 3
- conv_bias: float32 [16384], P('expert'), may hold values from -3 to 3
- dt_bias: float32 [16384], P('expert'), may hold values from -3 to 1
- decay_rate: float32 [16, 16384], P(None, 'expert'), may hold values from 0.02 to 4
- skip_gain: float32 [16384], P('expert'), may hold values from 0.5 to 1.5
- out_weight: bfloat16 [16384, 8192], P('expert', 'dp'), may hold values from -0.046875 to 0.046875
- norm_gain: float32 [8192], replicated, may hold values from 0.25 to 1.75
- route_ids: int32 [2, 128, 2], replicated, may hold values from 0 to 15, all different within a row; in each aligned block of 256 rows (0 to 255, 256 to 511, ..., all dimensions but the last counted through in order) at most 64 rows name the same one
- route_weight: float32 [2, 128, 2], replicated, may hold values from 0.2 to 1
- expert_slots: int32 [4], replicated, may hold values from 0 to 15, as said below
- gate_weight: bfloat16 [8192, 49152], P(None, ('dp', 'expert')), may hold values from -0.0625 to 0.0625
- up_weight: bfloat16 [8192, 49152], P(None, ('dp', 'expert')), may hold values from -0.0625 to 0.0625
- down_weight: bfloat16 [49152, 8192], P(('dp', 'expert')), may hold values from -0.0546875 to 0.0546875
Outputs:
- mixed: bfloat16 [256, 8192], P(('dp', 'expert'))
- new_state: float32 [128, 16, 16384], P('dp', None, 'expert')
- new_tail: float32 [128, 3, 16384], P('dp', None, 'expert')
Inputs may be any that keep to these rules, and one draw needn't show every extreme that they name: For each owner o, send_slot[o] holds every local slot 0 to 31 exactly once. For each index d, recv_row[d] holds every local row 0 to 31 exactly once. `route_ids`: over both steps and all rows, no expert is named by more than 64 rows, and one is named by exactly 64. `expert_slots`: distinct expert ids; experts 0 and 15 are always among them, in slots that vary.
All inputs are finite; a program needn't handle non-finite values.
Results may differ from a plain program's by a relative error of at most 0.0057.
Values may be sent and summed in bfloat16 or wider, within the bound.
No kernel may reach another device: no remote copies, remote signals or barrier semaphores. Data moves between devices by JAX's collectives and lax.ppermute only.
A program may use at most 256 MiB of HBM per device.

v0:
```python
import jax
import jax.numpy as jnp
from jax import lax
from jax.sharding import PartitionSpec as P

FFW = 12288


def body(
    conv_cache,
    state_cache,
    send_slot,
    recv_row,
    prefix_length,
    x_input,
    z_input,
    dt_input,
    b_input,
    c_input,
    conv_weight,
    conv_bias,
    dt_bias,
    decay_rate,
    skip_gain,
    out_weight,
    norm_gain,
    route_ids,
    route_weight,
    expert_slots,
    gate_weight,
    up_weight,
    down_weight,
):
    dp_count = lax.axis_size("dp")
    exp_count = lax.axis_size("expert")
    dp_place = lax.axis_index("dp")
    exp_place = lax.axis_index("expert")
    rows_here = x_input.shape[1]
    channels = x_input.shape[2]
    taps = conv_cache.shape[1]
    states = state_cache.shape[1]
    receive_list = recv_row[0].reshape(-1)
    mine = lax.dynamic_index_in_dim(send_slot, dp_place, 0, keepdims=False).reshape(-1)
    packed_tail = conv_cache[mine].reshape(dp_count, -1, taps, channels)
    packed_state = state_cache[mine].reshape(dp_count, -1, states, channels)
    got_tail, got_state = (
        lax.all_to_all(packed_tail, "dp", split_axis=0, concat_axis=0, tiled=True),
        lax.all_to_all(packed_state, "dp", split_axis=0, concat_axis=0, tiled=True),
    )
    inverse = (
        jnp.zeros((rows_here,), jnp.int32)
        .at[receive_list]
        .set(jnp.arange(rows_here, dtype=jnp.int32))
    )
    tail = got_tail.reshape(rows_here, taps, channels)[inverse]
    state = got_state.reshape(rows_here, states, channels)[inverse]
    offsets = taps - jnp.arange(taps, dtype=jnp.int32)
    valid = (offsets[None, :] <= prefix_length[:, None]).astype(jnp.float32)
    tail = tail * valid[:, :, None]
    outputs = []
    for step in range(x_input.shape[0]):
        window = jnp.concatenate([tail, x_input[step].astype(jnp.float32)[:, None, :]], axis=1)
        xc = jax.nn.silu(jnp.sum(window * conv_weight[None], axis=1) + conv_bias)
        tail = window[:, 1:, :]
        delta = jax.nn.softplus(dt_input[step].astype(jnp.float32) + dt_bias)
        state = (
            jnp.exp(-delta[:, None, :] * decay_rate[None]) * state
            + (delta * xc)[:, None, :] * b_input[step][:, :, None]
        )
        out_y = jnp.sum(c_input[step][:, :, None] * state, axis=1) + skip_gain * xc
        out_y = out_y * jax.nn.silu(z_input[step].astype(jnp.float32))
        outputs.append(out_y.astype(jnp.bfloat16))
    y_local = jnp.stack(outputs)
    partial_out = jnp.einsum(
        "trc,cd->trd",
        lax.all_gather(y_local, "dp", axis=1, tiled=True),
        out_weight,
        preferred_element_type=jnp.float32,
    )
    flat_part = partial_out.reshape(-1, partial_out.shape[2])
    column_part = lax.psum(flat_part, "expert").astype(jnp.bfloat16)
    hidden = lax.all_gather(column_part, "dp", axis=1, tiled=True)
    hidden_f = hidden.astype(jnp.float32)
    normed = (
        hidden_f
        * lax.rsqrt(jnp.mean(hidden_f * hidden_f, axis=-1, keepdims=True) + 1e-05)
        * norm_gain
    ).astype(jnp.bfloat16)
    total_rows = hidden.shape[0]
    ids = route_ids.reshape(total_rows, -1)
    weights = route_weight.reshape(total_rows, -1)
    share = jnp.sum(
        weights[:, :, None] * (ids[:, :, None] == expert_slots[None, None, :]).astype(jnp.float32),
        axis=1,
    )
    width_here = gate_weight.shape[1]
    linear_place = dp_place * exp_count + exp_place
    my_slot = linear_place * width_here // FFW
    slot_mask = (jnp.arange(expert_slots.shape[0], dtype=jnp.int32) == my_slot).astype(jnp.float32)
    my_share = jnp.sum(share * slot_mask[None, :], axis=1, keepdims=True)
    rows_mine = total_rows // (dp_count * exp_count)
    gated = jnp.dot(normed, gate_weight, preferred_element_type=jnp.float32)
    upped = jnp.dot(normed, up_weight, preferred_element_type=jnp.float32)
    act = (jax.nn.silu(gated) * upped * my_share).astype(jnp.bfloat16)
    summed = lax.psum_scatter(
        jnp.dot(act, down_weight, preferred_element_type=jnp.float32),
        ("dp", "expert"),
        scatter_dimension=0,
        tiled=True,
    )
    own_hidden = lax.dynamic_slice_in_dim(hidden_f, linear_place * rows_mine, rows_mine, 0)
    mixed = (own_hidden + summed).astype(jnp.bfloat16)
    return (mixed, state, tail)


def solution(mesh):
    in_specs = (
        P("dp", None, "expert"),
        P("dp", None, "expert"),
        P(),
        P("dp", None, None),
        P("dp"),
        P(None, "dp", "expert"),
        P(None, "dp", "expert"),
        P(None, "dp", "expert"),
        P(None, "dp", None),
        P(None, "dp", None),
        P(None, "expert"),
        P("expert"),
        P("expert"),
        P(None, "expert"),
        P("expert"),
        P("expert", "dp"),
        P(),
        P(),
        P(),
        P(),
        P(None, ("dp", "expert")),
        P(None, ("dp", "expert")),
        P(("dp", "expert"), None),
    )
    out_specs = (P(("dp", "expert"), None), P("dp", None, "expert"), P("dp", None, "expert"))
    return jax.shard_map(body, mesh=mesh, in_specs=in_specs, out_specs=out_specs, check_vma=False)
```

profile of v0, /device:TPU:0, one launch (start us, length us, event | category | flops | bytes accessed | tf_op | source)
XLA Modules:
  0.0 441.8 jit_solution(2541765381131850697)
XLA Ops:
  7.2 0.8 reshape_squeeze.3
  8.0 0.7 constant_dynamic-slice_fusion
  8.8 1.7 gather_fusion.2
  10.5 0.9 copy.61
  11.5 5.2 %all-to-all-start.1 = ((f32[4,8,3,2048]{3,1,2,0:T(8,128)}), f32[4,8,3,2048]{3,1,2,0:T(8,128)S(1)}, u32[]{:S(2)}, u32[]{:S(2)}) async-start(f32[4,8,3,2048]{3,1,2,0:T(8,128)} %copy.61), calls=%async_computation.1 | async-start | bytes 1572864 | tf_op jit(solution)/shard_map/all_to_all | solution.py:47
  16.8 5.0 %gather_fusion = f32[32,16,2048]{2,1,0:T(8,128)} fusion(f32[32,16,2048]{2,1,0:T(8,128)} %param.24, s32[1024]{0:T(1024)S(1)} %pad_clamp_fusion.1), kind=kCustom, calls=%fused_computation | custom fusion | bytes 8388736 | tf_op jit(solution)/shard_map/gather | solution.py:45
  21.8 5.6 %all-to-all-done.1 = f32[4,8,3,2048]{3,1,2,0:T(8,128)S(1)} async-done(((f32[4,8,3,2048]{3,1,2,0:T(8,128)}), f32[4,8,3,2048]{3,1,2,0:T(8,128)S(1)}, u32[]{:S(2)}, u32[]{:S(2)}) %all-to-all-start.1) | async-done | bytes 786464 | tf_op jit(solution)/shard_map/all_to_all | solution.py:47
  27.5 5.0 %all-to-all-start = ((f32[4,8,16,2048]{3,2,1,0:T(8,128)}), f32[4,8,16,2048]{3,2,1,0:T(8,128)}, u32[]{:S(2)}, u32[]{:S(2)}) async-start(f32[4,8,16,2048]{3,2,1,0:T(8,128)} %bitcast.69), calls=%async_computation | async-start | bytes 8388608 | tf_op jit(solution)/shard_map/all_to_all | solution.py:48
  32.8 0.7 scatter_custom_fusion
  34.0 0.5 copy.62
  34.6 1.2 gather_fusion.3
  36.0 0.6 fusion.16
  36.6 1.0 copy-done.3
  37.7 2.1 fusion.15
  39.8 0.5 multiply_multiply_fusion.1
  40.2 39.1 %all-to-all-done = f32[4,8,16,2048]{3,2,1,0:T(8,128)} async-done(((f32[4,8,16,2048]{3,2,1,0:T(8,128)}), f32[4,8,16,2048]{3,2,1,0:T(8,128)}, u32[]{:S(2)}, u32[]{:S(2)}) %all-to-all-start) | async-done | bytes 4194336 | tf_op jit(solution)/shard_map/all_to_all | solution.py:48
  79.3 5.0 %gather_fusion.1 = f32[32,16,2048]{2,1,0:T(8,128)} fusion(f32[32,16,2048]{2,1,0:T(8,128)} %bitcast.4, s32[1024]{0:T(1024)S(1)} %pad_clamp_fusion), kind=kCustom, calls=%fused_computation.1 | custom fusion | bytes 8388736 | tf_op jit(solution)/shard_map/gather | solution.py:56
  84.4 6.6 %multiply_reduce_fusion.1 = (f32[32,2048]{1,0:T(8,128)S(1)}, f32[32,16,2048]{2,1,0:T(8,128)}, f32[32,2048]{1,0:T(8,128)S(1)}) fusion(f32[32,16]{1,0:T(8,128)S(1)} %copy.66, f32[32,16]{1,0:T(8,128)S(1)} %copy.68, f32[32,2048]{1,0:T(8,128)S(1)} %get-tuple-element.23, f32[32,16]{1,0:T(8,128)S(1)} %copy.65, f32[32,2048]{1,0:T(8,128)S(1)} %get-tuple-element.22, ...), kind=kLoop, calls=%fused_computation.9 | loop fusion | flops 12451840 | bytes 10100736 | tf_op jit(solution)/shard_map/reduce_sum | solution.py:70
  91.2 0.7 pad_maximum_fusion.2
  92.2 26.9 %all-gather.3.cloned.1.call-done = bf16[2,128,2048]{2,1,0:T(8,128)(2,1)} async-done(((bf16[2,32,2048]{2,1,0:T(8,128)(2,1)}), bf16[2,128,2048]{2,1,0:T(8,128)(2,1)}) %all-gather.3.cloned.1.call-update) | async-done | bytes 1048592 | tf_op jit(solution)/shard_map/all_gather | solution.py:76
  119.1 6.0 %fusion = f32[2,128,2048]{2,1,0:T(8,128)S(1)} fusion(bf16[2,128,2048]{2,1,0:T(8,128)(2,1)} %all-gather.3.cloned.1.call-done, bf16[2048,2048]{1,0:T(8,128)(2,1)} %param.38), kind=kOutput, calls=%fused_computation.5 | convolution fusion | flops 2147483648 | bytes 11534336 | tf_op jit(solution)/shard_map/trc,cd->trd/dot_general | solution.py:74
  125.2 64.5 %all-reduce.1 = bf16[256,2048]{1,0:T(8,128)(2,1)} all-reduce(f32[256,2048]{1,0:T(8,128)S(1)} %bitcast.72), channel_id=1, replica_groups=mesh['dp'=4,'expert'=8] {'expert'}, use_global_device_ids=true, to_apply=%region_5.6 | all-reduce | flops 524288 | bytes 3145728 | tf_op jit(solution)/shard_map/psum | solution.py:81
  190.0 50.7 %all-gather.5.cloned.1.call-done = bf16[256,8192]{1,0:T(8,128)(2,1)} async-done(((bf16[256,2048]{1,0:T(8,128)(2,1)}), bf16[256,8192]{1,0:T(8,128)(2,1)}) %all-gather.5.cloned.1.call-update) | async-done | bytes 4194320 | tf_op jit(solution)/shard_map/all_gather | solution.py:82
  240.6 3.3 multiply_reduce_fusion
  244.1 11.9 %fusion.10 = f32[256,1536]{1,0:T(8,128)S(1)} fusion(bf16[8192,1536]{1,0:T(8,128)(2,1)} %param.43, f32[8192]{0:T(1024)S(1)} %copy-done.21, f32[256]{0:T(256)S(1)} %add_rsqrt_fusion, bf16[256,8192]{1,0:T(8,128)(2,1)S(1)} %copy-done.2), kind=kOutput, calls=%fused_computation.26 | convolution fusion | flops 6450839552 | bytes 30966784 | tf_op jit(solution)/shard_map/dot_general | solution.py:102
  256.0 25.6 %fusion.4 = f32[256,8192]{1,0:T(8,128)} fusion(bf16[1536,8192]{1,0:T(8,128)(2,1)} %param.45, bf16[8192,1536]{1,0:T(8,128)(2,1)} %param.44, f32[256,1536]{1,0:T(8,128)S(1)} %fusion.10, f32[8192]{0:T(1024)S(1)} %copy-done.21, f32[256]{0:T(256)S(1)} %add_rsqrt_fusion, bf16[256,8192]{1,0:T(8,128)(2,1)} %all-gather.5.cloned.1.call-done, ...), kind=kOutput, calls=%fused_computation.16 | convolution fusion | flops 12896043008 | bytes 64522240 | tf_op jit(solution)/shard_map/dot_general | solution.py:106
  281.6 1.2 copy-done.4
  282.9 0.6 fusion.13
  283.4 1.3 copy.69
  284.8 6.4 %convert_element_type.112 = f32[256,8192]{1,0:T(8,128)} convert(bf16[256,8192]{1,0:T(8,128)(2,1)} %all-gather.5.cloned.1.call-done) | non-fusion elementwise | flops 2097152 | bytes 12582912 | tf_op jit(solution)/shard_map/convert_element_type | solution.py:83
  291.2 142.4 %reduce-scatter.2.cloned.1.call-done = f32[8,8192]{1,0:T(8,128)} async-done(((f32[256,8192]{1,0:T(8,128)}), f32[8,8192]{1,0:T(8,128)}) %reduce-scatter.2.cloned.1.call-update) | async-done | bytes 262160 | tf_op jit(solution)/shard_map/reduce_scatter | solution.py:105
  433.5 1.7 add_convert_fusion
  (71 shorter events, 2.4 us)
Async XLA Ops:
  7.2 1.6 copy-start
  8.8 7.8 %copy-start.20 = (s32[32]{0:T(128)S(1)}, s32[32]{0:T(128)}, u32[]{:S(2)}) copy-start(s32[32]{0:T(128)} %param.27) | copy-start | bytes 388
  11.5 16.0 %all-to-all-start.1 = ((f32[4,8,3,2048]{3,1,2,0:T(8,128)}), f32[4,8,3,2048]{3,1,2,0:T(8,128)S(1)}, u32[]{:S(2)}, u32[]{:S(2)}) async-start(f32[4,8,3,2048]{3,1,2,0:T(8,128)} %copy.61), calls=%async_computation.1 | async-start | bytes 1572864 | tf_op jit(solution)/shard_map/all_to_all | solution.py:47
  27.5 5.0 %copy-start.13 = (f32[2,32,16]{1,2,0:T(8,128)S(1)}, f32[2,32,16]{1,2,0:T(8,128)}, u32[]{:S(2)}) copy-start(f32[2,32,16]{1,2,0:T(8,128)} %param.31) | copy-start | bytes 12292
  27.5 5.2 %copy-start.14 = (f32[2,32,16]{1,2,0:T(8,128)S(1)}, f32[2,32,16]{1,2,0:T(8,128)}, u32[]{:S(2)}) copy-start(f32[2,32,16]{1,2,0:T(8,128)} %param.32) | copy-start | bytes 12292
  27.5 6.1 %copy-start.9 = (bf16[2,32,2048]{2,1,0:T(8,128)(2,1)S(1)}, bf16[2,32,2048]{2,1,0:T(8,128)(2,1)}, u32[]{:S(2)}) copy-start(bf16[2,32,2048]{2,1,0:T(8,128)(2,1)} %param.28) | copy-start | bytes 786436
  27.5 51.9 %all-to-all-start = ((f32[4,8,16,2048]{3,2,1,0:T(8,128)}), f32[4,8,16,2048]{3,2,1,0:T(8,128)}, u32[]{:S(2)}, u32[]{:S(2)}) async-start(f32[4,8,16,2048]{3,2,1,0:T(8,128)} %bitcast.69), calls=%async_computation | async-start | bytes 8388608 | tf_op jit(solution)/shard_map/all_to_all | solution.py:48
  32.5 86.6 %all-gather.3.cloned.1.call-start = ((), (), s32[]{:S(2)}) async-start(), calls=%async_computation.3 | async-start | bytes 1310720 | tf_op jit(solution)/shard_map/all_gather | solution.py:76
  34.0 2.6 copy-start.5
  34.0 3.7 copy-start.11
  35.8 4.0 copy-start.7
  35.8 4.0 copy-start.12
  35.8 4.0 copy-start.15
  36.6 1.1 copy-start.3
  79.3 5.1 %copy-start.10 = (f32[16,2048]{1,0:T(8,128)S(1)}, f32[16,2048]{1,0:T(8,128)}, u32[]{:S(2)}) copy-start(f32[16,2048]{1,0:T(8,128)} %param.36) | copy-start | bytes 393220
  84.4 6.6 %copy-start.8 = (bf16[2,32,2048]{2,1,0:T(8,128)(2,1)S(1)}, bf16[2,32,2048]{2,1,0:T(8,128)(2,1)}, u32[]{:S(2)}) copy-start(bf16[2,32,2048]{2,1,0:T(8,128)(2,1)} %param.29) | copy-start | bytes 786436
  84.4 6.6 %copy-start.16 = (f32[2048]{0:T(1024)S(1)}, f32[2048]{0:T(1024)}, u32[]{:S(2)}) copy-start(f32[2048]{0:T(1024)} %param.37) | copy-start | bytes 24580
  92.0 148.6 %all-gather.5.cloned.1.call-start = ((), (), s32[]{:S(2)}) async-start(), calls=%async_computation.4 | async-start | bytes 5242880 | tf_op jit(solution)/shard_map/all_gather | solution.py:82
  125.1 64.6 %copy-start.17 = (f32[2,128,2]{1,2,0:T(2,128)S(1)}, f32[2,128,2]{1,2,0:T(2,128)}, u32[]{:S(2)}) copy-start(f32[2,128,2]{1,2,0:T(2,128)} %param.41) | copy-start | bytes 6148
  125.1 64.6 %copy-start.18 = (s32[2,128,2]{1,2,0:T(2,128)S(1)}, s32[2,128,2]{1,2,0:T(2,128)}, u32[]{:S(2)}) copy-start(s32[2,128,2]{1,2,0:T(2,128)} %param.40) | copy-start | bytes 6148
  125.2 64.6 %copy-start.19 = (s32[4]{0:T(128)S(1)}, s32[4]{0:T(128)}, u32[]{:S(2)}) copy-start(s32[4]{0:T(128)} %param.42) | copy-start | bytes 52
  125.2 118.7 %copy-start.21 = (f32[8192]{0:T(1024)S(1)}, f32[8192]{0:T(1024)}, u32[]{:S(2)}) copy-start(f32[8192]{0:T(1024)} %param.39) | copy-start | bytes 98308
  189.7 243.9 %reduce-scatter.2.cloned.1.call-start = ((), (), s32[]{:S(2)}) async-start(), calls=%async_computation.5 | async-start | bytes 8650752 | tf_op jit(solution)/shard_map/reduce_scatter | solution.py:105
  240.6 3.4 copy-start.2
  281.6 1.2 copy-start.4
  281.6 1.3 copy-start.6
  283.4 151.8 %copy-start.1 = (f32[32,3,2048]{2,0,1:T(8,128)S(1)}, f32[32,3,2048]{2,0,1:T(8,128)}, u32[]{:S(2)}) copy-start(f32[32,3,2048]{2,0,1:T(8,128)} %param.23) | copy-start | bytes 2359300
Sparse Core Ops, SparseCore 0:
  92.1 26.9 all-gather.2
  189.8 50.7 all-gather.4
  281.7 151.7 reduce-scatter.1
where the time goes:
time: 442 us
  waiting for transfers between devices  265 us (60%)
  blocking collectives  64.5 us (15%)
  matrix products  43.6 us (10%)
  other arithmetic  23.5 us (5%)
  local copies, waits for them, and re-layouts  21 us (5%)
  between operations  14.1 us (3%)
  starting transfers between devices  10.5 us (2%)
    reduce_scatter x1, waiting for transfers between devices, body(): lax.psum_scatter(jnp.dot(act, down_weight, preferred_element_type=jnp.flo...  142 us
    psum x1, blocking collectives, body(): column_part = lax.psum(flat_part, 'expert').astype(jnp.bfloat16)  64.5 us
    all_gather x1, waiting for transfers between devices, body(): hidden = lax.all_gather(column_part, 'dp', axis=1, tiled=True)  50.7 us
    all_to_all x1, waiting for transfers between devices, body(): lax.all_to_all(packed_state, 'dp', split_axis=0, concat_axis=0, tiled=True)  39.1 us
    all_gather x1, waiting for transfers between devices, body(): lax.all_gather(y_local, 'dp', axis=1, tiled=True)  26.9 us
    dot_general x1, matrix products, body(): jnp.dot(act, down_weight, preferred_element_type=jnp.float32)  25.6 us
    dot_general x1, matrix products, body(): gated = jnp.dot(normed, gate_weight, preferred_element_type=jnp.float32)  11.9 us
  transfers between devices with their start and end apart: 5, of which 5 were waited for; matrix products, arithmetic and copies ran while one was open for 5% of the time, Pallas kernels for 0%

commit v1 on v0

v1 whole, which is shorter than its diff:
```python
import functools

import jax
import jax.numpy as jnp
from jax import lax
from jax.experimental import pallas as pl
from jax.experimental.pallas import tpu as pltpu
from jax.sharding import Mesh
from jax.sharding import PartitionSpec as P

FFW = 12288
BF = jnp.bfloat16
F32 = jnp.float32
META = 256
TABLE = 96
PREFIX = 64
NT = (((1,), (1,)), ((), ()))
TN = (((0,), (0,)), ((), ()))


def cost(flops, moved):
    return pl.CostEstimate(flops=int(flops), bytes_accessed=int(moved), transcendentals=0)


def params(limit):
    return pltpu.CompilerParams(vmem_limit_bytes=limit << 20)


def iota(shape, dim):
    return lax.broadcasted_iota(jnp.int32, shape, dim)


def trade(piece, axis, size, k):
    return lax.ppermute(piece, axis, [(i, i ^ k) for i in range(size)])


def pack_kernel(n, per, me, rr, x, z, dt, b, c, prefix, *rest):
    outs, m_scr = rest[:n], rest[n]
    steps, rows, ch = x.shape
    states = b.shape[1]
    m_scr[...] = jnp.zeros_like(m_scr)
    for t in range(steps):
        m_scr[2 * t * states : (2 * t + 1) * states, :] = b[t]
        m_scr[(2 * t + 1) * states : (2 * t + 2) * states, :] = c[t]
    m_scr[PREFIX : PREFIX + 1, :] = prefix[...].astype(F32)
    rowcol = jnp.zeros((n * per, 1), jnp.int32)
    table = jnp.zeros((1, 128), F32)
    sub = iota((n * per, 1), 0)
    lane = iota((1, 128), 1)
    for k in range(n):
        for i in range(per):
            rowcol = jnp.where(sub == k * per + i, rr[(me[0] ^ k) * per + i], rowcol)
            q = k * per + i
            table = jnp.where(lane == TABLE + q, rr[q].astype(F32), table)
    hot = rowcol == iota((n * per, rows), 1)
    hot_b = hot.astype(BF)
    for a, src in enumerate((x, z, dt)):
        for t in range(steps):
            got = jnp.dot(hot_b, src[t], preferred_element_type=F32).astype(BF)
            at = (a * steps + t) * ch
            for k in range(n):
                outs[k][:, at : at + ch] = got[k * per : (k + 1) * per]
    meta = lax.dot_general(
        hot.astype(F32), m_scr[...], NT, precision=lax.Precision.HIGHEST, preferred_element_type=F32
    )
    meta = meta + table
    hi = meta.astype(BF)
    lo = (meta - hi.astype(F32)).astype(BF)
    at = 3 * steps * ch
    for k in range(n):
        outs[k][:, at : at + 128] = hi[k * per : (k + 1) * per]
        outs[k][:, at + 128 : at + 256] = lo[k * per : (k + 1) * per]


def ssm_kernel(k, n, per, steps, me, ss, *refs):
    arrs = refs[: 3 * steps]
    meta, par, decay, conv = refs[3 * steps : 3 * steps + 4]
    state = refs[3 * steps + 4 : 3 * steps + 4 + per]
    y_out, st_out, y_scr, tail_scr = refs[-4:]
    taps = conv.shape[0]
    states, cb = decay.shape
    val = meta[:, :128].astype(F32) + meta[:, 128:].astype(F32)
    val_t = jnp.transpose(jnp.concatenate([val, jnp.zeros((128 - per, 128), F32)], axis=0))
    base = (me[0] * n + (me[0] ^ k)) * per
    for j in range(taps):
        for i in range(per):
            tail_scr[j, i : i + 1, :] = conv[j, pl.ds(ss[base + i], 1), :]
    prefix = val[:, PREFIX : PREFIX + 1]
    window = [
        tail_scr[j] * (prefix >= float(taps - j)).astype(F32) for j in range(taps)
    ]
    deltas, us, skips, gates = [], [], [], []
    for t in range(steps):
        window.append(arrs[t][...].astype(F32))
        acc = window[t] * par[0:1, :]
        for j in range(1, taps + 1):
            acc = acc + window[t + j] * par[j : j + 1, :]
        acc = acc + par[taps + 1 : taps + 2, :]
        xc = acc * jax.nn.sigmoid(acc)
        raw = arrs[2 * steps + t][...].astype(F32) + par[taps + 2 : taps + 3, :]
        delta = jnp.maximum(raw, 0.0) + jnp.log1p(jnp.exp(-jnp.abs(raw)))
        zt = arrs[steps + t][...].astype(F32)
        deltas.append(delta)
        us.append(delta * xc)
        skips.append(par[taps + 3 : taps + 4, :] * xc)
        gates.append(zt * jax.nn.sigmoid(zt))
    dec = decay[...]
    for i in range(per):
        st = state[i][0]
        for t in range(steps):
            at = 2 * t * states
            bcol = val_t[at : at + states, i : i + 1]
            ccol = val_t[at + states : at + 2 * states, i : i + 1]
            st = jnp.exp(-(deltas[t][i : i + 1] * dec)) * st + us[t][i : i + 1] * bcol
            y_scr[t, i : i + 1, :] = jnp.sum(ccol * st, axis=0, keepdims=True)
        st_out[i * states : (i + 1) * states, :] = st.astype(st_out.dtype)
    for t in range(steps):
        out = (y_scr[t] + skips[t]) * gates[t]
        y_out[0, t * per : (t + 1) * per, :] = out.astype(BF)
    kept = window[steps:taps]
    low = st_out.shape[0] - per * states
    kept.append(jnp.zeros((low - per * len(kept), cb), F32))
    st_out[per * states :, :] = jnp.concatenate(kept, axis=0).astype(st_out.dtype)


def drop_first(fn):
    return lambda me, ss, alias, *refs: fn(me, ss, *refs)


def ssm(k, n, per, steps, me, ss, payload, par, decay, conv, state, y_buf):
    states, ch = decay.shape
    cb = ch // 4
    blocks = ch // cb
    taps = conv.shape[0]
    low = -(-(taps - steps) * per // 16) * 16
    specs = [
        pl.BlockSpec((per, cb), functools.partial(lambda a, g, *_: (0, a * blocks + g), a))
        for a in range(3 * steps)
    ]
    specs.append(pl.BlockSpec((per, META), lambda g, *_: (0, 3 * steps * ch // META)))
    specs.append(pl.BlockSpec((par.shape[0], cb), lambda g, *_: (0, g)))
    specs.append(pl.BlockSpec((states, cb), lambda g, *_: (0, g)))
    specs.append(pl.BlockSpec((taps, conv.shape[1], cb), lambda g, *_: (0, 0, g)))
    for i in range(per):
        specs.append(
            pl.BlockSpec(
                (1, states, cb),
                functools.partial(
                    lambda i, g, m, s: (s[(m[0] * n + (m[0] ^ k)) * per + i], 0, g), i
                ),
            )
        )
    args = [payload] * (3 * steps + 1) + [par, decay, conv] + [state] * per
    body = functools.partial(ssm_kernel, k, n, per, steps)
    alias = {}
    if y_buf is not None:
        specs = [pl.BlockSpec(memory_space=pl.ANY)] + specs
        args = [y_buf] + args
        body = drop_first(body)
        alias = {2: 0}
    st_type = F32 if k == 0 else BF
    return pl.pallas_call(
        body,
        grid_spec=pltpu.PrefetchScalarGridSpec(
            num_scalar_prefetch=2,
            grid=(blocks,),
            in_specs=specs,
            out_specs=[
                pl.BlockSpec((1, steps * per, cb), lambda g, *_: (k, 0, g)),
                pl.BlockSpec((per * states + low, cb), lambda g, *_: (0, g)),
            ],
            scratch_shapes=[
                pltpu.VMEM((steps, per, cb), F32),
                pltpu.VMEM((taps, per, cb), F32),
            ],
        ),
        out_shape=[
            jax.ShapeDtypeStruct((n, steps * per, ch), BF),
            jax.ShapeDtypeStruct((per * states + low, ch), st_type),
        ],
        input_output_aliases=alias,
        compiler_params=params(24),
        cost_estimate=cost(3e6, 3 << 20),
        name=f"ssm{k}",
    )(me, ss, *args)


def select_kernel(n, m, per, steps, rows, rm, pe, width, me, es, ids, wts, *refs):
    tables = refs[:n]
    sel, share, expand = refs[n:]
    cores = m * 2
    d, zz, cc = me[0], me[1], me[2]
    total = steps * n * rows
    choices = ids.shape[0]
    sub8 = iota((8, total), 0)
    match = jnp.zeros((8, total), F32)
    own_share = jnp.zeros((1, total), F32)
    hits = []
    for kd in range(n):
        eid = es[((d ^ kd) * (cores * width)) // FFW]
        hit = jnp.zeros((1, total), F32)
        for q in range(choices):
            same = ids[q : q + 1, :] == eid
            hit = jnp.where(same, 1.0, hit)
            if kd == 0:
                own_share = own_share + jnp.where(same, wts[q : q + 1, :], 0.0)
        hits.append(hit)
        match = jnp.where(sub8 == kd, hit, match)
    before = (iota((total, total), 0) < iota((total, total), 1)).astype(BF)
    pos = jnp.dot(match.astype(BF), before, preferred_element_type=F32)
    pos = jnp.where(match > 0.0, pos, -1.0)
    col = iota((pe, 1), 0)
    parts = []
    for h in range(2):
        for kz in range(m):
            first = ((zz ^ kz) * 2 + (cc ^ h)) * pe
            want = (col + first).astype(F32)
            for kd in range(n):
                parts.append((pos[kd : kd + 1, :] == want).astype(BF))
        row = iota((m * n * rm, 1), 0)
        kz_v = row // (n * rm)
        kd_v = (row // rm) % n
        true = ((d ^ kd_v) * cores + (zz ^ kz_v) * 2 + (cc ^ h)) * rm + row % rm
        parts.append((true == iota((m * n * rm, total), 1)).astype(BF))
    sel_true = jnp.concatenate(parts, axis=0)
    j = iota((total, 1), 0)
    ko = j // (n * steps * per)
    kd = (j // (steps * per)) % n
    tab = jnp.zeros((8, 128), F32)
    for q in range(n):
        tab = jnp.where(iota((8, 128), 0) == q, tables[q][0:1, :].astype(F32), tab)
    pick = (iota((total, 8), 1) == (ko ^ kd)).astype(BF)
    tj = jnp.dot(pick, tab.astype(BF), preferred_element_type=F32)
    lane = TABLE + (d ^ ko) * per + j % per
    local = jnp.sum(jnp.where(iota((total, 128), 1) == lane, tj, 0.0), axis=1, keepdims=True)
    true = ((j // per) % steps) * (n * rows) + (d ^ ko ^ kd) * rows + local.astype(jnp.int32)
    perm = (true == iota((total, total), 1)).astype(BF)
    sel[...] = lax.dot_general(sel_true, perm, NT, preferred_element_type=F32).astype(BF)
    hot = pos[0:1, :] == iota((cores * pe, 1), 0).astype(F32)
    expand[...] = hot.astype(BF)
    mine = jnp.sum(jnp.where(hot, own_share, 0.0), axis=1, keepdims=True)
    share[...] = jnp.broadcast_to(mine, share.shape)


def project_kernel(n, counts, *refs):
    ys = refs[:n]
    sel, w = refs[n], refs[n + 1]
    outs = refs[n + 2 : n + 2 + len(counts)]
    y_all, y_sel = refs[-2:]

    @pl.when(pl.program_id(0) == 0)
    def _():
        size = ys[0].shape[0]
        for q in range(n):
            y_all[q * size : (q + 1) * size, :] = ys[q][...]
        y_sel[...] = jnp.dot(sel[...], y_all[...], preferred_element_type=F32).astype(BF)

    at = 0
    for out, count in zip(outs, counts):
        out[...] = jnp.dot(
            y_sel[at : at + count, :], w[...], preferred_element_type=F32
        ).astype(BF)
        at += count


def gate_kernel(pieces, me, *refs):
    xs = refs[:pieces]
    share, gw, uw, act, x_scr, g_acc, u_acc = refs[pieces:]
    g = pl.program_id(0)
    pe = xs[0].shape[0]

    @pl.when(g == 0)
    def _():
        first = me[2] == 0
        for kz in range(pieces // 2):
            own, other = xs[2 * kz][...].astype(F32), xs[2 * kz + 1][...].astype(F32)
            pair = jnp.concatenate(
                [jnp.where(first, own, other), jnp.where(first, other, own)], axis=0
            ).astype(BF)
            at = pl.multiple_of((me[1] ^ kz) * (2 * pe), 2 * pe)
            x_scr[pl.ds(at, 2 * pe), :] = pair
        g_acc[...] = jnp.zeros_like(g_acc)
        u_acc[...] = jnp.zeros_like(u_acc)

    kb = gw.shape[0]
    xk = x_scr[:, pl.ds(pl.multiple_of(g * kb, kb), kb)]
    g_acc[...] += jnp.dot(xk, gw[...], preferred_element_type=F32)
    u_acc[...] += jnp.dot(xk, uw[...], preferred_element_type=F32)

    @pl.when(g == pl.num_programs(0) - 1)
    def _():
        gated = g_acc[...]
        act[...] = (gated * jax.nn.sigmoid(gated) * u_acc[...] * share[:, 0:1]).astype(BF)


def down_kernel(me, act, dw, out):
    out[...] = jnp.dot(act[...], dw[...], preferred_element_type=F32).astype(BF)


def place_kernel(states, me, rr, src, *refs):
    out = refs[-1]
    out[0] = src[...].astype(F32)


def place(k, n, per, rows, states, me, rr, src, buf):
    ch = src.shape[1]
    specs = [pl.BlockSpec((states, ch), lambda i, *_: (i, 0))]
    args = [src]
    alias = {}
    if buf is not None:
        specs.append(pl.BlockSpec(memory_space=pl.ANY))
        args.append(buf)
        alias = {3: 0}
    return pl.pallas_call(
        functools.partial(place_kernel, states),
        grid_spec=pltpu.PrefetchScalarGridSpec(
            num_scalar_prefetch=2,
            grid=(per,),
            in_specs=specs,
            out_specs=pl.BlockSpec(
                (1, states, ch), lambda i, m, r: (r[(m[0] ^ k) * per + i], 0, 0)
            ),
        ),
        out_shape=jax.ShapeDtypeStruct((rows, states, ch), F32),
        input_output_aliases=alias,
        compiler_params=params(16),
        cost_estimate=cost(1e5, 2 << 20),
        name=f"place{k}",
    )(me, rr, *args)


def tail_kernel(n, per, taps, me, rr, x, *refs):
    tails, out = refs[:n], refs[n]
    steps = x.shape[0]
    keep = taps - steps
    for t in range(steps):
        out[keep + t] = x[t].astype(F32)
    for k in range(n):
        block = tails[k][...].astype(F32)
        for j in range(keep):
            for i in range(per):
                q = j * per + i
                out[j, pl.ds(rr[(me[0] ^ k) * per + i], 1), :] = block[q : q + 1, :]


def final_kernel(n, m, me, *refs):
    hid = refs[:n]
    parts = refs[n : n + 2 * m]
    out, acc = refs[-2:]
    wc = hid[0].shape[1]
    for k in range(n):
        acc[:, pl.ds(pl.multiple_of((me[0] ^ k) * wc, wc), wc)] = hid[k][...].astype(F32)
    pc = parts[0].shape[1]
    for q in range(2 * m):
        zs, cs = me[1] ^ (q // 2), me[2] ^ (q % 2)
        where = pl.ds(pl.multiple_of((cs * m + zs) * pc, pc), pc)
        acc[:, where] = acc[:, where] + parts[q][...].astype(F32)
    out[...] = acc[...].astype(BF)


def body(
    conv_cache,
    state_cache,
    send_slot,
    recv_row,
    prefix_length,
    x_input,
    z_input,
    dt_input,
    b_input,
    c_input,
    conv_weight,
    conv_bias,
    dt_bias,
    decay_rate,
    skip_gain,
    out_weight,
    norm_gain,
    route_ids,
    route_weight,
    expert_slots,
    gate_weight,
    up_weight,
    down_weight,
):
    n = lax.axis_size("dp")
    m = lax.axis_size("z")
    d, zz, cc = lax.axis_index("dp"), lax.axis_index("z"), lax.axis_index("core")
    me = jnp.stack([d, zz, cc]).astype(jnp.int32)
    steps, rows, ch = x_input.shape
    per = rows // n
    taps = conv_cache.shape[1]
    states = state_cache.shape[1]
    total = steps * n * rows
    cap = total // 4
    pe = cap // (2 * m)
    rm = total // (n * 2 * m)
    width = gate_weight.shape[1]
    wc = out_weight.shape[1]
    dm = n * wc
    rr = recv_row.reshape(-1)
    ss = send_slot.reshape(-1)
    vm = pl.BlockSpec(memory_space=pltpu.VMEM)
    sm = pl.BlockSpec(memory_space=pltpu.SMEM)

    payload = pl.pallas_call(
        functools.partial(pack_kernel, n, per),
        in_specs=[sm, sm] + [vm] * 6,
        out_specs=[vm] * n,
        out_shape=[jax.ShapeDtypeStruct((per, 3 * steps * ch + META), BF)] * n,
        scratch_shapes=[pltpu.VMEM((128, rows), F32)],
        compiler_params=params(16),
        cost_estimate=cost(1e6, 2 << 20),
        name="pack",
    )(
        me,
        rr,
        x_input,
        z_input,
        dt_input,
        jnp.transpose(b_input, (0, 2, 1)),
        jnp.transpose(c_input, (0, 2, 1)),
        prefix_length.reshape(1, rows),
    )
    payload = [payload[0]] + [trade(payload[k], "dp", n, k) for k in range(1, n)]
    par = jnp.concatenate(
        [conv_weight, conv_bias[None], dt_bias[None], skip_gain[None], jnp.zeros((1, ch), F32)], 0
    )
    conv = jnp.transpose(conv_cache, (1, 0, 2))
    y_buf, kept = None, []
    for k in range(n):
        y_buf, st = ssm(
            k, n, per, steps, me, ss, payload[k], par, decay_rate, conv, state_cache, y_buf
        )
        kept.append(st)
    y_own = y_buf.reshape(n * steps * per, ch)
    ys = [y_own] + [trade(y_own, "dp", n, k) for k in range(1, n)]

    total_sel = 2 * m * n * (pe + rm)
    ids_t = route_ids.reshape(total, -1).T
    wts_t = route_weight.reshape(total, -1).T
    meta_at = 3 * steps * ch // 128
    sel, share, expand = pl.pallas_call(
        functools.partial(select_kernel, n, m, per, steps, rows, rm, pe, width),
        grid=(1,),
        in_specs=[sm, sm]
        + [pl.BlockSpec(ids_t.shape, lambda g: (0, 0))] * 2
        + [pl.BlockSpec((per, 128), lambda g: (0, meta_at))] * n,
        out_specs=[
            pl.BlockSpec((total_sel, total), lambda g: (0, 0)),
            pl.BlockSpec((cap, 128), lambda g: (0, 0)),
            pl.BlockSpec((cap, total), lambda g: (0, 0)),
        ],
        out_shape=[
            jax.ShapeDtypeStruct((total_sel, total), BF),
            jax.ShapeDtypeStruct((cap, 128), F32),
            jax.ShapeDtypeStruct((cap, total), BF),
        ],
        compiler_params=params(24),
        cost_estimate=cost(1e7, 1 << 20),
        name="select",
    )(me, expert_slots, ids_t, wts_t, *payload)

    counts = (m * n * pe, m * n * rm) * 2
    wb = wc // 4
    keep_slot, keep_own, send_slot_rows, send_own = pl.pallas_call(
        functools.partial(project_kernel, n, counts),
        grid=(wc // wb,),
        in_specs=[pl.BlockSpec(y_own.shape, lambda g: (0, 0))] * n
        + [
            pl.BlockSpec((total_sel, total), lambda g: (0, 0)),
            pl.BlockSpec((ch, wb), lambda g: (0, g)),
        ],
        out_specs=[pl.BlockSpec((count, wb), lambda g: (0, g)) for count in counts],
        out_shape=[jax.ShapeDtypeStruct((count, wc), BF) for count in counts],
        scratch_shapes=[pltpu.VMEM((total, ch), BF), pltpu.VMEM((total_sel, ch), BF)],
        compiler_params=params(40),
        cost_estimate=cost(5e9, 12 << 20),
        name="project",
    )(*ys, sel, out_weight)

    def reduce_rows(keep, send, each):
        both = keep.astype(F32) + trade(send, "core", 2, 1).astype(F32)
        both = both.reshape(m, n * each, wc)
        out = both[0]
        narrow = both.astype(BF)
        for k in range(1, m):
            out = out + trade(narrow[k], "z", m, k).astype(F32)
        out = out.astype(BF).reshape(n, each, wc)
        return [out[0]] + [trade(out[k], "dp", n, k) for k in range(1, n)]

    hid = reduce_rows(keep_slot, send_slot_rows, pe)
    wide = [h.astype(F32) for h in hid]
    square = sum(jnp.sum(h * h, axis=1, keepdims=True) for h in wide)
    scale = lax.rsqrt(square / dm + 1e-05)
    normed = jnp.concatenate(
        [
            (wide[k] * scale * lax.dynamic_slice_in_dim(norm_gain, (d ^ k) * wc, wc)[None]).astype(BF)
            for k in range(n)
        ],
        axis=1,
    )
    near = [normed] + [trade(normed, "z", m, k) for k in range(1, m)]
    xs = []
    for piece in near:
        xs += [piece, trade(piece, "core", 2, 1)]

    kb = min(512, wc)
    wide_k = wc // kb
    act = pl.pallas_call(
        functools.partial(gate_kernel, 2 * m),
        grid_spec=pltpu.PrefetchScalarGridSpec(
            num_scalar_prefetch=1,
            grid=(dm // kb,),
            in_specs=[pl.BlockSpec((pe, dm), lambda g, *_: (0, 0))] * (2 * m)
            + [pl.BlockSpec((cap, 128), lambda g, *_: (0, 0))]
            + [
                pl.BlockSpec(
                    (kb, width), lambda g, w: ((w[0] ^ (g // wide_k)) * wide_k + g % wide_k, 0)
                )
            ]
            * 2,
            out_specs=pl.BlockSpec((cap, width), lambda g, *_: (0, 0)),
            scratch_shapes=[
                pltpu.VMEM((cap, dm), BF),
                pltpu.VMEM((cap, width), F32),
                pltpu.VMEM((cap, width), F32),
            ],
        ),
        out_shape=jax.ShapeDtypeStruct((cap, width), BF),
        compiler_params=params(40),
        cost_estimate=cost(4 * cap * dm * width, 4 * dm * width),
        name="gate",
    )(me, *xs, share, gate_weight, up_weight)

    half = dm // 2
    pc = half // m

    def down(h):
        cb = min(pc, 1024)
        per_z = pc // cb
        return pl.pallas_call(
            down_kernel,
            grid_spec=pltpu.PrefetchScalarGridSpec(
                num_scalar_prefetch=1,
                grid=(half // cb,),
                in_specs=[
                    pl.BlockSpec((cap, width), lambda g, *_: (0, 0)),
                    pl.BlockSpec(
                        (width, cb),
                        lambda g, w: (
                            0,
                            ((w[2] ^ h) * m + (w[1] ^ (g // per_z))) * per_z + g % per_z,
                        ),
                    ),
                ],
                out_specs=pl.BlockSpec((cap, cb), lambda g, *_: (0, g)),
            ),
            out_shape=jax.ShapeDtypeStruct((cap, half), BF),
            compiler_params=params(32),
            cost_estimate=cost(2 * cap * half * width, 2 * half * width),
            name=f"down{h}",
        )(me, act, down_weight)

    far = trade(down(1), "core", 2, 1)
    both = down(0).astype(F32) + far.astype(F32)
    out = both[:, :pc]
    narrow = both.astype(BF)
    for k in range(1, m):
        out = out + trade(narrow[:, k * pc : (k + 1) * pc], "z", m, k).astype(F32)
    spread = lax.dot_general(expand, out.astype(BF), TN, preferred_element_type=F32).astype(BF)
    share_rows = total // n
    mine = lax.dynamic_slice_in_dim(spread, d * share_rows, share_rows, 0).astype(F32)
    for k in range(1, n):
        piece = lax.dynamic_slice_in_dim(spread, (d ^ k) * share_rows, share_rows, 0)
        mine = mine + trade(piece, "dp", n, k).astype(F32)
    mine = mine.astype(BF)
    parts = []
    for q in range(2 * m):
        at = ((zz ^ (q // 2)) * 2 + (cc ^ (q % 2))) * rm
        piece = lax.dynamic_slice_in_dim(mine, at, rm, 0)
        parts.append(piece if q == 0 else trade(piece, ("z", "core"), 2 * m, q))

    own = reduce_rows(keep_own, send_own, rm)
    mixed = pl.pallas_call(
        functools.partial(final_kernel, n, m),
        in_specs=[sm] + [vm] * (n + 2 * m),
        out_specs=vm,
        out_shape=jax.ShapeDtypeStruct((rm, dm), BF),
        scratch_shapes=[pltpu.VMEM((rm, dm), F32)],
        compiler_params=params(16),
        cost_estimate=cost(1e5, 1 << 19),
        name="final",
    )(me, *own, *parts)

    back = [kept[0]] + [trade(kept[k], "dp", n, k) for k in range(1, n)]
    new_state = None
    for k in range(n):
        new_state = place(k, n, per, rows, states, me, rr, back[k], new_state)
    low = kept[0].shape[0] - per * states
    tail_at = per * states // low
    new_tail = pl.pallas_call(
        functools.partial(tail_kernel, n, per, taps),
        grid=(1,),
        in_specs=[sm, sm, pl.BlockSpec(x_input.shape, lambda g: (0, 0, 0))]
        + [pl.BlockSpec((low, ch), lambda g: (tail_at, 0))] * n,
        out_specs=pl.BlockSpec((taps, rows, ch), lambda g: (0, 0, 0)),
        out_shape=jax.ShapeDtypeStruct((taps, rows, ch), F32),
        compiler_params=params(16),
        cost_estimate=cost(1e5, 1 << 20),
        name="tail",
    )(me, rr, x_input, *back)
    return (mixed, new_state, jnp.transpose(new_tail, (1, 0, 2)))


def solution(mesh):
    n = mesh.shape["dp"]
    m = mesh.shape["expert"] // 2
    split = Mesh(mesh.devices.reshape(n, m, 2), ("dp", "z", "core"))
    e = ("z", "core")
    de = ("dp", "z", "core")
    in_specs = (
        P("dp", None, e),
        P("dp", None, e),
        P(),
        P("dp", None, None),
        P("dp"),
        P(None, "dp", e),
        P(None, "dp", e),
        P(None, "dp", e),
        P(None, "dp", None),
        P(None, "dp", None),
        P(None, e),
        P(e),
        P(e),
        P(None, e),
        P(e),
        P(e, "dp"),
        P(),
        P(),
        P(),
        P(),
        P(None, de),
        P(None, de),
        P(de, None),
    )
    out_specs = (P(de, None), P("dp", None, e), P("dp", None, e))
    return jax.shard_map(body, mesh=split, in_specs=in_specs, out_specs=out_specs, check_vma=False)
```

time: 442 us -> 205 us (0.46)
  waiting for transfers between devices: 265 us -> 61.4 us
  Pallas kernels: 0 us -> 74.8 us
  blocking collectives: 64.5 us -> 0 us
  matrix products: 43.6 us -> 0.32 us
  starting transfers between devices: 10.5 us -> 48.8 us
  other arithmetic: 23.5 us -> 3.43 us
  between operations: 14.1 us -> 1.02 us
  local copies, waits for them, and re-layouts: 21 us -> 14 us
    reduce_scatter x1 -> x0, waiting for transfers between devices: 142 us -> none  [body(): lax.psum_scatter(jnp.dot(act, down_weight, preferred_element_type=jnp.flo...]
    all_gather x2 -> x0, waiting for transfers between devices: 77.5 us -> none  [the longest x1 50.7 us: body(): hidden = lax.all_gather(column_part, 'dp', axis=1, tiled=True)]
    pallas_call x0 -> x16, Pallas kernels: none -> 74.8 us  [the longest x1 23.7 us: body(): pl.pallas_call(functools.partial(gate_kernel, 2 * m), grid_spec=pltpu.Pre...]
    psum x1 -> x0, blocking collectives: 64.5 us -> none  [body(): column_part = lax.psum(flat_part, 'expert').astype(jnp.bfloat16)]
    ppermute x0 -> x44, waiting for transfers between devices: none -> 61.4 us  [trade(): return lax.ppermute(piece, axis, [(i, i ^ k) for i in range(size)])]
    ppermute x0 -> x44, starting transfers between devices: none -> 48.8 us  [trade(): return lax.ppermute(piece, axis, [(i, i ^ k) for i in range(size)])]
    all_to_all x2 -> x0, waiting for transfers between devices: 44.7 us -> none  [the longest x1 39.1 us: body(): lax.all_to_all(packed_state, 'dp', split_axis=0, concat_axis=0, tiled=True)]
    dot_general x3 -> x1, matrix products: 43.6 us -> 0.32 us  [body(): lax.dot_general(expand, out.astype(BF), TN, preferred_element_type=F32)]
  transfers between devices with their start and end apart: 5 -> 44, of which waited for: 5 -> 19; matrix products, arithmetic and copies ran while one was open for 5% -> 2% of each run, Pallas kernels for 0% -> 31%
where the time goes in v1:
time: 205 us; the launch traced here: 204 us
  Pallas kernels  74.8 us (36%)
  waiting for transfers between devices  61.4 us (30%)
  starting transfers between devices  48.8 us (24%)
  local copies, waits for them, and re-layouts  14 us (7%)
  other arithmetic  3.43 us (2%)
    ppermute x44, waiting for transfers between devices, trade(): return lax.ppermute(piece, axis, [(i, i ^ k) for i in range(size)])  61.4 us
    ppermute x44, starting transfers between devices, trade(): return lax.ppermute(piece, axis, [(i, i ^ k) for i in range(size)])  48.8 us
    pallas_call x1, Pallas kernels, body(): pl.pallas_call(functools.partial(gate_kernel, 2 * m), grid_spec=pltpu.Pre...  23.7 us
    pallas_call x2, Pallas kernels, down(): pl.pallas_call(down_kernel, grid_spec=pltpu.PrefetchScalarGridSpec(num_sc...  13.8 us
    pallas_call x4, Pallas kernels, place(): pl.pallas_call(functools.partial(place_kernel, states), grid_spec=pltpu.P...  13.1 us
    pallas_call x4, Pallas kernels, ssm(): pl.pallas_call(body, grid_spec=pltpu.PrefetchScalarGridSpec(num_scalar_pr...  12.2 us
    unnamed x36, local copies, waits for them, and re-layouts  10 us
    pallas_call x1, Pallas kernels, body(): pl.pallas_call(functools.partial(project_kernel, n, counts), grid=(wc //...  7.26 us
  transfers between devices with their start and end apart: 44, of which 19 were waited for; matrix products, arithmetic and copies ran while one was open for 2% of the time, Pallas kernels for 31%

profile of v1, /device:TPU:0, one launch (start us, length us, event | category | flops | bytes accessed | tf_op | source)
XLA Modules:
  0.0 203.8 jit_solution(9754154408247732879)
XLA Ops:
  7.4 3.0 %collective-permute-start = (bf16[8,12544]{1,0:T(8,128)(2,1)S(1)}, bf16[8,12544]{1,0:T(8,128)(2,1)S(1)}, u32[]{:S(2)}, u32[]{:S(2)}) collective-permute-start(bf16[8,12544]{1,0:T(8,128)(2,1)S(1)} %get-tuple-element.24), channel_id=1, source_target_pairs={{0,8},{8,0},{16,24},{24,16},{1,9},{9,1},{17,25},{25,17},{2,10},{10... | collective-permute-start | bytes 602120 | tf_op jit(solution)/shard_map/ppermute | solution.py:34
  13.6 2.2 %copy-done = f32[32,16,2048]{2,1,0:T(8,128)S(1)} copy-done((f32[32,16,2048]{2,1,0:T(8,128)S(1)}, f32[32,16,2048]{2,1,0:T(8,128)}, u32[]{:S(2)}) %copy-start) | copy-done | bytes 4194328
  17.8 3.0 %ssm0.1 = (bf16[4,16,2048]{2,1,0:T(8,128)(2,1)S(1)}, f32[144,2048]{1,0:T(8,128)S(1)}) custom-call(s32[3]{0:T(128)S(1)} %pad_add_fusion.me, s32[128]{0:T(128)S(1)} %reshape.86.ss, bf16[8,12544]{1,0:T(8,128)(2,1)S(1)} %get-tuple-element.22.refs_0_.refs_1_.refs_2_.refs_3_.refs_4_.refs_5_.refs_6_, ...), custom_call_target="tpu_custom_call" | custom-call | flops 3000000 | bytes 3145728 | tf_op jit(solution)/shard_map/ssm0/pallas_call | solution.py:162
  20.9 3.1 %ssm1.1 = (bf16[4,16,2048]{2,1,0:T(8,128)(2,1)S(1)}, bf16[144,2048]{1,0:T(8,128)(2,1)S(1)}) custom-call(s32[3]{0:T(128)S(1)} %pad_add_fusion.me, s32[128]{0:T(128)S(1)} %reshape.86.ss, bf16[4,16,2048]{2,1,0:T(8,128)(2,1)S(1)} %get-tuple-element.23.alias, ...), custom_call_target="tpu_custom_call", output_to_operand_aliasing={{0}: (2, {})} | custom-call | flops 3000000 | bytes 3145728 | tf_op jit(solution)/shard_map/ssm1/pallas_call | solution.py:162
  23.9 3.1 %ssm2.1 = (bf16[4,16,2048]{2,1,0:T(8,128)(2,1)S(1)}, bf16[144,2048]{1,0:T(8,128)(2,1)S(1)}) custom-call(s32[3]{0:T(128)S(1)} %pad_add_fusion.me, s32[128]{0:T(128)S(1)} %reshape.86.ss, bf16[4,16,2048]{2,1,0:T(8,128)(2,1)S(1)} %get-tuple-element.25.alias, ...), custom_call_target="tpu_custom_call", output_to_operand_aliasing={{0}: (2, {})} | custom-call | flops 3000000 | bytes 3145728 | tf_op jit(solution)/shard_map/ssm2/pallas_call | solution.py:162
  27.8 3.1 %ssm3.1 = (bf16[4,16,2048]{2,1,0:T(8,128)(2,1)S(1)}, bf16[144,2048]{1,0:T(8,128)(2,1)S(1)}) custom-call(s32[3]{0:T(128)S(1)} %pad_add_fusion.me, s32[128]{0:T(128)S(1)} %reshape.86.ss, bf16[4,16,2048]{2,1,0:T(8,128)(2,1)S(1)} %get-tuple-element.27.alias, ...), custom_call_target="tpu_custom_call", output_to_operand_aliasing={{0}: (2, {})} | custom-call | flops 3000000 | bytes 3145728 | tf_op jit(solution)/shard_map/ssm3/pallas_call | solution.py:162
  30.9 3.0 %collective-permute-start.5 = (bf16[64,2048]{1,0:T(8,128)(2,1)S(1)}, bf16[64,2048]{1,0:T(8,128)(2,1)S(1)}, u32[]{:S(2)}, u32[]{:S(2)}) collective-permute-start(bf16[64,2048]{1,0:T(8,128)(2,1)S(1)} %bitcast.23), channel_id=1, source_target_pairs={{0,24},{8,16},{16,8},{24,0},{1,25},{9,17},{17,9},{25,1},{2,26},{10... | collective-permute-start | bytes 786440 | tf_op jit(solution)/shard_map/ppermute | solution.py:34
  35.6 5.6 %collective-permute-done.5.refs_3_ = bf16[64,2048]{1,0:T(8,128)(2,1)S(1)} collective-permute-done((bf16[64,2048]{1,0:T(8,128)(2,1)S(1)}, bf16[64,2048]{1,0:T(8,128)(2,1)S(1)}, u32[]{:S(2)}, u32[]{:S(2)}) %collective-permute-start.5) | collective-permute-done | bytes 262176 | tf_op jit(solution)/shard_map/ppermute | solution.py:34
  41.2 3.8 %collective-permute-done.4.refs_2_ = bf16[64,2048]{1,0:T(8,128)(2,1)S(1)} collective-permute-done((bf16[64,2048]{1,0:T(8,128)(2,1)S(1)}, bf16[64,2048]{1,0:T(8,128)(2,1)S(1)}, u32[]{:S(2)}, u32[]{:S(2)}) %collective-permute-start.4) | collective-permute-done | bytes 262176 | tf_op jit(solution)/shard_map/ppermute | solution.py:34
  45.3 7.3 %project.1 = (bf16[128,2048]{1,0:T(8,128)(2,1)S(1)}, bf16[128,2048]{1,0:T(8,128)(2,1)S(1)}, bf16[128,2048]{1,0:T(8,128)(2,1)S(1)}, bf16[128,2048]{1,0:T(8,128)(2,1)}) custom-call(bf16[64,2048]{1,0:T(8,128)(2,1)S(1)} %bitcast.26, bf16[64,2048]{1,0:T(8,128)(2,1)S(1)} %collective-permute-done.3.refs_1_, bf16[64,2048]{1,0:T(8,128)(2,1)S(1)} %collective-permute-done.4.refs_2_, ...), custom_call_target="tpu_custom_call" | custom-call | flops 5000000000 | bytes 12582912 | tf_op jit(solution)/shard_map/project/pallas_call | solution.py:466
  56.9 2.5 %collective-permute-start.16 = (bf16[32,2048]{1,0:T(8,128)(2,1)}, bf16[32,2048]{1,0:T(8,128)(2,1)}, u32[]{:S(2)}, u32[]{:S(2)}) collective-permute-start(bf16[32,2048]{1,0:T(8,128)(2,1)} %get-tuple-element.54), channel_id=1, source_target_pairs={{0,6},{2,4},{4,2},{6,0},{1,7},{3,5},{5,3},{7,1},{8,14},{10,12},{12... | collective-permute-start | bytes 393224 | tf_op jit(solution)/shard_map/ppermute | solution.py:34
  61.1 5.9 %collective-permute-done.16 = bf16[32,2048]{1,0:T(8,128)(2,1)} collective-permute-done((bf16[32,2048]{1,0:T(8,128)(2,1)}, bf16[32,2048]{1,0:T(8,128)(2,1)}, u32[]{:S(2)}, u32[]{:S(2)}) %collective-permute-start.16) | collective-permute-done | bytes 131104 | tf_op jit(solution)/shard_map/ppermute | solution.py:34
  67.0 4.8 %collective-permute-done.15 = bf16[32,2048]{1,0:T(8,128)(2,1)} collective-permute-done((bf16[32,2048]{1,0:T(8,128)(2,1)}, bf16[32,2048]{1,0:T(8,128)(2,1)}, u32[]{:S(2)}, u32[]{:S(2)}) %collective-permute-start.15) | collective-permute-done | bytes 131104 | tf_op jit(solution)/shard_map/ppermute | solution.py:34
  80.2 2.7 %collective-permute-start.25 = (bf16[8,8192]{1,0:T(8,128)(2,1)S(1)}, bf16[8,8192]{1,0:T(8,128)(2,1)S(1)}, u32[]{:S(2)}, u32[]{:S(2)}) collective-permute-start(bf16[8,8192]{1,0:T(8,128)(2,1)S(1)} %pad_maximum_fusion.refs_0_), channel_id=1, source_target_pairs={{0,6},{2,4},{4,2},{6,0},{1,7},{3,5},{5,3},{7,1},{8,14},{10,12},{12... | collective-permute-start | bytes 393224 | tf_op jit(solution)/shard_map/ppermute | solution.py:34
  85.2 3.1 %collective-permute-done.25.refs_6_ = bf16[8,8192]{1,0:T(8,128)(2,1)S(1)} collective-permute-done((bf16[8,8192]{1,0:T(8,128)(2,1)S(1)}, bf16[8,8192]{1,0:T(8,128)(2,1)S(1)}, u32[]{:S(2)}, u32[]{:S(2)}) %collective-permute-start.25) | collective-permute-done | bytes 131104 | tf_op jit(solution)/shard_map/ppermute | solution.py:34
  88.3 4.1 %collective-permute-done.23.refs_4_ = bf16[8,8192]{1,0:T(8,128)(2,1)S(1)} collective-permute-done((bf16[8,8192]{1,0:T(8,128)(2,1)S(1)}, bf16[8,8192]{1,0:T(8,128)(2,1)S(1)}, u32[]{:S(2)}, u32[]{:S(2)}) %collective-permute-start.23) | collective-permute-done | bytes 131104 | tf_op jit(solution)/shard_map/ppermute | solution.py:34
  95.1 23.7 %gate.1.act = bf16[64,1536]{1,0:T(8,128)(2,1)S(1)} custom-call(s32[3]{0:T(128)S(1)} %pad_add_fusion.me, bf16[8,8192]{1,0:T(8,128)(2,1)S(1)} %pad_maximum_fusion.refs_0_, bf16[8,8192]{1,0:T(8,128)(2,1)S(1)} %collective-permute-done.20.refs_1_, bf16[8,8192]{1,0:T(8,128)(2,1)S(1)} %collective-permute-done.21.refs_2_, ...), custom_call_target="tpu_custom_call" | custom-call | flops 3221225472 | bytes 50331648 | tf_op jit(solution)/shard_map/gate/pallas_call | solution.py:510
  118.8 6.9 %down1.1 = bf16[64,4096]{1,0:T(8,128)(2,1)S(1)} custom-call(s32[3]{0:T(128)S(1)} %pad_add_fusion.me, bf16[64,1536]{1,0:T(8,128)(2,1)S(1)} %gate.1.act, bf16[1536,8192]{1,0:T(8,128)(2,1)} %dw.3), custom_call_target="tpu_custom_call" | custom-call | flops 805306368 | bytes 12582912 | tf_op jit(solution)/shard_map/down1/pallas_call | solution.py:542
  127.0 6.9 %down0.1 = bf16[64,4096]{1,0:T(8,128)(2,1)S(1)} custom-call(s32[3]{0:T(128)S(1)} %pad_add_fusion.me, bf16[64,1536]{1,0:T(8,128)(2,1)S(1)} %gate.1.act, bf16[1536,8192]{1,0:T(8,128)(2,1)} %dw.3), custom_call_target="tpu_custom_call" | custom-call | flops 805306368 | bytes 12582912 | tf_op jit(solution)/shard_map/down0/pallas_call | solution.py:542
  134.2 2.2 %collective-permute-start.30 = (bf16[64,1024]{1,0:T(8,128)(2,1)S(1)}, bf16[64,1024]{1,0:T(8,128)(2,1)S(1)}, u32[]{:S(2)}, u32[]{:S(2)}) collective-permute-start(bf16[64,1024]{1,0:T(8,128)(2,1)S(1)} %get-tuple-element.51), channel_id=1, source_target_pairs={{0,6},{2,4},{4,2},{6,0},{1,7},{3,5},{5,3},{7,1},{8,14},{10,12},{12... | collective-permute-start | bytes 393224 | tf_op jit(solution)/shard_map/ppermute | solution.py:34
  137.7 2.4 %collective-permute-done.28 = bf16[64,1024]{1,0:T(8,128)(2,1)S(1)} collective-permute-done((bf16[64,1024]{1,0:T(8,128)(2,1)S(1)}, bf16[64,1024]{1,0:T(8,128)(2,1)S(1)}, u32[]{:S(2)}, u32[]{:S(2)}) %collective-permute-start.28) | collective-permute-done | bytes 131104 | tf_op jit(solution)/shard_map/ppermute | solution.py:34
  140.6 3.0 %collective-permute-done.30 = bf16[64,1024]{1,0:T(8,128)(2,1)S(1)} collective-permute-done((bf16[64,1024]{1,0:T(8,128)(2,1)S(1)}, bf16[64,1024]{1,0:T(8,128)(2,1)S(1)}, u32[]{:S(2)}, u32[]{:S(2)}) %collective-permute-start.30) | collective-permute-done | bytes 131104 | tf_op jit(solution)/shard_map/ppermute | solution.py:34
  145.3 7.9 %collective-permute-done.29 = bf16[64,1024]{1,0:T(8,128)(2,1)S(1)} collective-permute-done((bf16[64,1024]{1,0:T(8,128)(2,1)S(1)}, bf16[64,1024]{1,0:T(8,128)(2,1)S(1)}, u32[]{:S(2)}, u32[]{:S(2)}) %collective-permute-start.29) | collective-permute-done | bytes 131104 | tf_op jit(solution)/shard_map/ppermute | solution.py:34
  155.7 5.2 %collective-permute-done.8 = bf16[32,2048]{1,0:T(8,128)(2,1)S(1)} collective-permute-done((bf16[32,2048]{1,0:T(8,128)(2,1)S(1)}, bf16[32,2048]{1,0:T(8,128)(2,1)S(1)}, u32[]{:S(2)}, u32[]{:S(2)}) %collective-permute-start.8) | collective-permute-done | bytes 131104 | tf_op jit(solution)/shard_map/ppermute | solution.py:34
  162.6 6.6 %collective-permute-done.31 = bf16[64,1024]{1,0:T(8,128)(2,1)S(1)} collective-permute-done((bf16[64,1024]{1,0:T(8,128)(2,1)S(1)}, bf16[64,1024]{1,0:T(8,128)(2,1)S(1)}, u32[]{:S(2)}, u32[]{:S(2)}) %collective-permute-start.31) | collective-permute-done | bytes 131104 | tf_op jit(solution)/shard_map/ppermute | solution.py:34
  169.2 3.0 %collective-permute-start.32 = (bf16[64,1024]{1,0:T(8,128)(2,1)S(1)}, bf16[64,1024]{1,0:T(8,128)(2,1)S(1)}, u32[]{:S(2)}, u32[]{:S(2)}) collective-permute-start(bf16[64,1024]{1,0:T(8,128)(2,1)S(1)} %get-tuple-element.49), channel_id=1, source_target_pairs={{0,16},{8,24},{16,0},{24,8},{1,17},{9,25},{17,1},{25,9},{2,18},{10... | collective-permute-start | bytes 393224 | tf_op jit(solution)/shard_map/ppermute | solution.py:34
  177.6 2.2 %collective-permute-start.10 = (bf16[8,2048]{1,0:T(8,128)(2,1)S(1)}, bf16[8,2048]{1,0:T(8,128)(2,1)S(1)}, u32[]{:S(2)}, u32[]{:S(2)}) collective-permute-start(bf16[8,2048]{1,0:T(8,128)(2,1)S(1)} %get-tuple-element.72), channel_id=1, source_target_pairs={{0,8},{8,0},{16,24},{24,16},{1,9},{9,1},{17,25},{25,17},{2,10},{10... | collective-permute-start | bytes 98312 | tf_op jit(solution)/shard_map/ppermute | solution.py:34
  179.8 2.8 %collective-permute-start.39 = (bf16[8,1024]{1,0:T(8,128)(2,1)S(1)}, bf16[8,1024]{1,0:T(8,128)(2,1)S(1)}, u32[]{:S(2)}, u32[]{:S(2)}) collective-permute-start(bf16[8,1024]{1,0:T(8,128)(2,1)S(1)} %get-tuple-element.60), channel_id=1, source_target_pairs={{0,6},{1,7},{2,4},{3,5},{4,2},{5,3},{6,0},{7,1},{8,14},{9,15},{10,... | collective-permute-start | bytes 49160 | tf_op jit(solution)/shard_map/ppermute | solution.py:34
  187.9 3.3 %place0.1.refs_0_ = f32[32,16,2048]{2,1,0:T(8,128)} custom-call(s32[3]{0:T(128)S(1)} %pad_add_fusion.me, s32[32]{0:T(128)S(1)} %reshape.87.rr, f32[144,2048]{1,0:T(8,128)S(1)} %get-tuple-element.40.src.refs_0_), custom_call_target="tpu_custom_call" | custom-call | flops 100000 | bytes 2097152 | tf_op jit(solution)/shard_map/place0/pallas_call | solution.py:314
  191.2 3.3 %place1.1.refs_0_ = f32[32,16,2048]{2,1,0:T(8,128)} custom-call(s32[3]{0:T(128)S(1)} %pad_add_fusion.me, s32[32]{0:T(128)S(1)} %reshape.87.rr, bf16[144,2048]{1,0:T(8,128)(2,1)S(1)} %collective-permute-done.43.src.refs_1_, f32[32,16,2048]{2,1,0:T(8,128)} %place0.1.refs_0_), custom_call_target="tpu_custom_call", output_to_operand_aliasing={{}: (3, {})} | custom-call | flops 100000 | bytes 2097152 | tf_op jit(solution)/shard_map/place1/pallas_call | solution.py:314
  194.4 3.3 %place2.1.refs_0_ = f32[32,16,2048]{2,1,0:T(8,128)} custom-call(s32[3]{0:T(128)S(1)} %pad_add_fusion.me, s32[32]{0:T(128)S(1)} %reshape.87.rr, bf16[144,2048]{1,0:T(8,128)(2,1)S(1)} %collective-permute-done.42.src.refs_2_, f32[32,16,2048]{2,1,0:T(8,128)} %place1.1.refs_0_), custom_call_target="tpu_custom_call", output_to_operand_aliasing={{}: (3, {})} | custom-call | flops 100000 | bytes 2097152 | tf_op jit(solution)/shard_map/place2/pallas_call | solution.py:314
  199.2 3.3 %place3.1 = f32[32,16,2048]{2,1,0:T(8,128)} custom-call(s32[3]{0:T(128)S(1)} %pad_add_fusion.me, s32[32]{0:T(128)S(1)} %reshape.87.rr, bf16[144,2048]{1,0:T(8,128)(2,1)S(1)} %collective-permute-done.41.src.refs_3_, f32[32,16,2048]{2,1,0:T(8,128)} %place2.1.refs_0_), custom_call_target="tpu_custom_call", output_to_operand_aliasing={{}: (3, {})} | custom-call | flops 100000 | bytes 2097152 | tf_op jit(solution)/shard_map/place3/pallas_call | solution.py:314
  (136 shorter events, 56.9 us)
Async XLA Ops:
  7.4 13.4 %collective-permute-start = (bf16[8,12544]{1,0:T(8,128)(2,1)S(1)}, bf16[8,12544]{1,0:T(8,128)(2,1)S(1)}, u32[]{:S(2)}, u32[]{:S(2)}) collective-permute-start(bf16[8,12544]{1,0:T(8,128)(2,1)S(1)} %get-tuple-element.24), channel_id=1, source_target_pairs={{0,8},{8,0},{16,24},{24,16},{1,9},{9,1},{17,25},{25,17},{2,10},{10... | collective-permute-start | bytes 602120 | tf_op jit(solution)/shard_map/ppermute | solution.py:34
  10.4 13.5 %collective-permute-start.1 = (bf16[8,12544]{1,0:T(8,128)(2,1)S(1)}, bf16[8,12544]{1,0:T(8,128)(2,1)S(1)}, u32[]{:S(2)}, u32[]{:S(2)}) collective-permute-start(bf16[8,12544]{1,0:T(8,128)(2,1)S(1)} %get-tuple-element.26), channel_id=1, source_target_pairs={{0,16},{8,24},{16,0},{24,8},{1,17},{9,25},{17,1},{25,9},{2,18},{10... | collective-permute-start | bytes 602120 | tf_op jit(solution)/shard_map/ppermute | solution.py:34
  11.9 15.9 %collective-permute-start.2 = (bf16[8,12544]{1,0:T(8,128)(2,1)S(1)}, bf16[8,12544]{1,0:T(8,128)(2,1)S(1)}, u32[]{:S(2)}, u32[]{:S(2)}) collective-permute-start(bf16[8,12544]{1,0:T(8,128)(2,1)S(1)} %get-tuple-element.28), channel_id=1, source_target_pairs={{0,24},{8,16},{16,8},{24,0},{1,25},{9,17},{17,9},{25,1},{2,26},{10... | collective-permute-start | bytes 602120 | tf_op jit(solution)/shard_map/ppermute | solution.py:34
  30.9 10.3 %collective-permute-start.5 = (bf16[64,2048]{1,0:T(8,128)(2,1)S(1)}, bf16[64,2048]{1,0:T(8,128)(2,1)S(1)}, u32[]{:S(2)}, u32[]{:S(2)}) collective-permute-start(bf16[64,2048]{1,0:T(8,128)(2,1)S(1)} %bitcast.23), channel_id=1, source_target_pairs={{0,24},{8,16},{16,8},{24,0},{1,25},{9,17},{17,9},{25,1},{2,26},{10... | collective-permute-start | bytes 786440 | tf_op jit(solution)/shard_map/ppermute | solution.py:34
  33.9 11.1 %collective-permute-start.4 = (bf16[64,2048]{1,0:T(8,128)(2,1)S(1)}, bf16[64,2048]{1,0:T(8,128)(2,1)S(1)}, u32[]{:S(2)}, u32[]{:S(2)}) collective-permute-start(bf16[64,2048]{1,0:T(8,128)(2,1)S(1)} %bitcast.24), channel_id=1, source_target_pairs={{0,16},{8,24},{16,0},{24,8},{1,17},{9,25},{17,1},{25,9},{2,18},{10... | collective-permute-start | bytes 786440 | tf_op jit(solution)/shard_map/ppermute | solution.py:34
  34.4 10.9 %collective-permute-start.3 = (bf16[64,2048]{1,0:T(8,128)(2,1)S(1)}, bf16[64,2048]{1,0:T(8,128)(2,1)S(1)}, u32[]{:S(2)}, u32[]{:S(2)}) collective-permute-start(bf16[64,2048]{1,0:T(8,128)(2,1)S(1)} %bitcast.25), channel_id=1, source_target_pairs={{0,8},{8,0},{16,24},{24,16},{1,9},{9,1},{17,25},{25,17},{2,10},{10... | collective-permute-start | bytes 786440 | tf_op jit(solution)/shard_map/ppermute | solution.py:34
  56.9 10.0 %collective-permute-start.16 = (bf16[32,2048]{1,0:T(8,128)(2,1)}, bf16[32,2048]{1,0:T(8,128)(2,1)}, u32[]{:S(2)}, u32[]{:S(2)}) collective-permute-start(bf16[32,2048]{1,0:T(8,128)(2,1)} %get-tuple-element.54), channel_id=1, source_target_pairs={{0,6},{2,4},{4,2},{6,0},{1,7},{3,5},{5,3},{7,1},{8,14},{10,12},{12... | collective-permute-start | bytes 393224 | tf_op jit(solution)/shard_map/ppermute | solution.py:34
  59.4 12.3 %collective-permute-start.15 = (bf16[32,2048]{1,0:T(8,128)(2,1)}, bf16[32,2048]{1,0:T(8,128)(2,1)}, u32[]{:S(2)}, u32[]{:S(2)}) collective-permute-start(bf16[32,2048]{1,0:T(8,128)(2,1)} %get-tuple-element.55), channel_id=1, source_target_pairs={{0,4},{2,6},{4,0},{6,2},{1,5},{3,7},{5,1},{7,3},{8,12},{10,14},{12... | collective-permute-start | bytes 393224 | tf_op jit(solution)/shard_map/ppermute | solution.py:34
  80.2 8.0 %collective-permute-start.25 = (bf16[8,8192]{1,0:T(8,128)(2,1)S(1)}, bf16[8,8192]{1,0:T(8,128)(2,1)S(1)}, u32[]{:S(2)}, u32[]{:S(2)}) collective-permute-start(bf16[8,8192]{1,0:T(8,128)(2,1)S(1)} %pad_maximum_fusion.refs_0_), channel_id=1, source_target_pairs={{0,6},{2,4},{4,2},{6,0},{1,7},{3,5},{5,3},{7,1},{8,14},{10,12},{12... | collective-permute-start | bytes 393224 | tf_op jit(solution)/shard_map/ppermute | solution.py:34
  82.9 9.5 %collective-permute-start.23 = (bf16[8,8192]{1,0:T(8,128)(2,1)S(1)}, bf16[8,8192]{1,0:T(8,128)(2,1)S(1)}, u32[]{:S(2)}, u32[]{:S(2)}) collective-permute-start(bf16[8,8192]{1,0:T(8,128)(2,1)S(1)} %pad_maximum_fusion.refs_0_), channel_id=1, source_target_pairs={{0,4},{2,6},{4,0},{6,2},{1,5},{3,7},{5,1},{7,3},{8,12},{10,14},{12... | collective-permute-start | bytes 393224 | tf_op jit(solution)/shard_map/ppermute | solution.py:34
  82.9 9.5 %collective-permute-start.21 = (bf16[8,8192]{1,0:T(8,128)(2,1)S(1)}, bf16[8,8192]{1,0:T(8,128)(2,1)S(1)}, u32[]{:S(2)}, u32[]{:S(2)}) collective-permute-start(bf16[8,8192]{1,0:T(8,128)(2,1)S(1)} %pad_maximum_fusion.refs_0_), channel_id=1, source_target_pairs={{0,2},{2,0},{4,6},{6,4},{1,3},{3,1},{5,7},{7,5},{8,10},{10,8},{12,... | collective-permute-start | bytes 393224 | tf_op jit(solution)/shard_map/ppermute | solution.py:34
  84.7 41.1 %collective-permute-start.6 = (bf16[128,2048]{1,0:T(8,128)(2,1)}, bf16[128,2048]{1,0:T(8,128)(2,1)}, u32[]{:S(2)}, u32[]{:S(2)}) collective-permute-start(bf16[128,2048]{1,0:T(8,128)(2,1)} %get-tuple-element.32), channel_id=1, source_target_pairs={{0,1},{1,0},{2,3},{3,2},{4,5},{5,4},{6,7},{7,6},{8,9},{9,8},{10,11... | collective-permute-start | bytes 1572872 | tf_op jit(solution)/shard_map/ppermute | solution.py:34
  84.7 8.2 %collective-permute-start.20 = (bf16[8,8192]{1,0:T(8,128)(2,1)S(1)}, bf16[8,8192]{1,0:T(8,128)(2,1)S(1)}, u32[]{:S(2)}, u32[]{:S(2)}) collective-permute-start(bf16[8,8192]{1,0:T(8,128)(2,1)S(1)} %pad_maximum_fusion.refs_0_), channel_id=1, source_target_pairs={{0,1},{1,0},{2,3},{3,2},{4,5},{5,4},{6,7},{7,6},{8,9},{9,8},{10,11... | collective-permute-start | bytes 393224 | tf_op jit(solution)/shard_map/ppermute | solution.py:34
  92.9 84.7 %collective-permute-start.41 = (bf16[144,2048]{1,0:T(8,128)(2,1)}, bf16[144,2048]{1,0:T(8,128)(2,1)S(1)}, u32[]{:S(2)}, u32[]{:S(2)}) collective-permute-start(bf16[144,2048]{1,0:T(8,128)(2,1)} %copy-done.15), channel_id=1, source_target_pairs={{0,24},{8,16},{16,8},{24,0},{1,25},{9,17},{17,9},{25,1},{2,26},{10... | collective-permute-start | bytes 1769480 | tf_op jit(solution)/shard_map/ppermute | solution.py:34
  94.3 85.4 %collective-permute-start.42 = (bf16[144,2048]{1,0:T(8,128)(2,1)}, bf16[144,2048]{1,0:T(8,128)(2,1)S(1)}, u32[]{:S(2)}, u32[]{:S(2)}) collective-permute-start(bf16[144,2048]{1,0:T(8,128)(2,1)} %copy-done.14), channel_id=1, source_target_pairs={{0,16},{8,24},{16,0},{24,8},{1,17},{9,25},{17,1},{25,9},{2,18},{10... | collective-permute-start | bytes 1769480 | tf_op jit(solution)/shard_map/ppermute | solution.py:34
  125.7 8.2 %collective-permute-start.27 = (bf16[64,4096]{1,0:T(8,128)(2,1)S(1)}, bf16[64,4096]{1,0:T(8,128)(2,1)S(1)}, u32[]{:S(2)}, u32[]{:S(2)}) collective-permute-start(bf16[64,4096]{1,0:T(8,128)(2,1)S(1)} %down1.1), channel_id=1, source_target_pairs={{0,1},{1,0},{2,3},{3,2},{4,5},{5,4},{6,7},{7,6},{8,9},{9,8},{10,11... | collective-permute-start | bytes 1572872 | tf_op jit(solution)/shard_map/ppermute | solution.py:34
  134.2 9.4 %collective-permute-start.30 = (bf16[64,1024]{1,0:T(8,128)(2,1)S(1)}, bf16[64,1024]{1,0:T(8,128)(2,1)S(1)}, u32[]{:S(2)}, u32[]{:S(2)}) collective-permute-start(bf16[64,1024]{1,0:T(8,128)(2,1)S(1)} %get-tuple-element.51), channel_id=1, source_target_pairs={{0,6},{2,4},{4,2},{6,0},{1,7},{3,5},{5,3},{7,1},{8,14},{10,12},{12... | collective-permute-start | bytes 393224 | tf_op jit(solution)/shard_map/ppermute | solution.py:34
  136.4 16.8 %collective-permute-start.29 = (bf16[64,1024]{1,0:T(8,128)(2,1)S(1)}, bf16[64,1024]{1,0:T(8,128)(2,1)S(1)}, u32[]{:S(2)}, u32[]{:S(2)}) collective-permute-start(bf16[64,1024]{1,0:T(8,128)(2,1)S(1)} %get-tuple-element.52), channel_id=1, source_target_pairs={{0,4},{2,6},{4,0},{6,2},{1,5},{3,7},{5,1},{7,3},{8,12},{10,14},{12... | collective-permute-start | bytes 393224 | tf_op jit(solution)/shard_map/ppermute | solution.py:34
  140.1 13.5 %collective-permute-start.7 = (bf16[32,2048]{1,0:T(8,128)(2,1)S(1)}, bf16[32,2048]{1,0:T(8,128)(2,1)S(1)}, u32[]{:S(2)}, u32[]{:S(2)}) collective-permute-start(bf16[32,2048]{1,0:T(8,128)(2,1)S(1)} %get-tuple-element.56), channel_id=1, source_target_pairs={{0,2},{2,0},{4,6},{6,4},{1,3},{3,1},{5,7},{7,5},{8,10},{10,8},{12,... | collective-permute-start | bytes 393224 | tf_op jit(solution)/shard_map/ppermute | solution.py:34
  143.6 11.4 %collective-permute-start.9 = (bf16[32,2048]{1,0:T(8,128)(2,1)S(1)}, bf16[32,2048]{1,0:T(8,128)(2,1)S(1)}, u32[]{:S(2)}, u32[]{:S(2)}) collective-permute-start(bf16[32,2048]{1,0:T(8,128)(2,1)S(1)} %get-tuple-element.57), channel_id=1, source_target_pairs={{0,6},{2,4},{4,2},{6,0},{1,7},{3,5},{5,3},{7,1},{8,14},{10,12},{12... | collective-permute-start | bytes 393224 | tf_op jit(solution)/shard_map/ppermute | solution.py:34
  153.2 7.7 %collective-permute-start.8 = (bf16[32,2048]{1,0:T(8,128)(2,1)S(1)}, bf16[32,2048]{1,0:T(8,128)(2,1)S(1)}, u32[]{:S(2)}, u32[]{:S(2)}) collective-permute-start(bf16[32,2048]{1,0:T(8,128)(2,1)S(1)} %get-tuple-element.58), channel_id=1, source_target_pairs={{0,4},{2,6},{4,0},{6,2},{1,5},{3,7},{5,1},{7,3},{8,12},{10,14},{12... | collective-permute-start | bytes 393224 | tf_op jit(solution)/shard_map/ppermute | solution.py:34
  153.6 26.2 %collective-permute-start.43 = (bf16[144,2048]{1,0:T(8,128)(2,1)S(1)}, bf16[144,2048]{1,0:T(8,128)(2,1)S(1)}, u32[]{:S(2)}, u32[]{:S(2)}) collective-permute-start(bf16[144,2048]{1,0:T(8,128)(2,1)S(1)} %get-tuple-element.39), channel_id=1, source_target_pairs={{0,8},{8,0},{16,24},{24,16},{1,9},{9,1},{17,25},{25,17},{2,10},{10... | collective-permute-start | bytes 1769480 | tf_op jit(solution)/shard_map/ppermute | solution.py:34
  155.0 14.2 %collective-permute-start.31 = (bf16[64,1024]{1,0:T(8,128)(2,1)S(1)}, bf16[64,1024]{1,0:T(8,128)(2,1)S(1)}, u32[]{:S(2)}, u32[]{:S(2)}) collective-permute-start(bf16[64,1024]{1,0:T(8,128)(2,1)S(1)} %get-tuple-element.47), channel_id=1, source_target_pairs={{0,8},{8,0},{16,24},{24,16},{1,9},{9,1},{17,25},{25,17},{2,10},{10... | collective-permute-start | bytes 393224 | tf_op jit(solution)/shard_map/ppermute | solution.py:34
  161.0 12.0 %collective-permute-start.33 = (bf16[64,1024]{1,0:T(8,128)(2,1)S(1)}, bf16[64,1024]{1,0:T(8,128)(2,1)S(1)}, u32[]{:S(2)}, u32[]{:S(2)}) collective-permute-start(bf16[64,1024]{1,0:T(8,128)(2,1)S(1)} %get-tuple-element.48), channel_id=1, source_target_pairs={{0,24},{8,16},{16,8},{24,0},{1,25},{9,17},{17,9},{25,1},{2,26},{10... | collective-permute-start | bytes 393224 | tf_op jit(solution)/shard_map/ppermute | solution.py:34
  173.0 9.7 %collective-permute-start.12 = (bf16[8,2048]{1,0:T(8,128)(2,1)S(1)}, bf16[8,2048]{1,0:T(8,128)(2,1)S(1)}, u32[]{:S(2)}, u32[]{:S(2)}) collective-permute-start(bf16[8,2048]{1,0:T(8,128)(2,1)S(1)} %get-tuple-element.70), channel_id=1, source_target_pairs={{0,24},{8,16},{16,8},{24,0},{1,25},{9,17},{17,9},{25,1},{2,26},{10... | collective-permute-start | bytes 98312 | tf_op jit(solution)/shard_map/ppermute | solution.py:34
  175.5 8.6 %collective-permute-start.11 = (bf16[8,2048]{1,0:T(8,128)(2,1)S(1)}, bf16[8,2048]{1,0:T(8,128)(2,1)S(1)}, u32[]{:S(2)}, u32[]{:S(2)}) collective-permute-start(bf16[8,2048]{1,0:T(8,128)(2,1)S(1)} %get-tuple-element.71), channel_id=1, source_target_pairs={{0,16},{8,24},{16,0},{24,8},{1,17},{9,25},{17,1},{25,9},{2,18},{10... | collective-permute-start | bytes 98312 | tf_op jit(solution)/shard_map/ppermute | solution.py:34
  177.6 8.5 %collective-permute-start.10 = (bf16[8,2048]{1,0:T(8,128)(2,1)S(1)}, bf16[8,2048]{1,0:T(8,128)(2,1)S(1)}, u32[]{:S(2)}, u32[]{:S(2)}) collective-permute-start(bf16[8,2048]{1,0:T(8,128)(2,1)S(1)} %get-tuple-element.72), channel_id=1, source_target_pairs={{0,8},{8,0},{16,24},{24,16},{1,9},{9,1},{17,25},{25,17},{2,10},{10... | collective-permute-start | bytes 98312 | tf_op jit(solution)/shard_map/ppermute | solution.py:34
  182.7 19.8 %collective-permute-start.38 = (bf16[8,1024]{1,0:T(8,128)(2,1)S(1)}, bf16[8,1024]{1,0:T(8,128)(2,1)S(1)}, u32[]{:S(2)}, u32[]{:S(2)}) collective-permute-start(bf16[8,1024]{1,0:T(8,128)(2,1)S(1)} %get-tuple-element.61), channel_id=1, source_target_pairs={{0,5},{1,4},{2,7},{3,6},{4,1},{5,0},{6,3},{7,2},{8,13},{9,12},{10,... | collective-permute-start | bytes 49160 | tf_op jit(solution)/shard_map/ppermute | solution.py:34
  184.1 18.4 %collective-permute-start.37 = (bf16[8,1024]{1,0:T(8,128)(2,1)S(1)}, bf16[8,1024]{1,0:T(8,128)(2,1)S(1)}, u32[]{:S(2)}, u32[]{:S(2)}) collective-permute-start(bf16[8,1024]{1,0:T(8,128)(2,1)S(1)} %get-tuple-element.62), channel_id=1, source_target_pairs={{0,4},{1,5},{2,6},{3,7},{4,0},{5,1},{6,2},{7,3},{8,12},{9,13},{10,... | collective-permute-start | bytes 49160 | tf_op jit(solution)/shard_map/ppermute | solution.py:34
  186.0 16.5 %collective-permute-start.36 = (bf16[8,1024]{1,0:T(8,128)(2,1)S(1)}, bf16[8,1024]{1,0:T(8,128)(2,1)S(1)}, u32[]{:S(2)}, u32[]{:S(2)}) collective-permute-start(bf16[8,1024]{1,0:T(8,128)(2,1)S(1)} %get-tuple-element.63), channel_id=1, source_target_pairs={{0,3},{1,2},{2,1},{3,0},{4,7},{5,6},{6,5},{7,4},{8,11},{9,10},{10,... | collective-permute-start | bytes 49160 | tf_op jit(solution)/shard_map/ppermute | solution.py:34
  186.2 16.3 %collective-permute-start.35 = (bf16[8,1024]{1,0:T(8,128)(2,1)S(1)}, bf16[8,1024]{1,0:T(8,128)(2,1)S(1)}, u32[]{:S(2)}, u32[]{:S(2)}) collective-permute-start(bf16[8,1024]{1,0:T(8,128)(2,1)S(1)} %get-tuple-element.64), channel_id=1, source_target_pairs={{0,2},{1,3},{2,0},{3,1},{4,6},{5,7},{6,4},{7,5},{8,10},{9,11},{10,... | collective-permute-start | bytes 49160 | tf_op jit(solution)/shard_map/ppermute | solution.py:34
  187.3 15.2 %collective-permute-start.34 = (bf16[8,1024]{1,0:T(8,128)(2,1)S(1)}, bf16[8,1024]{1,0:T(8,128)(2,1)S(1)}, u32[]{:S(2)}, u32[]{:S(2)}) collective-permute-start(bf16[8,1024]{1,0:T(8,128)(2,1)S(1)} %get-tuple-element.65), channel_id=1, source_target_pairs={{0,1},{1,0},{2,3},{3,2},{4,5},{5,4},{6,7},{7,6},{8,9},{9,8},{10,11... | collective-permute-start | bytes 49160 | tf_op jit(solution)/shard_map/ppermute | solution.py:34
  (30 other events, 155.4 us)

commit v2 on v1

v2 whole, which is shorter than its diff:
```python
import functools

import jax
import jax.numpy as jnp
from jax import lax
from jax.experimental import pallas as pl
from jax.experimental.pallas import tpu as pltpu
from jax.sharding import Mesh
from jax.sharding import PartitionSpec as P

FFW = 12288
BF = jnp.bfloat16
F32 = jnp.float32
META = 256
TABLE = 96
PREFIX = 64
NT = (((1,), (1,)), ((), ()))
TN = (((0,), (0,)), ((), ()))


def cost(flops, moved):
    return pl.CostEstimate(flops=int(flops), bytes_accessed=int(moved), transcendentals=0)


def params(limit):
    return pltpu.CompilerParams(vmem_limit_bytes=limit << 20)


def iota(shape, dim):
    return lax.broadcasted_iota(jnp.int32, shape, dim)


def trade(piece, axis, size, k):
    return lax.ppermute(piece, axis, [(i, i ^ k) for i in range(size)])


def pack_kernel(n, per, me, rr, x, z, dt, b, c, prefix, *rest):
    outs, m_scr = rest[:n], rest[n]
    steps, rows, ch = x.shape
    states = b.shape[1]
    m_scr[...] = jnp.zeros_like(m_scr)
    for t in range(steps):
        m_scr[2 * t * states : (2 * t + 1) * states, :] = b[t]
        m_scr[(2 * t + 1) * states : (2 * t + 2) * states, :] = c[t]
    m_scr[PREFIX : PREFIX + 1, :] = prefix[...].astype(F32)
    rowcol = jnp.zeros((n * per, 1), jnp.int32)
    table = jnp.zeros((1, 128), F32)
    sub = iota((n * per, 1), 0)
    lane = iota((1, 128), 1)
    for k in range(n):
        for i in range(per):
            rowcol = jnp.where(sub == k * per + i, rr[0, me[0] ^ k, i], rowcol)
            q = k * per + i
            table = jnp.where(lane == TABLE + q, rr[0, k, i].astype(F32), table)
    hot = rowcol == iota((n * per, rows), 1)
    hot_b = hot.astype(BF)
    for a, src in enumerate((x, z, dt)):
        for t in range(steps):
            got = jnp.dot(hot_b, src[t], preferred_element_type=F32).astype(BF)
            at = (a * steps + t) * ch
            for k in range(n):
                outs[k][:, at : at + ch] = got[k * per : (k + 1) * per]
    meta = lax.dot_general(
        hot.astype(F32), m_scr[...], NT, precision=lax.Precision.HIGHEST, preferred_element_type=F32
    )
    meta = meta + table
    hi = meta.astype(BF)
    lo = (meta - hi.astype(F32)).astype(BF)
    at = 3 * steps * ch
    for k in range(n):
        outs[k][:, at : at + 128] = hi[k * per : (k + 1) * per]
        outs[k][:, at + 128 : at + 256] = lo[k * per : (k + 1) * per]


def ssm_kernel(first, groups, n, per, steps, me, ss, *refs):
    wide = 3 * steps + 1
    if first:
        refs = refs[1:]
    loads = refs[: groups * wide]
    par, decay, conv = refs[groups * wide : groups * wide + 3]
    rest = refs[groups * wide + 3 :]
    state, (y_out, *st_outs) = rest[:per], rest[per : per + 1 + groups]
    arrs, meta, y_scr, tail_scr, bc_scr = rest[per + 1 + groups :]
    group = pl.program_id(0)
    for q in range(groups):

        @pl.when(group == q)
        def _():
            for a in range(3 * steps):
                arrs[a] = loads[q * wide + a][...]
            meta[...] = loads[q * wide + wide - 1][...]

    taps = conv.shape[0]
    states, cb = decay.shape
    val = meta[:, :128].astype(F32) + meta[:, 128:].astype(F32)
    bc_scr[...] = jnp.transpose(jnp.concatenate([val, jnp.zeros((128 - per, 128), F32)], axis=0))
    src = me[0] ^ (group + first)
    for j in range(taps):
        for i in range(per):
            tail_scr[j, i : i + 1, :] = conv[j, pl.ds(ss[me[0], src, i], 1), :]
    prefix = val[:, PREFIX : PREFIX + 1]
    window = [
        tail_scr[j] * (prefix >= float(taps - j)).astype(F32) for j in range(taps)
    ]
    deltas, us, skips, gates = [], [], [], []
    for t in range(steps):
        window.append(arrs[t].astype(F32))
        acc = window[t] * par[0:1, :]
        for j in range(1, taps + 1):
            acc = acc + window[t + j] * par[j : j + 1, :]
        acc = acc + par[taps + 1 : taps + 2, :]
        xc = acc * jax.nn.sigmoid(acc)
        raw = arrs[2 * steps + t].astype(F32) + par[taps + 2 : taps + 3, :]
        delta = jnp.maximum(raw, 0.0) + jnp.log1p(jnp.exp(-jnp.abs(raw)))
        zt = arrs[steps + t].astype(F32)
        deltas.append(-delta)
        us.append(delta * xc)
        skips.append(par[taps + 3 : taps + 4, :] * xc)
        gates.append(zt * jax.nn.sigmoid(zt))
    dec = decay[...]
    low = st_outs[0].shape[0] - per * states
    kept = window[steps:taps]
    kept.append(jnp.zeros((low - per * len(kept), cb), F32))
    kept = jnp.concatenate(kept, axis=0)
    ends = []
    for i in range(per):
        st = state[i][0]
        for t in range(steps):
            at = 2 * t * states
            bcol = bc_scr[at : at + states, i : i + 1]
            ccol = bc_scr[at + states : at + 2 * states, i : i + 1]
            st = jnp.exp(deltas[t][i : i + 1] * dec) * st + us[t][i : i + 1] * bcol
            y_scr[t, i : i + 1, :] = jnp.sum(ccol * st, axis=0, keepdims=True)
        for q in range(groups):

            @pl.when(group == q)
            def _():
                st_outs[q][i * states : (i + 1) * states, :] = st.astype(st_outs[q].dtype)

    for q in range(groups):

        @pl.when(group == q)
        def _():
            st_outs[q][per * states :, :] = kept.astype(st_outs[q].dtype)

    for t in range(steps):
        out = (y_scr[t] + skips[t]) * gates[t]
        y_out[0, t * per : (t + 1) * per, :] = out.astype(BF)


def ssm(first, n, per, steps, me, ss, payloads, par, decay, conv, state, y_buf):
    groups = len(payloads)
    states, ch = decay.shape
    blocks = 2
    cb = ch // blocks
    taps = conv.shape[0]
    low = -(-(taps - steps) * per // 16) * 16

    def held(q, gk, g):
        return jnp.where(gk < q, 0, jnp.where(gk > q, blocks - 1, g))

    specs, args = [], []
    for q in range(groups):
        for a in range(3 * steps):
            specs.append(
                pl.BlockSpec(
                    (per, cb),
                    functools.partial(
                        lambda q, a, gk, g, *_: (0, a * blocks + held(q, gk, g)), q, a
                    ),
                )
            )
        specs.append(pl.BlockSpec((per, META), lambda gk, g, *_: (0, 3 * steps * ch // META)))
        args += [payloads[q]] * (3 * steps + 1)
    specs.append(pl.BlockSpec((par.shape[0], cb), lambda gk, g, *_: (0, g)))
    specs.append(pl.BlockSpec((states, cb), lambda gk, g, *_: (0, g)))
    specs.append(pl.BlockSpec((taps, conv.shape[1], cb), lambda gk, g, *_: (0, 0, g)))
    for i in range(per):
        specs.append(
            pl.BlockSpec(
                (1, states, cb),
                functools.partial(
                    lambda i, gk, g, m, s: (s[m[0], m[0] ^ (gk + first), i], 0, g), i
                ),
            )
        )
    args += [par, decay, conv] + [state] * per
    alias = {}
    if first:
        specs = [pl.BlockSpec(memory_space=pl.ANY)] + specs
        args = [y_buf] + args
        alias = {2: 0}
    st_type = BF if first else F32
    return pl.pallas_call(
        functools.partial(ssm_kernel, first, groups, n, per, steps),
        grid_spec=pltpu.PrefetchScalarGridSpec(
            num_scalar_prefetch=2,
            grid=(groups, blocks),
            in_specs=specs,
            out_specs=[pl.BlockSpec((1, steps * per, cb), lambda gk, g, *_: (gk + first, 0, g))]
            + [
                pl.BlockSpec(
                    (per * states + low, cb),
                    functools.partial(lambda q, gk, g, *_: (0, held(q, gk, g)), q),
                )
                for q in range(groups)
            ],
            scratch_shapes=[
                pltpu.VMEM((3 * steps, per, cb), BF),
                pltpu.VMEM((per, META), BF),
                pltpu.VMEM((steps, per, cb), F32),
                pltpu.VMEM((taps, per, cb), F32),
                pltpu.VMEM((128, 128), F32),
            ],
        ),
        out_shape=[jax.ShapeDtypeStruct((n, steps * per, ch), BF)]
        + [jax.ShapeDtypeStruct((per * states + low, ch), st_type)] * groups,
        input_output_aliases=alias,
        compiler_params=params(16),
        cost_estimate=cost(3e6 * groups, groups * 3 << 20),
        name=f"ssm{first}",
    )(me, ss, *args)


def select_kernel(n, m, per, steps, rows, rm, pe, width, me, es, ids, wts, *refs):
    tables = refs[:n]
    sel_slot, sel_own, share, expand = refs[n:]
    cores = m * 2
    d, zz, cc = me[0], me[1], me[2]
    total = steps * n * rows
    choices = ids.shape[0]
    sub8 = iota((8, total), 0)
    match = jnp.zeros((8, total), F32)
    own_share = jnp.zeros((1, total), F32)
    hits = []
    for kd in range(n):
        eid = es[((d ^ kd) * (cores * width)) // FFW]
        hit = jnp.zeros((1, total), F32)
        for q in range(choices):
            same = ids[q : q + 1, :] == eid
            hit = jnp.where(same, 1.0, hit)
            if kd == 0:
                own_share = own_share + jnp.where(same, wts[q : q + 1, :], 0.0)
        hits.append(hit)
        match = jnp.where(sub8 == kd, hit, match)
    before = (iota((total, total), 0) < iota((total, total), 1)).astype(BF)
    pos = jnp.dot(match.astype(BF), before, preferred_element_type=F32)
    pos = jnp.where(match > 0.0, pos, -1.0)
    col = iota((pe, 1), 0)
    parts, owns = [], []
    for h in range(2):
        for kz in range(m):
            first = ((zz ^ kz) * 2 + (cc ^ h)) * pe
            want = (col + first).astype(F32)
            for kd in range(n):
                parts.append((pos[kd : kd + 1, :] == want).astype(BF))
        row = iota((m * n * rm, 1), 0)
        kz_v = row // (n * rm)
        kd_v = (row // rm) % n
        true = ((d ^ kd_v) * cores + (zz ^ kz_v) * 2 + (cc ^ h)) * rm + row % rm
        owns.append((true == iota((m * n * rm, total), 1)).astype(BF))
    sel_true = jnp.concatenate(parts + owns, axis=0)
    j = iota((total, 1), 0)
    ko = j // (n * steps * per)
    kd = (j // (steps * per)) % n
    tab = jnp.zeros((8, 128), F32)
    for q in range(n):
        tab = jnp.where(iota((8, 128), 0) == q, tables[q][0:1, :].astype(F32), tab)
    pick = (iota((total, 8), 1) == (ko ^ kd)).astype(BF)
    tj = jnp.dot(pick, tab.astype(BF), preferred_element_type=F32)
    lane = TABLE + (d ^ ko) * per + j % per
    local = jnp.sum(jnp.where(iota((total, 128), 1) == lane, tj, 0.0), axis=1, keepdims=True)
    true = ((j // per) % steps) * (n * rows) + (d ^ ko ^ kd) * rows + local.astype(jnp.int32)
    perm = (true == iota((total, total), 1)).astype(BF)
    sel = lax.dot_general(sel_true, perm, NT, preferred_element_type=F32).astype(BF)
    count = sel_slot.shape[0]
    sel_slot[...] = sel[:count]
    sel_own[...] = sel[count:]
    hot = pos[0:1, :] == iota((cores * pe, 1), 0).astype(F32)
    expand[...] = hot.astype(BF)
    mine = jnp.sum(jnp.where(hot, own_share, 0.0), axis=1, keepdims=True)
    share[...] = jnp.broadcast_to(mine, share.shape)


def project_kernel(n, *refs):
    ys = refs[:n]
    sel, w = refs[n : n + 2]
    keep, send, y_all, y_sel = refs[-4:]
    size = ys[0].shape[0]
    for q in range(n):
        y_all[q * size : (q + 1) * size, :] = ys[q][...]
    y_sel[...] = jnp.dot(sel[...], y_all[...], preferred_element_type=F32).astype(BF)
    half = keep.shape[0]
    wb = min(512, w.shape[1])

    @pl.loop(0, w.shape[1] // wb)
    def _(g):
        at = pl.ds(pl.multiple_of(g * wb, wb), wb)
        out = jnp.dot(y_sel[...], w[:, at], preferred_element_type=F32).astype(BF)
        keep[:, at] = out[:half]
        send[:, at] = out[half:]


def project(n, ys, sel, w, name, dep):
    vm = pl.BlockSpec(memory_space=pltpu.VMEM)
    count, total = sel.shape
    ch, wc = w.shape
    return pl.pallas_call(
        functools.partial(project_kernel, n),
        in_specs=[vm] * (n + 2) + [pl.BlockSpec(memory_space=pl.ANY)],
        out_specs=[vm] * 2,
        out_shape=[jax.ShapeDtypeStruct((count // 2, wc), BF)] * 2,
        scratch_shapes=[pltpu.VMEM((total, ch), BF), pltpu.VMEM((count, ch), BF)],
        compiler_params=params(8),
        cost_estimate=cost(2 * count * ch * wc, 2 * ch * wc),
        name=name,
    )(*ys, sel, w, dep)


def load_kernel(chunks, w, *refs):
    out, token, sem = refs[-3:]
    token[...] = jnp.zeros_like(token)
    size = w.shape[0] // chunks
    copies = [
        pltpu.make_async_copy(
            w.at[pl.ds(q * size, size)], out.at[pl.ds(q * size, size)], sem.at[q]
        )
        for q in range(chunks)
    ]
    for copy in copies:
        copy.start()
    for copy in copies:
        copy.wait()


def gate_kernel(m, me, *refs):
    pieces = 2 * m
    xs = refs[:pieces]
    share, gw, uw, act, x_scr, ubuf, usem = refs[pieces:]
    pe = xs[0].shape[0]
    ub, deep = ubuf.shape[2], ubuf.shape[0]
    nu = gw.shape[1] // ub

    def up_copy(j):
        return pltpu.make_async_copy(
            uw.at[:, pl.ds(pl.multiple_of(j * ub, ub), ub)],
            ubuf.at[lax.rem(j, deep)],
            usem.at[lax.rem(j, deep)],
        )

    for j in range(min(deep, nu)):
        up_copy(j).start()
    first = me[2] == 0
    for kz in range(m):
        own, other = xs[2 * kz][...].astype(F32), xs[2 * kz + 1][...].astype(F32)
        pair = jnp.concatenate(
            [jnp.where(first, own, other), jnp.where(first, other, own)], axis=0
        ).astype(BF)
        at = pl.multiple_of((me[1] ^ kz) * (2 * pe), 2 * pe)
        x_scr[pl.ds(at, 2 * pe), :] = pair

    @pl.loop(0, nu)
    def _(j):
        at = pl.ds(pl.multiple_of(j * ub, ub), ub)
        gated = jnp.dot(x_scr[...], gw[:, at], preferred_element_type=F32)
        up_copy(j).wait()
        upped = jnp.dot(x_scr[...], ubuf[lax.rem(j, deep)], preferred_element_type=F32)

        @pl.when(j + deep < nu)
        def _():
            up_copy(j + deep).start()

        act[:, at] = (gated * jax.nn.sigmoid(gated) * upped * share[:, 0:1]).astype(BF)


def down_kernel(m, deps, me, act, dw, *refs):
    send, keep, dbuf, dsem = refs[deps:]
    pc, deep = dbuf.shape[2], dbuf.shape[0]
    nd = 2 * m

    def down_copy(i):
        h = jnp.where(i < m, 1, 0)
        block = (me[2] ^ h) * m + (me[1] ^ lax.rem(i, m))
        return pltpu.make_async_copy(
            dw.at[:, pl.ds(pl.multiple_of(block * pc, pc), pc)],
            dbuf.at[lax.rem(i, deep)],
            dsem.at[lax.rem(i, deep)],
        )

    for i in range(min(deep, nd)):
        down_copy(i).start()

    @pl.loop(0, nd)
    def _(i):
        down_copy(i).wait()
        out = jnp.dot(act[...], dbuf[lax.rem(i, deep)], preferred_element_type=F32).astype(BF)
        at = pl.ds(pl.multiple_of(lax.rem(i, m) * pc, pc), pc)

        @pl.when(i < m)
        def _():
            send[:, at] = out

        @pl.when(i >= m)
        def _():
            keep[:, at] = out

        @pl.when(i + deep < nd)
        def _():
            down_copy(i + deep).start()


def pair_rows_kernel(count, keep, got, *refs):
    outs = refs[-count:]
    size = outs[0].shape[0]
    for k in range(count):
        at = slice(k * size, (k + 1) * size)
        both = keep[at].astype(F32) + got[at].astype(F32)
        outs[k][...] = both.astype(outs[k].dtype)


def pair_cols_kernel(count, keep, got, *refs):
    outs = refs[-count:]
    size = outs[0].shape[1]
    for k in range(count):
        at = slice(k * size, (k + 1) * size)
        both = keep[:, at].astype(F32) + got[:, at].astype(F32)
        outs[k][...] = both.astype(outs[k].dtype)


def sum_rows_kernel(count, parts, *refs):
    outs = refs[-parts:]
    size = outs[0].shape[0]
    total = refs[0][...]
    for k in range(1, count):
        total = total + refs[k][...].astype(F32)
    for k in range(parts):
        outs[k][...] = total[k * size : (k + 1) * size].astype(BF)


def norm_kernel(n, me, gain, *refs):
    hid, out = refs[:n], refs[n]
    wc = hid[0].shape[1]
    wide = [h[...].astype(F32) for h in hid]
    square = sum(jnp.sum(h * h, axis=1, keepdims=True) for h in wide)
    scale = lax.rsqrt(square / (n * wc) + 1e-05)
    for k in range(n):
        at = pl.ds(pl.multiple_of((me[0] ^ k) * wc, wc), wc)
        out[:, at] = (wide[k] * scale * gain[:, at]).astype(BF)


def spread_kernel(n, m, me, expand, *refs):
    outs, scr = refs[-n - 1 : -1], refs[-1]
    out = refs[0][...]
    for k in range(1, m):
        out = out + refs[k][...].astype(F32)
    scr[...] = lax.dot_general(expand[...], out.astype(BF), TN, preferred_element_type=F32)
    size = outs[0].shape[0]
    for k in range(n):
        got = scr[pl.ds(pl.multiple_of((me[0] ^ k) * size, size), size), :]
        outs[k][...] = got.astype(outs[k].dtype)


def deal_kernel(n, m, me, *refs):
    keep, send, scr = refs[n:]
    total = refs[0][...]
    for k in range(1, n):
        total = total + refs[k][...].astype(F32)
    scr[...] = total
    rm = keep.shape[0] // m
    for q in range(2 * m):
        block = (me[1] ^ (q // 2)) * 2 + (me[2] ^ (q % 2))
        out = send if q % 2 else keep
        if rm % 8 == 0:
            got = scr[pl.ds(pl.multiple_of(block * rm, rm), rm), :]
        else:
            got = scr[:rm]
            for b in range(1, 2 * m):
                got = jnp.where(block == b, scr[b * rm : (b + 1) * rm], got)
        out[(q // 2) * rm : (q // 2 + 1) * rm, :] = got.astype(BF)


def pair_kernel(m, keep, got, *outs):
    rm = outs[0].shape[0]
    pc = keep.shape[1]
    for k in range(m):
        outs[k][:, :pc] = keep[k * rm : (k + 1) * rm]
        outs[k][:, pc:] = got[k * rm : (k + 1) * rm]


def hold_kernel(*refs):
    pass


def small(kern, name, outs, args, deps=(), scr=()):
    vm = pl.BlockSpec(memory_space=pltpu.VMEM)
    sm = pl.BlockSpec(memory_space=pltpu.SMEM)
    count = len(args)

    def run(*refs):
        kern(*refs[:count], *refs[count + len(deps) :])

    specs = [sm if a.dtype == jnp.int32 and a.ndim == 1 else vm for a in args]
    return pl.pallas_call(
        run,
        in_specs=specs + [pl.BlockSpec(memory_space=pl.ANY)] * len(deps),
        out_specs=[vm] * len(outs),
        out_shape=[jax.ShapeDtypeStruct(*o) for o in outs],
        scratch_shapes=list(scr),
        compiler_params=params(8),
        cost_estimate=cost(1e6, 1 << 20),
        name=name,
    )(*args, *deps)


def place_kernel(n, states, me, rr, *refs):
    srcs, (out, token, buf, sem) = refs[:n], refs[-4:]
    token[...] = jnp.zeros_like(token)
    i, last = pl.program_id(0), pl.num_programs(0) - 1
    slot = lax.rem(i, 2)

    def copies(step, where):
        return [
            pltpu.make_async_copy(buf.at[where, k], out.at[rr[0, me[0] ^ k, step]], sem.at[where, k])
            for k in range(n)
        ]

    @pl.when(i >= 2)
    def _():
        for copy in copies(i - 2, slot):
            copy.wait()

    for k in range(n):
        buf[slot, k] = srcs[k][...].astype(F32)
    for copy in copies(i, slot):
        copy.start()

    @pl.when(i == last)
    def _():
        for copy in copies(i - 1, 1 - slot):
            copy.wait()
        for copy in copies(i, slot):
            copy.wait()


def place(n, per, rows, states, me, rr, srcs, dep):
    ch = srcs[0].shape[1]
    return pl.pallas_call(
        functools.partial(place_kernel, n, states),
        grid_spec=pltpu.PrefetchScalarGridSpec(
            num_scalar_prefetch=2,
            grid=(per,),
            in_specs=[pl.BlockSpec((states, ch), lambda i, *_: (i, 0))] * n
            + [pl.BlockSpec(memory_space=pl.ANY)],
            out_specs=[
                pl.BlockSpec(memory_space=pl.ANY),
                pl.BlockSpec((8, 128), lambda i, *_: (0, 0)),
            ],
            scratch_shapes=[
                pltpu.VMEM((2, n, states, ch), F32),
                pltpu.SemaphoreType.DMA((2, n)),
            ],
        ),
        out_shape=[
            jax.ShapeDtypeStruct((rows, states, ch), F32),
            jax.ShapeDtypeStruct((8, 128), F32),
        ],
        compiler_params=params(8),
        cost_estimate=cost(1e5, 8 << 20),
        name="place",
    )(me, rr, *srcs, dep)


def tail_kernel(n, per, taps, me, rr, x, *refs):
    tails, (out, token) = refs[:n], refs[-2:]
    token[...] = jnp.zeros_like(token)
    steps = x.shape[0]
    keep = taps - steps
    for t in range(steps):
        out[keep + t] = x[t].astype(F32)
    for k in range(n):
        block = tails[k][...].astype(F32)
        for j in range(keep):
            for i in range(per):
                q = j * per + i
                out[j, pl.ds(rr[0, me[0] ^ k, i], 1), :] = block[q : q + 1, :]


def final_kernel(n, m, me, *refs):
    hid = refs[:n]
    parts = refs[n : n + m]
    out, acc = refs[-2:]
    wc = hid[0].shape[1]
    for k in range(n):
        acc[:, pl.ds(pl.multiple_of((me[0] ^ k) * wc, wc), wc)] = hid[k][...].astype(F32)
    pc = parts[0].shape[1] // 2
    for q in range(2 * m):
        zs, h = me[1] ^ (q // 2), q % 2
        where = pl.ds(pl.multiple_of(((me[2] ^ h) * m + zs) * pc, pc), pc)
        got = parts[q // 2][:, h * pc : (h + 1) * pc].astype(F32)
        acc[:, where] = acc[:, where] + got
    out[...] = acc[...].astype(BF)


def body(
    conv_cache,
    state_cache,
    send_slot,
    recv_row,
    prefix_length,
    x_input,
    z_input,
    dt_input,
    b_input,
    c_input,
    conv_weight,
    conv_bias,
    dt_bias,
    decay_rate,
    skip_gain,
    out_weight,
    norm_gain,
    route_ids,
    route_weight,
    expert_slots,
    gate_weight,
    up_weight,
    down_weight,
):
    n = lax.axis_size("dp")
    m = lax.axis_size("z")
    d, zz, cc = lax.axis_index("dp"), lax.axis_index("z"), lax.axis_index("core")
    me = jnp.stack([d, zz, cc]).astype(jnp.int32)
    steps, rows, ch = x_input.shape
    per = rows // n
    taps = conv_cache.shape[1]
    states = state_cache.shape[1]
    total = steps * n * rows
    cap = total // 4
    pe = cap // (2 * m)
    rm = total // (n * 2 * m)
    width = gate_weight.shape[1]
    wc = out_weight.shape[1]
    dm = n * wc
    rr, ss = recv_row, send_slot
    vm = pl.BlockSpec(memory_space=pltpu.VMEM)
    sm = pl.BlockSpec(memory_space=pltpu.SMEM)

    in_hbm = functools.partial(pltpu.with_memory_space_constraint, memory_space=pltpu.HBM)

    def whole(a):
        return pl.BlockSpec(a.shape, lambda g: (0,) * a.ndim)

    src = (
        x_input,
        z_input,
        dt_input,
        jnp.transpose(b_input, (0, 2, 1)),
        jnp.transpose(c_input, (0, 2, 1)),
        prefix_length.reshape(1, rows),
    )
    src = [in_hbm(a) for a in src]
    packed = jax.ShapeDtypeStruct((per, 3 * steps * ch + META), BF)
    payload = pl.pallas_call(
        functools.partial(pack_kernel, n, per),
        grid=(1,),
        in_specs=[sm, sm] + [whole(a) for a in src],
        out_specs=[whole(packed)] * n,
        out_shape=[packed] * n,
        scratch_shapes=[pltpu.VMEM((128, rows), F32)],
        compiler_params=params(12),
        cost_estimate=cost(1e6, 2 << 20),
        name="pack",
    )(me, recv_row, *src)
    payload = [payload[0]] + [trade(payload[k], "dp", n, k) for k in range(1, n)]
    par = jnp.concatenate(
        [conv_weight, conv_bias[None], dt_bias[None], skip_gain[None], jnp.zeros((1, ch), F32)], 0
    )
    conv = jnp.transpose(conv_cache, (1, 0, 2))
    fixed = (par, decay_rate, conv, in_hbm(state_cache))
    y_buf, own_kept = ssm(0, n, per, steps, me, ss, payload[:1], *fixed, None)
    y_buf, *kept = ssm(1, n, per, steps, me, ss, payload[1:], *fixed, y_buf)
    kept = [own_kept] + kept
    y_own = y_buf.reshape(n * steps * per, ch)
    ys = [y_own] + [trade(y_own, "dp", n, k) for k in range(1, n)]

    n_slot, n_own = 2 * m * n * pe, 2 * m * n * rm
    ids_t = route_ids.reshape(total, -1).T
    wts_t = route_weight.reshape(total, -1).T
    meta_at = 3 * steps * ch // 128
    sel_slot, sel_own, share, expand = pl.pallas_call(
        functools.partial(select_kernel, n, m, per, steps, rows, rm, pe, width),
        grid=(1,),
        in_specs=[sm, sm]
        + [pl.BlockSpec(ids_t.shape, lambda g: (0, 0))] * 2
        + [pl.BlockSpec((per, 128), lambda g: (0, meta_at))] * n,
        out_specs=[
            pl.BlockSpec((n_slot, total), lambda g: (0, 0)),
            pl.BlockSpec((n_own, total), lambda g: (0, 0)),
            pl.BlockSpec((cap, 128), lambda g: (0, 0)),
            pl.BlockSpec((cap, total), lambda g: (0, 0)),
        ],
        out_shape=[
            jax.ShapeDtypeStruct((n_slot, total), BF),
            jax.ShapeDtypeStruct((n_own, total), BF),
            jax.ShapeDtypeStruct((cap, 128), F32),
            jax.ShapeDtypeStruct((cap, total), BF),
        ],
        compiler_params=params(10),
        cost_estimate=cost(1e7, 1 << 20),
        name="select",
    )(me, expert_slots, ids_t, wts_t, *payload)

    width = gate_weight.shape[1]
    chunks = 8
    gate_here, loaded = pl.pallas_call(
        functools.partial(load_kernel, chunks),
        in_specs=[pl.BlockSpec(memory_space=pltpu.HBM), pl.BlockSpec(memory_space=pl.ANY)],
        out_specs=[vm, vm],
        out_shape=[pltpu.VMEM(gate_weight.shape, BF), jax.ShapeDtypeStruct((8, 128), F32)],
        scratch_shapes=[pltpu.SemaphoreType.DMA((chunks,))],
        compiler_params=params(1),
        cost_estimate=cost(0, 4 * gate_weight.size),
        name="load",
    )(in_hbm(gate_weight), y_own)
    anyspace = pl.BlockSpec(memory_space=pl.ANY)

    def add_core(keep, send, each, name, dep=()):
        got = trade(send, "core", 2, 1)
        shape = (n * each, wc)
        outs = [(shape, F32)] + [(shape, BF)] * (m - 1)
        return small(functools.partial(pair_rows_kernel, m), name, outs, (keep, got), dep)

    def send_z(parts):
        return [parts[0]] + [trade(parts[k], "z", m, k) for k in range(1, m)]

    def add_z(got, each, name, dep=()):
        outs = [((each, wc), BF)] * n
        out = small(functools.partial(sum_rows_kernel, m, n), name, outs, got, dep)
        return [out[0]] + [trade(out[k], "dp", n, k) for k in range(1, n)]

    keep_slot, send_slot_rows = project(n, ys, sel_slot, out_weight, "project_slot", loaded)
    parts = add_core(keep_slot, send_slot_rows, pe, "core_slot")
    slot_z = send_z(parts)
    keep_own, send_own = project(n, ys, sel_own, out_weight, "project_own", slot_z[1])
    hid = add_z(slot_z, pe, "z_slot", (keep_own,))
    [normed] = small(
        functools.partial(norm_kernel, n),
        "norm",
        [((pe, dm), BF)],
        (me, norm_gain.reshape(1, dm), *hid),
    )
    near = [normed] + [trade(normed, "z", m, k) for k in range(1, m)]
    xs = []
    for piece in near:
        xs += [piece, trade(piece, "core", 2, 1)]
    own_parts = add_core(keep_own, send_own, rm, "core_own", (near[1],))
    held = pl.pallas_call(
        hold_kernel,
        in_specs=[anyspace] * n,
        out_specs=[anyspace] * (n - 1),
        out_shape=[jax.ShapeDtypeStruct(k.shape, k.dtype) for k in kept[1:]],
        input_output_aliases={k: k for k in range(n - 1)},
        compiler_params=params(1),
        name="hold",
    )(*kept[1:], normed)
    back = [kept[0]] + [trade(held[k - 1], "dp", n, k) for k in range(1, n)]

    half = dm // 2
    pc = half // m
    ub = 256 if width % 256 == 0 else 128
    act = pl.pallas_call(
        functools.partial(gate_kernel, m),
        in_specs=[sm] + [vm] * (2 * m + 2) + [pl.BlockSpec(memory_space=pltpu.HBM)],
        out_specs=vm,
        out_shape=jax.ShapeDtypeStruct((cap, width), BF),
        scratch_shapes=[
            pltpu.VMEM((cap, dm), BF),
            pltpu.VMEM((2, dm, ub), BF),
            pltpu.SemaphoreType.DMA((2,)),
        ],
        compiler_params=params(14),
        cost_estimate=cost(4 * cap * dm * width, 4 * dm * width),
        name="gate",
    )(me, *xs, share, gate_here, in_hbm(up_weight))
    own_z = send_z(own_parts)
    own = add_z(own_z, rm, "z_own", (act,))
    deps = own_z[1:] + back[1:]
    send, keep = pl.pallas_call(
        functools.partial(down_kernel, m, len(deps)),
        in_specs=[sm, vm, pl.BlockSpec(memory_space=pltpu.HBM)] + [anyspace] * len(deps),
        out_specs=[vm] * 2,
        out_shape=[jax.ShapeDtypeStruct((cap, half), BF)] * 2,
        scratch_shapes=[pltpu.VMEM((3, width, pc), BF), pltpu.SemaphoreType.DMA((3,))],
        compiler_params=params(14),
        cost_estimate=cost(2 * cap * dm * width, 2 * dm * width),
        name="down",
    )(me, act, in_hbm(down_weight), *deps)

    got = trade(send, "core", 2, 1)
    outs = [((cap, pc), F32)] + [((cap, pc), BF)] * (m - 1)
    cols = small(functools.partial(pair_cols_kernel, m), "core_out", outs, (keep, got))
    moved = [cols[0]] + [trade(cols[k], "z", m, k) for k in range(1, m)]

    new_state, placed = place(n, per, rows, states, me, rr, back, cols[1])
    low = kept[0].shape[0] - per * states
    tail_at = per * states // low
    new_tail, placed = pl.pallas_call(
        functools.partial(tail_kernel, n, per, taps),
        grid=(1,),
        in_specs=[sm, sm, pl.BlockSpec(x_input.shape, lambda g: (0, 0, 0))]
        + [pl.BlockSpec((low, ch), lambda g: (tail_at, 0))] * n
        + [anyspace],
        out_specs=[
            pl.BlockSpec((taps, rows, ch), lambda g: (0, 0, 0)),
            pl.BlockSpec((8, 128), lambda g: (0, 0)),
        ],
        out_shape=[
            jax.ShapeDtypeStruct((taps, rows, ch), F32),
            jax.ShapeDtypeStruct((8, 128), F32),
        ],
        compiler_params=params(16),
        cost_estimate=cost(1e5, 1 << 20),
        name="tail",
    )(me, rr, x_input, *back, placed)

    share_rows = total // n
    outs = [((share_rows, pc), F32)] + [((share_rows, pc), BF)] * (n - 1)
    rows_out = small(
        functools.partial(spread_kernel, n, m),
        "spread",
        outs,
        (me, expand, *moved),
        (placed,),
        [pltpu.VMEM((total, pc), F32)],
    )
    mine = [rows_out[0]] + [trade(rows_out[k], "dp", n, k) for k in range(1, n)]
    deal_keep, deal_send = small(
        functools.partial(deal_kernel, n, m),
        "deal",
        [((m * rm, pc), BF)] * 2,
        (me, *mine),
        (),
        [pltpu.VMEM((share_rows, pc), F32)],
    )
    pieces = small(
        functools.partial(pair_kernel, m),
        "pair",
        [((rm, 2 * pc), BF)] * m,
        (deal_keep, trade(deal_send, "core", 2, 1)),
    )
    pieces = send_z(pieces)
    [mixed] = small(
        functools.partial(final_kernel, n, m),
        "final",
        [((rm, dm), BF)],
        (me, *own, *pieces),
        (),
        [pltpu.VMEM((rm, dm), F32)],
    )
    return (mixed, new_state, jnp.transpose(new_tail, (1, 0, 2)))


def solution(mesh):
    n = mesh.shape["dp"]
    m = mesh.shape["expert"] // 2
    split = Mesh(mesh.devices.reshape(n, m, 2), ("dp", "z", "core"))
    e = ("z", "core")
    de = ("dp", "z", "core")
    in_specs = (
        P("dp", None, e),
        P("dp", None, e),
        P(),
        P("dp", None, None),
        P("dp"),
        P(None, "dp", e),
        P(None, "dp", e),
        P(None, "dp", e),
        P(None, "dp", None),
        P(None, "dp", None),
        P(None, e),
        P(e),
        P(e),
        P(None, e),
        P(e),
        P(e, "dp"),
        P(),
        P(),
        P(),
        P(),
        P(None, de),
        P(None, de),
        P(de, None),
    )
    out_specs = (P(de, None), P("dp", None, e), P("dp", None, e))
    return jax.shard_map(body, mesh=split, in_specs=in_specs, out_specs=out_specs, check_vma=False)
```

time: 205 us -> 160 us (0.78)
  waiting for transfers between devices: 61.4 us -> 38 us
  local copies, waits for them, and re-layouts: 14 us -> 4.33 us
  Pallas kernels: 74.8 us -> 68.4 us
  other arithmetic: 3.43 us -> 0.08 us
    ppermute x44 -> x41, waiting for transfers between devices: 61.4 us -> 38 us  [trade(): return lax.ppermute(piece, axis, [(i, i ^ k) for i in range(size)])]
    unnamed x36 -> x30, local copies, waits for them, and re-layouts: 10 us -> 3.48 us
    pallas_call x14 -> x20, Pallas kernels: 72.2 us -> 65.7 us  [the longest x1 17.3 us: body(): pl.pallas_call(functools.partial(gate_kernel, m), in_specs=[sm] + [vm] *...]
    convert_element_type x7 -> x0, other arithmetic: 2.81 us -> none  [the longest x2 1.38 us: reduce_rows(): narrow = both.astype(BF)]
    ppermute x44 -> x41, starting transfers between devices: 48.8 us -> 48.1 us  [trade(): return lax.ppermute(piece, axis, [(i, i ^ k) for i in range(size)])]
  transfers between devices with their start and end apart: 44 -> 41, of which waited for: 19 -> 19; matrix products, arithmetic and copies ran while one was open for 2% -> 1% of each run, Pallas kernels for 31% -> 25%
where the time goes in v2:
time: 160 us
  Pallas kernels  68.4 us (43%)
  starting transfers between devices  48.1 us (30%)
  waiting for transfers between devices  38 us (24%)
  local copies, waits for them, and re-layouts  4.33 us (3%)
    ppermute x41, starting transfers between devices, trade(): return lax.ppermute(piece, axis, [(i, i ^ k) for i in range(size)])  48.1 us
    ppermute x41, waiting for transfers between devices, trade(): return lax.ppermute(piece, axis, [(i, i ^ k) for i in range(size)])  38 us
    pallas_call x1, Pallas kernels, body(): pl.pallas_call(functools.partial(gate_kernel, m), in_specs=[sm] + [vm] *...  17.3 us
    pallas_call x2, Pallas kernels, ssm(): pl.pallas_call(functools.partial(ssm_kernel, first, groups, n, per, steps...  13.8 us
    pallas_call x1, Pallas kernels, body(): pl.pallas_call(functools.partial(down_kernel, m, len(deps)), in_specs=[sm...  9.9 us
    pallas_call x1, Pallas kernels, body(): pl.pallas_call(functools.partial(load_kernel, chunks), in_specs=[pl.Block...  8.33 us
    pallas_call x2, Pallas kernels, project(): pl.pallas_call(functools.partial(project_kernel, n), in_specs=[vm] * (n +...  6.69 us
    pallas_call x1, Pallas kernels, place(): pl.pallas_call(functools.partial(place_kernel, n, states), grid_spec=pltp...  4.1 us
  transfers between devices with their start and end apart: 41, of which 19 were waited for; matrix products, arithmetic and copies ran while one was open for 1% of the time, Pallas kernels for 25%

profile of v2, /device:TPU:0, one launch (start us, length us, event | category | flops | bytes accessed | tf_op | source)
XLA Modules:
  0.0 159.9 jit_solution(14995640971903716625)
XLA Ops:
  1.4 1.6 pack.1
  3.0 3.0 %collective-permute-start = (bf16[8,12544]{1,0:T(8,128)(2,1)S(1)}, bf16[8,12544]{1,0:T(8,128)(2,1)S(1)}, u32[]{:S(2)}, u32[]{:S(2)}) collective-permute-start(bf16[8,12544]{1,0:T(8,128)(2,1)S(1)} %get-tuple-element.64), channel_id=1, source_target_pairs={{0,8},{8,0},{16,24},{24,16},{1,9},{9,1},{17,25},{25,17},{2,10},{10... | collective-permute-start | bytes 602120 | tf_op jit(solution)/shard_map/ppermute | solution.py:34
  11.1 3.5 %ssm0.1 = (bf16[4,16,2048]{2,1,0:T(8,128)(2,1)S(1)}, f32[144,2048]{1,0:T(8,128)S(1)}) custom-call(s32[3]{0:T(128)S(1)} %pad_add_fusion.me.refs_0_, s32[4,4,8]{2,1,0:T(4,128)S(1)} %copy-done.7, bf16[8,12544]{1,0:T(8,128)(2,1)S(1)} %get-tuple-element.62.refs_0_.refs_1_.refs_2_.refs_3_.refs_4_.refs_5_.refs_6_, ...), custom_call_target="tpu_custom_call" | custom-call | flops 3000000 | bytes 3145728 | tf_op jit(solution)/shard_map/ssm0/pallas_call | solution.py:194
  14.6 2.1 %collective-permute-done.1.refs_8_.refs_9_.refs_10_.refs_11_.refs_12_.refs_13_.refs_14_.refs_2_ = bf16[8,12544]{1,0:T(8,128)(2,1)S(1)} collective-permute-done((bf16[8,12544]{1,0:T(8,128)(2,1)S(1)}, bf16[8,12544]{1,0:T(8,128)(2,1)S(1)}, u32[]{:S(2)}, u32[]{:S(2)}) %collective-permute-start.1) | collective-permute-done | bytes 200736 | tf_op jit(solution)/shard_map/ppermute | solution.py:34
  16.8 10.3 %ssm1.1 = (bf16[4,16,2048]{2,1,0:T(8,128)(2,1)S(1)}, bf16[144,2048]{1,0:T(8,128)(2,1)S(1)}, bf16[144,2048]{1,0:T(8,128)(2,1)S(1)}, bf16[144,2048]{1,0:T(8,128)(2,1)S(1)}) custom-call(s32[3]{0:T(128)S(1)} %pad_add_fusion.me.refs_0_, s32[4,4,8]{2,1,0:T(4,128)S(1)} %copy-done.7, ...), custom_call_target="tpu_custom_call", output_to_operand_aliasing={{0}: (2, {})} | custom-call | flops 9000000 | bytes 9437184 | tf_op jit(solution)/shard_map/ssm1/pallas_call | solution.py:194
  30.7 8.3 %load.1 = (bf16[8192,1536]{1,0:T(8,128)(2,1)S(1)}, f32[8,128]{1,0:T(8,128)S(1)}) custom-call(bf16[8192,1536]{1,0:T(8,128)(2,1)} %w.1, bf16[64,2048]{1,0:T(8,128)(2,1)S(1)} %bitcast.24), custom_call_target="tpu_custom_call" | custom-call | bytes 50331648 | tf_op jit(solution)/shard_map/load/pallas_call | solution.py:715
  41.0 3.3 %project_slot.1 = (bf16[128,2048]{1,0:T(8,128)(2,1)S(1)}, bf16[128,2048]{1,0:T(8,128)(2,1)S(1)}) custom-call(bf16[64,2048]{1,0:T(8,128)(2,1)S(1)} %bitcast.25, bf16[64,2048]{1,0:T(8,128)(2,1)S(1)} %collective-permute-done.3.refs_1_, bf16[64,2048]{1,0:T(8,128)(2,1)S(1)} %collective-permute-done.4.refs_2_, ...), custom_call_target="tpu_custom_call" | custom-call | flops 2147483648 | bytes 8388608 | tf_op jit(solution)/shard_map/project_slot/pallas_call | solution.py:308
  44.4 1.9 %collective-permute-done.6.refs_1_ = bf16[128,2048]{1,0:T(8,128)(2,1)S(1)} collective-permute-done((bf16[128,2048]{1,0:T(8,128)(2,1)S(1)}, bf16[128,2048]{1,0:T(8,128)(2,1)S(1)}, u32[]{:S(2)}, u32[]{:S(2)}) %collective-permute-start.6) | collective-permute-done | bytes 524320 | tf_op jit(solution)/shard_map/ppermute | solution.py:34
  46.4 1.7 %collective-permute-start.7 = (bf16[32,2048]{1,0:T(8,128)(2,1)S(1)}, bf16[32,2048]{1,0:T(8,128)(2,1)S(1)}, u32[]{:S(2)}, u32[]{:S(2)}) collective-permute-start(bf16[32,2048]{1,0:T(8,128)(2,1)S(1)} %get-tuple-element.73), channel_id=1, source_target_pairs={{0,2},{2,0},{4,6},{6,4},{1,3},{3,1},{5,7},{7,5},{8,10},{10,8},{12,... | collective-permute-start | bytes 393224 | tf_op jit(solution)/shard_map/ppermute | solution.py:34
  48.1 2.6 %collective-permute-start.9 = (bf16[32,2048]{1,0:T(8,128)(2,1)S(1)}, bf16[32,2048]{1,0:T(8,128)(2,1)S(1)}, u32[]{:S(2)}, u32[]{:S(2)}) collective-permute-start(bf16[32,2048]{1,0:T(8,128)(2,1)S(1)} %get-tuple-element.77), channel_id=1, source_target_pairs={{0,4},{2,6},{4,0},{6,2},{1,5},{3,7},{5,1},{7,3},{8,12},{10,14},{12... | collective-permute-start | bytes 393224 | tf_op jit(solution)/shard_map/ppermute | solution.py:34
  50.9 3.1 %collective-permute-done.7.refs_6_.refs_1_ = bf16[32,2048]{1,0:T(8,128)(2,1)S(1)} collective-permute-done((bf16[32,2048]{1,0:T(8,128)(2,1)S(1)}, bf16[32,2048]{1,0:T(8,128)(2,1)S(1)}, u32[]{:S(2)}, u32[]{:S(2)}) %collective-permute-start.7) | collective-permute-done | bytes 131104 | tf_op jit(solution)/shard_map/ppermute | solution.py:34
  53.9 3.3 %project_own.1 = (bf16[128,2048]{1,0:T(8,128)(2,1)S(1)}, bf16[128,2048]{1,0:T(8,128)(2,1)S(1)}) custom-call(bf16[64,2048]{1,0:T(8,128)(2,1)S(1)} %bitcast.26, bf16[64,2048]{1,0:T(8,128)(2,1)S(1)} %collective-permute-done.3.refs_1_, bf16[64,2048]{1,0:T(8,128)(2,1)S(1)} %collective-permute-done.4.refs_2_, bf16[64,2048]{1,0:T(8,128)(2,1)S(1)} %collective-permute-done.5.refs_3_, ...), custom_call_target="tpu_custom_call" | custom-call | flops 2147483648 | bytes 8388608 | tf_op jit(solution)/shard_map/project_own/pallas_call | solution.py:308
  57.4 3.6 %collective-permute-done.9.refs_2_ = bf16[32,2048]{1,0:T(8,128)(2,1)S(1)} collective-permute-done((bf16[32,2048]{1,0:T(8,128)(2,1)S(1)}, bf16[32,2048]{1,0:T(8,128)(2,1)S(1)}, u32[]{:S(2)}, u32[]{:S(2)}) %collective-permute-start.9) | collective-permute-done | bytes 131104 | tf_op jit(solution)/shard_map/ppermute | solution.py:34
  62.9 1.7 %collective-permute-start.13 = (bf16[8,2048]{1,0:T(8,128)(2,1)S(1)}, bf16[8,2048]{1,0:T(8,128)(2,1)S(1)}, u32[]{:S(2)}, u32[]{:S(2)}) collective-permute-start(bf16[8,2048]{1,0:T(8,128)(2,1)S(1)} %get-tuple-element.82), channel_id=1, source_target_pairs={{0,24},{8,16},{16,8},{24,0},{1,25},{9,17},{17,9},{25,1},{2,26},{10... | collective-permute-start | bytes 98312 | tf_op jit(solution)/shard_map/ppermute | solution.py:34
  65.6 2.1 %collective-permute-done.13.refs_5_ = bf16[8,2048]{1,0:T(8,128)(2,1)S(1)} collective-permute-done((bf16[8,2048]{1,0:T(8,128)(2,1)S(1)}, bf16[8,2048]{1,0:T(8,128)(2,1)S(1)}, u32[]{:S(2)}, u32[]{:S(2)}) %collective-permute-start.13) | collective-permute-done | bytes 32800 | tf_op jit(solution)/shard_map/ppermute | solution.py:34
  69.5 2.3 %collective-permute-start.14 = (bf16[8,8192]{1,0:T(8,128)(2,1)S(1)}, bf16[8,8192]{1,0:T(8,128)(2,1)S(1)}, u32[]{:S(2)}, u32[]{:S(2)}) collective-permute-start(bf16[8,8192]{1,0:T(8,128)(2,1)S(1)} %norm.1.refs_0_.refs_3_), channel_id=1, source_target_pairs={{0,2},{2,0},{4,6},{6,4},{1,3},{3,1},{5,7},{7,5},{8,10},{10,8},{12,... | collective-permute-start | bytes 393224 | tf_op jit(solution)/shard_map/ppermute | solution.py:34
  72.8 2.4 %collective-permute-done.14.refs_2_ = bf16[8,8192]{1,0:T(8,128)(2,1)S(1)} collective-permute-done((bf16[8,8192]{1,0:T(8,128)(2,1)S(1)}, bf16[8,8192]{1,0:T(8,128)(2,1)S(1)}, u32[]{:S(2)}, u32[]{:S(2)}) %collective-permute-start.14) | collective-permute-done | bytes 131104 | tf_op jit(solution)/shard_map/ppermute | solution.py:34
  75.2 3.0 %collective-permute-start.22 = (bf16[8,8192]{1,0:T(8,128)(2,1)S(1)}, bf16[8,8192]{1,0:T(8,128)(2,1)S(1)}, u32[]{:S(2)}, u32[]{:S(2)}) collective-permute-start(bf16[8,8192]{1,0:T(8,128)(2,1)S(1)} %norm.1.refs_0_.refs_3_), channel_id=1, source_target_pairs={{0,6},{2,4},{4,2},{6,0},{1,7},{3,5},{5,3},{7,1},{8,14},{10,12},{12... | collective-permute-start | bytes 393224 | tf_op jit(solution)/shard_map/ppermute | solution.py:34
  79.4 4.9 %collective-permute-done.20.refs_4_ = bf16[8,8192]{1,0:T(8,128)(2,1)S(1)} collective-permute-done((bf16[8,8192]{1,0:T(8,128)(2,1)S(1)}, bf16[8,8192]{1,0:T(8,128)(2,1)S(1)}, u32[]{:S(2)}, u32[]{:S(2)}) %collective-permute-start.20) | collective-permute-done | bytes 131104 | tf_op jit(solution)/shard_map/ppermute | solution.py:34
  88.2 1.9 %collective-permute-start.15 = (bf16[32,2048]{1,0:T(8,128)(2,1)S(1)}, bf16[32,2048]{1,0:T(8,128)(2,1)S(1)}, u32[]{:S(2)}, u32[]{:S(2)}) collective-permute-start(bf16[32,2048]{1,0:T(8,128)(2,1)S(1)} %get-tuple-element.84), channel_id=1, source_target_pairs={{0,2},{2,0},{4,6},{6,4},{1,3},{3,1},{5,7},{7,5},{8,10},{10,8},{12,... | collective-permute-start | bytes 393224 | tf_op jit(solution)/shard_map/ppermute | solution.py:34
  92.7 17.3 %gate.1.refs_4_.act = bf16[64,1536]{1,0:T(8,128)(2,1)S(1)} custom-call(s32[3]{0:T(128)S(1)} %pad_add_fusion.me.refs_0_, bf16[8,8192]{1,0:T(8,128)(2,1)S(1)} %norm.1.refs_0_.refs_3_, bf16[8,8192]{1,0:T(8,128)(2,1)S(1)} %collective-permute-done.18.refs_1_, bf16[8,8192]{1,0:T(8,128)(2,1)S(1)} %collective-permute-done.14.refs_2_, ...), custom_call_target="tpu_custom_call" | custom-call | flops 3221225472 | bytes 50331648 | tf_op jit(solution)/shard_map/gate/pallas_call | solution.py:771
  110.1 9.9 %down.1 = (bf16[64,4096]{1,0:T(8,128)(2,1)S(1)}, bf16[64,4096]{1,0:T(8,128)(2,1)S(1)}) custom-call(s32[3]{0:T(128)S(1)} %pad_add_fusion.me.refs_0_, bf16[64,1536]{1,0:T(8,128)(2,1)S(1)} %gate.1.refs_4_.act, bf16[1536,8192]{1,0:T(8,128)(2,1)} %dw.1, bf16[32,2048]{1,0:T(8,128)(2,1)S(1)} %collective-permute-done.15.refs_1_.refs_0_, ...), custom_call_target="tpu_custom_call" | custom-call | flops 1610612736 | bytes 25165824 | tf_op jit(solution)/shard_map/down/pallas_call | solution.py:788
  120.1 1.9 %collective-permute-done.30.refs_1_ = bf16[64,4096]{1,0:T(8,128)(2,1)S(1)} collective-permute-done((bf16[64,4096]{1,0:T(8,128)(2,1)S(1)}, bf16[64,4096]{1,0:T(8,128)(2,1)S(1)}, u32[]{:S(2)}, u32[]{:S(2)}) %collective-permute-start.30) | collective-permute-done | bytes 524320 | tf_op jit(solution)/shard_map/ppermute | solution.py:34
  123.1 2.0 %collective-permute-start.32 = (bf16[64,1024]{1,0:T(8,128)(2,1)S(1)}, bf16[64,1024]{1,0:T(8,128)(2,1)S(1)}, u32[]{:S(2)}, u32[]{:S(2)}) collective-permute-start(bf16[64,1024]{1,0:T(8,128)(2,1)S(1)} %get-tuple-element.104), channel_id=1, source_target_pairs={{0,4},{2,6},{4,0},{6,2},{1,5},{3,7},{5,1},{7,3},{8,12},{10,14},{12... | collective-permute-start | bytes 393224 | tf_op jit(solution)/shard_map/ppermute | solution.py:34
  126.6 4.1 %place.1 = (f32[32,16,2048]{2,1,0:T(8,128)}, f32[8,128]{1,0:T(8,128)S(1)}) custom-call(s32[3]{0:T(128)S(1)} %pad_add_fusion.me.refs_0_, s32[1,4,8]{2,1,0:T(4,128)S(1)} %copy-done.9, f32[144,2048]{1,0:T(8,128)S(1)} %get-tuple-element.106.refs_0_, bf16[144,2048]{1,0:T(8,128)(2,1)S(1)} %collective-permute-done.27.refs_3_.refs_1_, ...), custom_call_target="tpu_custom_call" | custom-call | flops 100000 | bytes 8388608 | tf_op jit(solution)/shard_map/place/pallas_call | solution.py:547
  130.7 1.5 tail.1
  132.2 3.8 %collective-permute-done.32.refs_4_ = bf16[64,1024]{1,0:T(8,128)(2,1)S(1)} collective-permute-done((bf16[64,1024]{1,0:T(8,128)(2,1)S(1)}, bf16[64,1024]{1,0:T(8,128)(2,1)S(1)}, u32[]{:S(2)}, u32[]{:S(2)}) %collective-permute-start.32) | collective-permute-done | bytes 131104 | tf_op jit(solution)/shard_map/ppermute | solution.py:34
  138.8 1.7 %collective-permute-start.36 = (bf16[64,1024]{1,0:T(8,128)(2,1)S(1)}, bf16[64,1024]{1,0:T(8,128)(2,1)S(1)}, u32[]{:S(2)}, u32[]{:S(2)}) collective-permute-start(bf16[64,1024]{1,0:T(8,128)(2,1)S(1)} %get-tuple-element.112), channel_id=1, source_target_pairs={{0,24},{8,16},{16,8},{24,0},{1,25},{9,17},{17,9},{25,1},{2,26},{10... | collective-permute-start | bytes 393224 | tf_op jit(solution)/shard_map/ppermute | solution.py:34
  140.5 1.7 %collective-permute-done.34.refs_2_ = bf16[64,1024]{1,0:T(8,128)(2,1)S(1)} collective-permute-done((bf16[64,1024]{1,0:T(8,128)(2,1)S(1)}, bf16[64,1024]{1,0:T(8,128)(2,1)S(1)}, u32[]{:S(2)}, u32[]{:S(2)}) %collective-permute-start.34) | collective-permute-done | bytes 131104 | tf_op jit(solution)/shard_map/ppermute | solution.py:34
  143.0 1.7 %collective-permute-done.36.refs_4_ = bf16[64,1024]{1,0:T(8,128)(2,1)S(1)} collective-permute-done((bf16[64,1024]{1,0:T(8,128)(2,1)S(1)}, bf16[64,1024]{1,0:T(8,128)(2,1)S(1)}, u32[]{:S(2)}, u32[]{:S(2)}) %collective-permute-start.36) | collective-permute-done | bytes 131104 | tf_op jit(solution)/shard_map/ppermute | solution.py:34
  149.1 2.9 %collective-permute-start.38 = (bf16[8,2048]{1,0:T(8,128)(2,1)S(1)}, bf16[8,2048]{1,0:T(8,128)(2,1)S(1)}, u32[]{:S(2)}, u32[]{:S(2)}) collective-permute-start(bf16[8,2048]{1,0:T(8,128)(2,1)S(1)} %get-tuple-element.116), channel_id=1, source_target_pairs={{0,2},{2,0},{4,6},{6,4},{1,3},{3,1},{5,7},{7,5},{8,10},{10,8},{12,... | collective-permute-start | bytes 98312 | tf_op jit(solution)/shard_map/ppermute | solution.py:34
  154.4 3.0 %collective-permute-done.39.refs_7_ = bf16[8,2048]{1,0:T(8,128)(2,1)S(1)} collective-permute-done((bf16[8,2048]{1,0:T(8,128)(2,1)S(1)}, bf16[8,2048]{1,0:T(8,128)(2,1)S(1)}, u32[]{:S(2)}, u32[]{:S(2)}) %collective-permute-start.39) | collective-permute-done | bytes 32800 | tf_op jit(solution)/shard_map/ppermute | solution.py:34
  (106 shorter events, 40.8 us)
Async XLA Ops:
  3.0 11.6 %collective-permute-start = (bf16[8,12544]{1,0:T(8,128)(2,1)S(1)}, bf16[8,12544]{1,0:T(8,128)(2,1)S(1)}, u32[]{:S(2)}, u32[]{:S(2)}) collective-permute-start(bf16[8,12544]{1,0:T(8,128)(2,1)S(1)} %get-tuple-element.64), channel_id=1, source_target_pairs={{0,8},{8,0},{16,24},{24,16},{1,9},{9,1},{17,25},{25,17},{2,10},{10... | collective-permute-start | bytes 602120 | tf_op jit(solution)/shard_map/ppermute | solution.py:34
  6.0 10.8 %collective-permute-start.1 = (bf16[8,12544]{1,0:T(8,128)(2,1)S(1)}, bf16[8,12544]{1,0:T(8,128)(2,1)S(1)}, u32[]{:S(2)}, u32[]{:S(2)}) collective-permute-start(bf16[8,12544]{1,0:T(8,128)(2,1)S(1)} %get-tuple-element.65), channel_id=1, source_target_pairs={{0,16},{8,24},{16,0},{24,8},{1,17},{9,25},{17,1},{25,9},{2,18},{10... | collective-permute-start | bytes 602120 | tf_op jit(solution)/shard_map/ppermute | solution.py:34
  7.5 9.2 %collective-permute-start.2 = (bf16[8,12544]{1,0:T(8,128)(2,1)S(1)}, bf16[8,12544]{1,0:T(8,128)(2,1)S(1)}, u32[]{:S(2)}, u32[]{:S(2)}) collective-permute-start(bf16[8,12544]{1,0:T(8,128)(2,1)S(1)} %get-tuple-element.66), channel_id=1, source_target_pairs={{0,24},{8,16},{16,8},{24,0},{1,25},{9,17},{17,9},{25,1},{2,26},{10... | collective-permute-start | bytes 602120 | tf_op jit(solution)/shard_map/ppermute | solution.py:34
  27.2 13.0 %collective-permute-start.3 = (bf16[64,2048]{1,0:T(8,128)(2,1)S(1)}, bf16[64,2048]{1,0:T(8,128)(2,1)S(1)}, u32[]{:S(2)}, u32[]{:S(2)}) collective-permute-start(bf16[64,2048]{1,0:T(8,128)(2,1)S(1)} %bitcast.21), channel_id=1, source_target_pairs={{0,8},{8,0},{16,24},{24,16},{1,9},{9,1},{17,25},{25,17},{2,10},{10... | collective-permute-start | bytes 786440 | tf_op jit(solution)/shard_map/ppermute | solution.py:34
  28.4 12.5 %collective-permute-start.4 = (bf16[64,2048]{1,0:T(8,128)(2,1)S(1)}, bf16[64,2048]{1,0:T(8,128)(2,1)S(1)}, u32[]{:S(2)}, u32[]{:S(2)}) collective-permute-start(bf16[64,2048]{1,0:T(8,128)(2,1)S(1)} %bitcast.22), channel_id=1, source_target_pairs={{0,16},{8,24},{16,0},{24,8},{1,17},{9,25},{17,1},{25,9},{2,18},{10... | collective-permute-start | bytes 786440 | tf_op jit(solution)/shard_map/ppermute | solution.py:34
  29.3 11.7 %collective-permute-start.5 = (bf16[64,2048]{1,0:T(8,128)(2,1)S(1)}, bf16[64,2048]{1,0:T(8,128)(2,1)S(1)}, u32[]{:S(2)}, u32[]{:S(2)}) collective-permute-start(bf16[64,2048]{1,0:T(8,128)(2,1)S(1)} %bitcast.23), channel_id=1, source_target_pairs={{0,24},{8,16},{16,8},{24,0},{1,25},{9,17},{17,9},{25,1},{2,26},{10... | collective-permute-start | bytes 786440 | tf_op jit(solution)/shard_map/ppermute | solution.py:34
  46.4 7.5 %collective-permute-start.7 = (bf16[32,2048]{1,0:T(8,128)(2,1)S(1)}, bf16[32,2048]{1,0:T(8,128)(2,1)S(1)}, u32[]{:S(2)}, u32[]{:S(2)}) collective-permute-start(bf16[32,2048]{1,0:T(8,128)(2,1)S(1)} %get-tuple-element.73), channel_id=1, source_target_pairs={{0,2},{2,0},{4,6},{6,4},{1,3},{3,1},{5,7},{7,5},{8,10},{10,8},{12,... | collective-permute-start | bytes 393224 | tf_op jit(solution)/shard_map/ppermute | solution.py:34
  48.1 12.9 %collective-permute-start.9 = (bf16[32,2048]{1,0:T(8,128)(2,1)S(1)}, bf16[32,2048]{1,0:T(8,128)(2,1)S(1)}, u32[]{:S(2)}, u32[]{:S(2)}) collective-permute-start(bf16[32,2048]{1,0:T(8,128)(2,1)S(1)} %get-tuple-element.77), channel_id=1, source_target_pairs={{0,4},{2,6},{4,0},{6,2},{1,5},{3,7},{5,1},{7,3},{8,12},{10,14},{12... | collective-permute-start | bytes 393224 | tf_op jit(solution)/shard_map/ppermute | solution.py:34
  50.7 10.3 %collective-permute-start.10 = (bf16[32,2048]{1,0:T(8,128)(2,1)S(1)}, bf16[32,2048]{1,0:T(8,128)(2,1)S(1)}, u32[]{:S(2)}, u32[]{:S(2)}) collective-permute-start(bf16[32,2048]{1,0:T(8,128)(2,1)S(1)} %get-tuple-element.78), channel_id=1, source_target_pairs={{0,6},{2,4},{4,2},{6,0},{1,7},{3,5},{5,3},{7,1},{8,14},{10,12},{12... | collective-permute-start | bytes 393224 | tf_op jit(solution)/shard_map/ppermute | solution.py:34
  57.3 29.7 %collective-permute-start.8 = (bf16[128,2048]{1,0:T(8,128)(2,1)S(1)}, bf16[128,2048]{1,0:T(8,128)(2,1)S(1)}, u32[]{:S(2)}, u32[]{:S(2)}) collective-permute-start(bf16[128,2048]{1,0:T(8,128)(2,1)S(1)} %get-tuple-element.75), channel_id=1, source_target_pairs={{0,1},{1,0},{2,3},{3,2},{4,5},{5,4},{6,7},{7,6},{8,9},{9,8},{10,11... | collective-permute-start | bytes 1572872 | tf_op jit(solution)/shard_map/ppermute | solution.py:34
  68.4 22.7 %collective-permute-start.27 = (bf16[144,2048]{1,0:T(8,128)(2,1)S(1)}, bf16[144,2048]{1,0:T(8,128)(2,1)S(1)}, u32[]{:S(2)}, u32[]{:S(2)}) collective-permute-start(bf16[144,2048]{1,0:T(8,128)(2,1)S(1)} %get-tuple-element.97), channel_id=1, source_target_pairs={{0,8},{8,0},{16,24},{24,16},{1,9},{9,1},{17,25},{25,17},{2,10},{10... | collective-permute-start | bytes 1769480 | tf_op jit(solution)/shard_map/ppermute | solution.py:34
  69.5 5.7 %collective-permute-start.14 = (bf16[8,8192]{1,0:T(8,128)(2,1)S(1)}, bf16[8,8192]{1,0:T(8,128)(2,1)S(1)}, u32[]{:S(2)}, u32[]{:S(2)}) collective-permute-start(bf16[8,8192]{1,0:T(8,128)(2,1)S(1)} %norm.1.refs_0_.refs_3_), channel_id=1, source_target_pairs={{0,2},{2,0},{4,6},{6,4},{1,3},{3,1},{5,7},{7,5},{8,10},{10,8},{12,... | collective-permute-start | bytes 393224 | tf_op jit(solution)/shard_map/ppermute | solution.py:34
  71.8 6.4 %collective-permute-start.18 = (bf16[8,8192]{1,0:T(8,128)(2,1)S(1)}, bf16[8,8192]{1,0:T(8,128)(2,1)S(1)}, u32[]{:S(2)}, u32[]{:S(2)}) collective-permute-start(bf16[8,8192]{1,0:T(8,128)(2,1)S(1)} %norm.1.refs_0_.refs_3_), channel_id=1, source_target_pairs={{0,1},{1,0},{2,3},{3,2},{4,5},{5,4},{6,7},{7,6},{8,9},{9,8},{10,11... | collective-permute-start | bytes 393224 | tf_op jit(solution)/shard_map/ppermute | solution.py:34
  71.8 12.5 %collective-permute-start.20 = (bf16[8,8192]{1,0:T(8,128)(2,1)S(1)}, bf16[8,8192]{1,0:T(8,128)(2,1)S(1)}, u32[]{:S(2)}, u32[]{:S(2)}) collective-permute-start(bf16[8,8192]{1,0:T(8,128)(2,1)S(1)} %norm.1.refs_0_.refs_3_), channel_id=1, source_target_pairs={{0,4},{2,6},{4,0},{6,2},{1,5},{3,7},{5,1},{7,3},{8,12},{10,14},{12... | collective-permute-start | bytes 393224 | tf_op jit(solution)/shard_map/ppermute | solution.py:34
  75.2 10.4 %collective-permute-start.22 = (bf16[8,8192]{1,0:T(8,128)(2,1)S(1)}, bf16[8,8192]{1,0:T(8,128)(2,1)S(1)}, u32[]{:S(2)}, u32[]{:S(2)}) collective-permute-start(bf16[8,8192]{1,0:T(8,128)(2,1)S(1)} %norm.1.refs_0_.refs_3_), channel_id=1, source_target_pairs={{0,6},{2,4},{4,2},{6,0},{1,7},{3,5},{5,3},{7,1},{8,14},{10,12},{12... | collective-permute-start | bytes 393224 | tf_op jit(solution)/shard_map/ppermute | solution.py:34
  78.2 31.9 %collective-permute-start.28 = (bf16[144,2048]{1,0:T(8,128)(2,1)S(1)}, bf16[144,2048]{1,0:T(8,128)(2,1)S(1)}, u32[]{:S(2)}, u32[]{:S(2)}) collective-permute-start(bf16[144,2048]{1,0:T(8,128)(2,1)S(1)} %get-tuple-element.98), channel_id=1, source_target_pairs={{0,16},{8,24},{16,0},{24,8},{1,17},{9,25},{17,1},{25,9},{2,18},{10... | collective-permute-start | bytes 1769480 | tf_op jit(solution)/shard_map/ppermute | solution.py:34
  84.3 25.8 %collective-permute-start.29 = (bf16[144,2048]{1,0:T(8,128)(2,1)S(1)}, bf16[144,2048]{1,0:T(8,128)(2,1)S(1)}, u32[]{:S(2)}, u32[]{:S(2)}) collective-permute-start(bf16[144,2048]{1,0:T(8,128)(2,1)S(1)} %get-tuple-element.99), channel_id=1, source_target_pairs={{0,24},{8,16},{16,8},{24,0},{1,25},{9,17},{17,9},{25,1},{2,26},{10... | collective-permute-start | bytes 1769480 | tf_op jit(solution)/shard_map/ppermute | solution.py:34
  88.2 21.8 %collective-permute-start.15 = (bf16[32,2048]{1,0:T(8,128)(2,1)S(1)}, bf16[32,2048]{1,0:T(8,128)(2,1)S(1)}, u32[]{:S(2)}, u32[]{:S(2)}) collective-permute-start(bf16[32,2048]{1,0:T(8,128)(2,1)S(1)} %get-tuple-element.84), channel_id=1, source_target_pairs={{0,2},{2,0},{4,6},{6,4},{1,3},{3,1},{5,7},{7,5},{8,10},{10,8},{12,... | collective-permute-start | bytes 393224 | tf_op jit(solution)/shard_map/ppermute | solution.py:34
  90.1 20.0 %collective-permute-start.16 = (bf16[32,2048]{1,0:T(8,128)(2,1)S(1)}, bf16[32,2048]{1,0:T(8,128)(2,1)S(1)}, u32[]{:S(2)}, u32[]{:S(2)}) collective-permute-start(bf16[32,2048]{1,0:T(8,128)(2,1)S(1)} %get-tuple-element.85), channel_id=1, source_target_pairs={{0,4},{2,6},{4,0},{6,2},{1,5},{3,7},{5,1},{7,3},{8,12},{10,14},{12... | collective-permute-start | bytes 393224 | tf_op jit(solution)/shard_map/ppermute | solution.py:34
  91.2 18.9 %collective-permute-start.17 = (bf16[32,2048]{1,0:T(8,128)(2,1)S(1)}, bf16[32,2048]{1,0:T(8,128)(2,1)S(1)}, u32[]{:S(2)}, u32[]{:S(2)}) collective-permute-start(bf16[32,2048]{1,0:T(8,128)(2,1)S(1)} %get-tuple-element.86), channel_id=1, source_target_pairs={{0,6},{2,4},{4,2},{6,0},{1,7},{3,5},{5,3},{7,1},{8,14},{10,12},{12... | collective-permute-start | bytes 393224 | tf_op jit(solution)/shard_map/ppermute | solution.py:34
  122.1 10.1 %collective-permute-start.31 = (bf16[64,1024]{1,0:T(8,128)(2,1)S(1)}, bf16[64,1024]{1,0:T(8,128)(2,1)S(1)}, u32[]{:S(2)}, u32[]{:S(2)}) collective-permute-start(bf16[64,1024]{1,0:T(8,128)(2,1)S(1)} %get-tuple-element.103.refs_4_), channel_id=1, source_target_pairs={{0,2},{2,0},{4,6},{6,4},{1,3},{3,1},{5,7},{7,5},{8,10},{10,8},{12,... | collective-permute-start | bytes 393224 | tf_op jit(solution)/shard_map/ppermute | solution.py:34
  123.1 12.9 %collective-permute-start.32 = (bf16[64,1024]{1,0:T(8,128)(2,1)S(1)}, bf16[64,1024]{1,0:T(8,128)(2,1)S(1)}, u32[]{:S(2)}, u32[]{:S(2)}) collective-permute-start(bf16[64,1024]{1,0:T(8,128)(2,1)S(1)} %get-tuple-element.104), channel_id=1, source_target_pairs={{0,4},{2,6},{4,0},{6,2},{1,5},{3,7},{5,1},{7,3},{8,12},{10,14},{12... | collective-permute-start | bytes 393224 | tf_op jit(solution)/shard_map/ppermute | solution.py:34
  125.1 10.9 %collective-permute-start.33 = (bf16[64,1024]{1,0:T(8,128)(2,1)S(1)}, bf16[64,1024]{1,0:T(8,128)(2,1)S(1)}, u32[]{:S(2)}, u32[]{:S(2)}) collective-permute-start(bf16[64,1024]{1,0:T(8,128)(2,1)S(1)} %get-tuple-element.105), channel_id=1, source_target_pairs={{0,6},{2,4},{4,2},{6,0},{1,7},{3,5},{5,3},{7,1},{8,14},{10,12},{12... | collective-permute-start | bytes 393224 | tf_op jit(solution)/shard_map/ppermute | solution.py:34
  136.9 5.3 %collective-permute-start.34 = (bf16[64,1024]{1,0:T(8,128)(2,1)S(1)}, bf16[64,1024]{1,0:T(8,128)(2,1)S(1)}, u32[]{:S(2)}, u32[]{:S(2)}) collective-permute-start(bf16[64,1024]{1,0:T(8,128)(2,1)S(1)} %get-tuple-element.110), channel_id=1, source_target_pairs={{0,8},{8,0},{16,24},{24,16},{1,9},{9,1},{17,25},{25,17},{2,10},{10... | collective-permute-start | bytes 393224 | tf_op jit(solution)/shard_map/ppermute | solution.py:34
  138.0 5.0 %collective-permute-start.35 = (bf16[64,1024]{1,0:T(8,128)(2,1)S(1)}, bf16[64,1024]{1,0:T(8,128)(2,1)S(1)}, u32[]{:S(2)}, u32[]{:S(2)}) collective-permute-start(bf16[64,1024]{1,0:T(8,128)(2,1)S(1)} %get-tuple-element.111), channel_id=1, source_target_pairs={{0,16},{8,24},{16,0},{24,8},{1,17},{9,25},{17,1},{25,9},{2,18},{10... | collective-permute-start | bytes 393224 | tf_op jit(solution)/shard_map/ppermute | solution.py:34
  138.8 5.9 %collective-permute-start.36 = (bf16[64,1024]{1,0:T(8,128)(2,1)S(1)}, bf16[64,1024]{1,0:T(8,128)(2,1)S(1)}, u32[]{:S(2)}, u32[]{:S(2)}) collective-permute-start(bf16[64,1024]{1,0:T(8,128)(2,1)S(1)} %get-tuple-element.112), channel_id=1, source_target_pairs={{0,24},{8,16},{16,8},{24,0},{1,25},{9,17},{17,9},{25,1},{2,26},{10... | collective-permute-start | bytes 393224 | tf_op jit(solution)/shard_map/ppermute | solution.py:34
  145.5 7.4 %collective-permute-start.24 = (bf16[8,2048]{1,0:T(8,128)(2,1)S(1)}, bf16[8,2048]{1,0:T(8,128)(2,1)S(1)}, u32[]{:S(2)}, u32[]{:S(2)}) collective-permute-start(bf16[8,2048]{1,0:T(8,128)(2,1)S(1)} %get-tuple-element.90), channel_id=1, source_target_pairs={{0,8},{8,0},{16,24},{24,16},{1,9},{9,1},{17,25},{25,17},{2,10},{10... | collective-permute-start | bytes 98312 | tf_op jit(solution)/shard_map/ppermute | solution.py:34
  147.0 7.4 %collective-permute-start.25 = (bf16[8,2048]{1,0:T(8,128)(2,1)S(1)}, bf16[8,2048]{1,0:T(8,128)(2,1)S(1)}, u32[]{:S(2)}, u32[]{:S(2)}) collective-permute-start(bf16[8,2048]{1,0:T(8,128)(2,1)S(1)} %get-tuple-element.91), channel_id=1, source_target_pairs={{0,16},{8,24},{16,0},{24,8},{1,17},{9,25},{17,1},{25,9},{2,18},{10... | collective-permute-start | bytes 98312 | tf_op jit(solution)/shard_map/ppermute | solution.py:34
  147.8 6.6 %collective-permute-start.26 = (bf16[8,2048]{1,0:T(8,128)(2,1)S(1)}, bf16[8,2048]{1,0:T(8,128)(2,1)S(1)}, u32[]{:S(2)}, u32[]{:S(2)}) collective-permute-start(bf16[8,2048]{1,0:T(8,128)(2,1)S(1)} %get-tuple-element.92), channel_id=1, source_target_pairs={{0,24},{8,16},{16,8},{24,0},{1,25},{9,17},{17,9},{25,1},{2,26},{10... | collective-permute-start | bytes 98312 | tf_op jit(solution)/shard_map/ppermute | solution.py:34
  149.1 5.3 %collective-permute-start.38 = (bf16[8,2048]{1,0:T(8,128)(2,1)S(1)}, bf16[8,2048]{1,0:T(8,128)(2,1)S(1)}, u32[]{:S(2)}, u32[]{:S(2)}) collective-permute-start(bf16[8,2048]{1,0:T(8,128)(2,1)S(1)} %get-tuple-element.116), channel_id=1, source_target_pairs={{0,2},{2,0},{4,6},{6,4},{1,3},{3,1},{5,7},{7,5},{8,10},{10,8},{12,... | collective-permute-start | bytes 98312 | tf_op jit(solution)/shard_map/ppermute | solution.py:34
  151.9 5.4 %collective-permute-start.39 = (bf16[8,2048]{1,0:T(8,128)(2,1)S(1)}, bf16[8,2048]{1,0:T(8,128)(2,1)S(1)}, u32[]{:S(2)}, u32[]{:S(2)}) collective-permute-start(bf16[8,2048]{1,0:T(8,128)(2,1)S(1)} %get-tuple-element.117), channel_id=1, source_target_pairs={{0,4},{2,6},{4,0},{6,2},{1,5},{3,7},{5,1},{7,3},{8,12},{10,14},{12... | collective-permute-start | bytes 98312 | tf_op jit(solution)/shard_map/ppermute | solution.py:34
  152.9 5.7 %collective-permute-start.40 = (bf16[8,2048]{1,0:T(8,128)(2,1)S(1)}, bf16[8,2048]{1,0:T(8,128)(2,1)S(1)}, u32[]{:S(2)}, u32[]{:S(2)}) collective-permute-start(bf16[8,2048]{1,0:T(8,128)(2,1)S(1)} %get-tuple-element.118), channel_id=1, source_target_pairs={{0,6},{2,4},{4,2},{6,0},{1,7},{3,5},{5,3},{7,1},{8,14},{10,12},{12... | collective-permute-start | bytes 98312 | tf_op jit(solution)/shard_map/ppermute | solution.py:34
  (24 other events, 238.9 us)

commit v3 on v2

--- a/solution.py
+++ b/solution.py
@@ -72,153 +72,107 @@
         outs[k][:, at + 128 : at + 256] = lo[k * per : (k + 1) * per]
 
 
-def ssm_kernel(first, groups, n, per, steps, me, ss, *refs):
-    wide = 3 * steps + 1
-    if first:
-        refs = refs[1:]
-    loads = refs[: groups * wide]
-    par, decay, conv = refs[groups * wide : groups * wide + 3]
-    rest = refs[groups * wide + 3 :]
-    state, (y_out, *st_outs) = rest[:per], rest[per : per + 1 + groups]
-    arrs, meta, y_scr, tail_scr, bc_scr = rest[per + 1 + groups :]
-    group = pl.program_id(0)
+def ssm_kernel(groups, per, steps, me, ss, *refs):
+    loads = refs[:groups]
+    par, decay, conv, state, y_out = refs[groups : groups + 5]
+    st_outs = refs[groups + 5 : 2 * groups + 5]
+    y_scr, tail_scr, bc_scr, du_scr = refs[2 * groups + 5 :]
+    taps, _, ch = conv.shape
+    states = decay.shape[0]
+    cb = y_scr.shape[2]
+    lb = min(256, cb)
+    low = st_outs[0].shape[0] - per * states
+    at = 3 * steps * ch
+    masks = []
     for q in range(groups):
-
-        @pl.when(group == q)
-        def _():
-            for a in range(3 * steps):
-                arrs[a] = loads[q * wide + a][...]
-            meta[...] = loads[q * wide + wide - 1][...]
-
-    taps = conv.shape[0]
-    states, cb = decay.shape
-    val = meta[:, :128].astype(F32) + meta[:, 128:].astype(F32)
-    bc_scr[...] = jnp.transpose(jnp.concatenate([val, jnp.zeros((128 - per, 128), F32)], axis=0))
-    src = me[0] ^ (group + first)
-    for j in range(taps):
-        for i in range(per):
-            tail_scr[j, i : i + 1, :] = conv[j, pl.ds(ss[me[0], src, i], 1), :]
-    prefix = val[:, PREFIX : PREFIX + 1]
-    window = [
-        tail_scr[j] * (prefix >= float(taps - j)).astype(F32) for j in range(taps)
-    ]
-    deltas, us, skips, gates = [], [], [], []
-    for t in range(steps):
-        window.append(arrs[t].astype(F32))
-        acc = window[t] * par[0:1, :]
-        for j in range(1, taps + 1):
-            acc = acc + window[t + j] * par[j : j + 1, :]
-        acc = acc + par[taps + 1 : taps + 2, :]
-        xc = acc * jax.nn.sigmoid(acc)
-        raw = arrs[2 * steps + t].astype(F32) + par[taps + 2 : taps + 3, :]
-        delta = jnp.maximum(raw, 0.0) + jnp.log1p(jnp.exp(-jnp.abs(raw)))
-        zt = arrs[steps + t].astype(F32)
-        deltas.append(-delta)
-        us.append(delta * xc)
-        skips.append(par[taps + 3 : taps + 4, :] * xc)
-        gates.append(zt * jax.nn.sigmoid(zt))
-    dec = decay[...]
-    low = st_outs[0].shape[0] - per * states
-    kept = window[steps:taps]
-    kept.append(jnp.zeros((low - per * len(kept), cb), F32))
-    kept = jnp.concatenate(kept, axis=0)
-    ends = []
-    for i in range(per):
-        st = state[i][0]
-        for t in range(steps):
-            at = 2 * t * states
-            bcol = bc_scr[at : at + states, i : i + 1]
-            ccol = bc_scr[at + states : at + 2 * states, i : i + 1]
-            st = jnp.exp(deltas[t][i : i + 1] * dec) * st + us[t][i : i + 1] * bcol
-            y_scr[t, i : i + 1, :] = jnp.sum(ccol * st, axis=0, keepdims=True)
+        val = loads[q][:, at : at + 128].astype(F32) + loads[q][:, at + 128 : at + 256].astype(F32)
+        full = jnp.concatenate([val, jnp.zeros((128 - per, 128), F32)], axis=0)
+        bc_scr[q] = jnp.transpose(full)
+        prefix = val[:, PREFIX : PREFIX + 1]
+        masks.append([(prefix >= float(taps - j)).astype(F32) for j in range(taps)])
+
+    @pl.loop(0, ch // cb)
+    def _(g):
+        base = pl.multiple_of(g * cb, cb)
+        wide = pl.ds(base, cb)
         for q in range(groups):
-
-            @pl.when(group == q)
-            def _():
-                st_outs[q][i * states : (i + 1) * states, :] = st.astype(st_outs[q].dtype)
-
-    for q in range(groups):
-
-        @pl.when(group == q)
-        def _():
-            st_outs[q][per * states :, :] = kept.astype(st_outs[q].dtype)
-
-    for t in range(steps):
-        out = (y_scr[t] + skips[t]) * gates[t]
-        y_out[0, t * per : (t + 1) * per, :] = out.astype(BF)
-
-
-def ssm(first, n, per, steps, me, ss, payloads, par, decay, conv, state, y_buf):
+            slots = [ss[me[0], me[0] ^ q, i] for i in range(per)]
+
+            def load(a):
+                return loads[q][:, pl.ds(pl.multiple_of(a * ch + base, cb), cb)].astype(F32)
+
+            for j in range(taps):
+                for i in range(per):
+                    tail_scr[j, i : i + 1, :] = conv[j, pl.ds(slots[i], 1), wide]
+            window = [tail_scr[j] * masks[q][j] for j in range(taps)]
+            skips, gates = [], []
+            for t in range(steps):
+                window.append(load(t))
+                acc = window[t] * par[0:1, wide]
+                for j in range(1, taps + 1):
+                    acc = acc + window[t + j] * par[j : j + 1, wide]
+                acc = acc + par[taps + 1 : taps + 2, wide]
+                xc = acc * jax.nn.sigmoid(acc)
+                raw = load(2 * steps + t) + par[taps + 2 : taps + 3, wide]
+                delta = jnp.maximum(raw, 0.0) + jnp.log1p(jnp.exp(-jnp.abs(raw)))
+                zt = load(steps + t)
+                du_scr[2 * t] = delta * -1.4426950408889634
+                du_scr[2 * t + 1] = delta * xc
+                skips.append(par[taps + 3 : taps + 4, wide] * xc)
+                gates.append(zt * jax.nn.sigmoid(zt))
+            kept = window[steps:taps]
+            kept.append(jnp.zeros((low - per * len(kept), cb), F32))
+            kept = jnp.concatenate(kept, axis=0)
+            st_outs[q][per * states :, wide] = kept.astype(st_outs[q].dtype)
+            for i in range(per):
+                cols = []
+                for k in range(2 * steps):
+                    col = bc_scr[q, k * states : (k + 1) * states, i : i + 1]
+                    cols.append(jnp.broadcast_to(col, (states, lb)))
+                for l in range(cb // lb):
+                    here = slice(l * lb, (l + 1) * lb)
+                    there = pl.ds(pl.multiple_of(base + l * lb, lb), lb)
+                    st = state[slots[i], :, there]
+                    for t in range(steps):
+                        dl = du_scr[2 * t, i : i + 1, here]
+                        ul = du_scr[2 * t + 1, i : i + 1, here]
+                        st = jnp.exp2(dl * decay[:, there]) * st + ul * cols[2 * t]
+                        y_scr[t, i : i + 1, here] = jnp.sum(
+                            cols[2 * t + 1] * st, axis=0, keepdims=True
+                        )
+                    st_outs[q][i * states : (i + 1) * states, there] = st.astype(st_outs[q].dtype)
+            for t in range(steps):
+                row = (q * steps + t) * per
+                y_out[row : row + per, wide] = ((y_scr[t] + skips[t]) * gates[t]).astype(BF)
+
+
+def ssm(per, steps, me, ss, payloads, par, decay, conv, state):
     groups = len(payloads)
     states, ch = decay.shape
-    blocks = 2
-    cb = ch // blocks
+    cb = ch // 4
     taps = conv.shape[0]
     low = -(-(taps - steps) * per // 16) * 16
-
-    def held(q, gk, g):
-        return jnp.where(gk < q, 0, jnp.where(gk > q, blocks - 1, g))
-
-    specs, args = [], []
-    for q in range(groups):
-        for a in range(3 * steps):
-            specs.append(
-                pl.BlockSpec(
-                    (per, cb),
-                    functools.partial(
-                        lambda q, a, gk, g, *_: (0, a * blocks + held(q, gk, g)), q, a
-                    ),
-                )
-            )
-        specs.append(pl.BlockSpec((per, META), lambda gk, g, *_: (0, 3 * steps * ch // META)))
-        args += [payloads[q]] * (3 * steps + 1)
-    specs.append(pl.BlockSpec((par.shape[0], cb), lambda gk, g, *_: (0, g)))
-    specs.append(pl.BlockSpec((states, cb), lambda gk, g, *_: (0, g)))
-    specs.append(pl.BlockSpec((taps, conv.shape[1], cb), lambda gk, g, *_: (0, 0, g)))
-    for i in range(per):
-        specs.append(
-            pl.BlockSpec(
-                (1, states, cb),
-                functools.partial(
-                    lambda i, gk, g, m, s: (s[m[0], m[0] ^ (gk + first), i], 0, g), i
-                ),
-            )
-        )
-    args += [par, decay, conv] + [state] * per
-    alias = {}
-    if first:
-        specs = [pl.BlockSpec(memory_space=pl.ANY)] + specs
-        args = [y_buf] + args
-        alias = {2: 0}
-    st_type = BF if first else F32
+    vm = pl.BlockSpec(memory_space=pltpu.VMEM)
+    sm = pl.BlockSpec(memory_space=pltpu.SMEM)
+    args = list(payloads) + [par, decay, conv, state]
     return pl.pallas_call(
-        functools.partial(ssm_kernel, first, groups, n, per, steps),
-        grid_spec=pltpu.PrefetchScalarGridSpec(
-            num_scalar_prefetch=2,
-            grid=(groups, blocks),
-            in_specs=specs,
-            out_specs=[pl.BlockSpec((1, steps * per, cb), lambda gk, g, *_: (gk + first, 0, g))]
-            + [
-                pl.BlockSpec(
-                    (per * states + low, cb),
-                    functools.partial(lambda q, gk, g, *_: (0, held(q, gk, g)), q),
-                )
-                for q in range(groups)
-            ],
-            scratch_shapes=[
-                pltpu.VMEM((3 * steps, per, cb), BF),
-                pltpu.VMEM((per, META), BF),
-                pltpu.VMEM((steps, per, cb), F32),
-                pltpu.VMEM((taps, per, cb), F32),
-                pltpu.VMEM((128, 128), F32),
-            ],
-        ),
-        out_shape=[jax.ShapeDtypeStruct((n, steps * per, ch), BF)]
-        + [jax.ShapeDtypeStruct((per * states + low, ch), st_type)] * groups,
-        input_output_aliases=alias,
-        compiler_params=params(16),
+        functools.partial(ssm_kernel, groups, per, steps),
+        in_specs=[sm, sm] + [vm] * len(args),
+        out_specs=[vm] * (1 + groups),
+        out_shape=[jax.ShapeDtypeStruct((groups * steps * per, ch), BF)]
+        + [
+            jax.ShapeDtypeStruct((per * states + low, ch), BF if q else F32)
+            for q in range(groups)
+        ],
+        scratch_shapes=[
+            pltpu.VMEM((steps, per, cb), F32),
+            pltpu.VMEM((taps, per, cb), F32),
+            pltpu.VMEM((groups, 128, 128), F32),
+            pltpu.VMEM((2 * steps, per, cb), F32),
+        ],
+        compiler_params=params(4),
         cost_estimate=cost(3e6 * groups, groups * 3 << 20),
-        name=f"ssm{first}",
+        name="ssm",
     )(me, ss, *args)
 
 
@@ -284,37 +238,44 @@
 
 def project_kernel(n, *refs):
     ys = refs[:n]
-    sel, w = refs[n : n + 2]
-    keep, send, y_all, y_sel = refs[-4:]
+    sel_slot, sel_own, w = refs[n : n + 3]
+    *outs, y_all, y_sel = refs[-6:]
     size = ys[0].shape[0]
     for q in range(n):
         y_all[q * size : (q + 1) * size, :] = ys[q][...]
-    y_sel[...] = jnp.dot(sel[...], y_all[...], preferred_element_type=F32).astype(BF)
-    half = keep.shape[0]
+    at = 0
+    for sel in (sel_slot, sel_own):
+        got = jnp.dot(sel[...], y_all[...], preferred_element_type=F32).astype(BF)
+        y_sel[at : at + got.shape[0], :] = got
+        at += got.shape[0]
     wb = min(512, w.shape[1])
 
     @pl.loop(0, w.shape[1] // wb)
     def _(g):
         at = pl.ds(pl.multiple_of(g * wb, wb), wb)
         out = jnp.dot(y_sel[...], w[:, at], preferred_element_type=F32).astype(BF)
-        keep[:, at] = out[:half]
-        send[:, at] = out[half:]
-
-
-def project(n, ys, sel, w, name, dep):
+        row = 0
+        for part in outs:
+            part[:, at] = out[row : row + part.shape[0]]
+            row += part.shape[0]
+
+
+def project(n, ys, sel_slot, sel_own, w, dep):
     vm = pl.BlockSpec(memory_space=pltpu.VMEM)
-    count, total = sel.shape
+    slot, total = sel_slot.shape
+    own = sel_own.shape[0]
     ch, wc = w.shape
     return pl.pallas_call(
         functools.partial(project_kernel, n),
-        in_specs=[vm] * (n + 2) + [pl.BlockSpec(memory_space=pl.ANY)],
-        out_specs=[vm] * 2,
-        out_shape=[jax.ShapeDtypeStruct((count // 2, wc), BF)] * 2,
-        scratch_shapes=[pltpu.VMEM((total, ch), BF), pltpu.VMEM((count, ch), BF)],
-        compiler_params=params(8),
-        cost_estimate=cost(2 * count * ch * wc, 2 * ch * wc),
-        name=name,
-    )(*ys, sel, w, dep)
+        in_specs=[vm] * (n + 3) + [pl.BlockSpec(memory_space=pl.ANY)],
+        out_specs=[vm] * 4,
+        out_shape=[jax.ShapeDtypeStruct((slot // 2, wc), BF)] * 2
+        + [jax.ShapeDtypeStruct((own // 2, wc), BF)] * 2,
+        scratch_shapes=[pltpu.VMEM((total, ch), BF), pltpu.VMEM((slot + own, ch), BF)],
+        compiler_params=params(10),
+        cost_estimate=cost(1e5, 1 << 12),
+        name="project",
+    )(*ys, sel_slot, sel_own, w, dep)
 
 
 def load_kernel(chunks, w, *refs):
@@ -333,6 +294,15 @@
         copy.wait()
 
 
+def fetch_kernel(count, *refs):
+    srcs, outs, sem = refs[:count], refs[-count - 1 : -1], refs[-1]
+    copies = [pltpu.make_async_copy(srcs[q], outs[q], sem.at[q]) for q in range(count)]
+    for copy in copies:
+        copy.start()
+    for copy in copies:
+        copy.wait()
+
+
 def gate_kernel(m, me, *refs):
     pieces = 2 * m
     xs = refs[:pieces]
@@ -376,11 +346,13 @@
 def down_kernel(m, deps, me, act, dw, *refs):
     send, keep, dbuf, dsem = refs[deps:]
     pc, deep = dbuf.shape[2], dbuf.shape[0]
-    nd = 2 * m
+    nh = send.shape[1] // pc
+    cut = nh // m
+    nd = 2 * nh
 
     def down_copy(i):
-        h = jnp.where(i < m, 1, 0)
-        block = (me[2] ^ h) * m + (me[1] ^ lax.rem(i, m))
+        h, j = jnp.where(i < nh, 1, 0), lax.rem(i, nh)
+        block = ((me[2] ^ h) * m + (me[1] ^ lax.div(j, cut))) * cut + lax.rem(j, cut)
         return pltpu.make_async_copy(
             dw.at[:, pl.ds(pl.multiple_of(block * pc, pc), pc)],
             dbuf.at[lax.rem(i, deep)],
@@ -394,13 +366,13 @@
     def _(i):
         down_copy(i).wait()
         out = jnp.dot(act[...], dbuf[lax.rem(i, deep)], preferred_element_type=F32).astype(BF)
-        at = pl.ds(pl.multiple_of(lax.rem(i, m) * pc, pc), pc)
-
-        @pl.when(i < m)
+        at = pl.ds(pl.multiple_of(lax.rem(i, nh) * pc, pc), pc)
+
+        @pl.when(i < nh)
         def _():
             send[:, at] = out
 
-        @pl.when(i >= m)
+        @pl.when(i >= nh)
         def _():
             keep[:, at] = out
 
@@ -507,7 +479,7 @@
         out_shape=[jax.ShapeDtypeStruct(*o) for o in outs],
         scratch_shapes=list(scr),
         compiler_params=params(8),
-        cost_estimate=cost(1e6, 1 << 20),
+        cost_estimate=cost(1e5, 1 << 12),
         name=name,
     )(*args, *deps)
 
@@ -565,7 +537,7 @@
             jax.ShapeDtypeStruct((8, 128), F32),
         ],
         compiler_params=params(8),
-        cost_estimate=cost(1e5, 8 << 20),
+        cost_estimate=cost(1e5, 1 << 12),
         name="place",
     )(me, rr, *srcs, dep)
 
@@ -676,11 +648,19 @@
         [conv_weight, conv_bias[None], dt_bias[None], skip_gain[None], jnp.zeros((1, ch), F32)], 0
     )
     conv = jnp.transpose(conv_cache, (1, 0, 2))
-    fixed = (par, decay_rate, conv, in_hbm(state_cache))
-    y_buf, own_kept = ssm(0, n, per, steps, me, ss, payload[:1], *fixed, None)
-    y_buf, *kept = ssm(1, n, per, steps, me, ss, payload[1:], *fixed, y_buf)
-    kept = [own_kept] + kept
-    y_own = y_buf.reshape(n * steps * per, ch)
+    fixed = (par, decay_rate, conv, state_cache)
+    hbm = pl.BlockSpec(memory_space=pltpu.HBM)
+    fixed = pl.pallas_call(
+        functools.partial(fetch_kernel, len(fixed)),
+        in_specs=[hbm] * len(fixed) + [pl.BlockSpec(memory_space=pl.ANY)],
+        out_specs=[vm] * len(fixed),
+        out_shape=[pltpu.VMEM(a.shape, a.dtype) for a in fixed],
+        scratch_shapes=[pltpu.SemaphoreType.DMA((len(fixed),))],
+        compiler_params=params(1),
+        cost_estimate=cost(1e5, 1 << 12),
+        name="fetch",
+    )(*[in_hbm(a) for a in fixed], payload[0])
+    y_own, *kept = ssm(per, steps, me, ss, payload, *fixed)
     ys = [y_own] + [trade(y_own, "dp", n, k) for k in range(1, n)]
 
     n_slot, n_own = 2 * m * n * pe, 2 * m * n * rm
@@ -719,7 +699,7 @@
         out_shape=[pltpu.VMEM(gate_weight.shape, BF), jax.ShapeDtypeStruct((8, 128), F32)],
         scratch_shapes=[pltpu.SemaphoreType.DMA((chunks,))],
         compiler_params=params(1),
-        cost_estimate=cost(0, 4 * gate_weight.size),
+        cost_estimate=cost(1e5, 1 << 12),
         name="load",
     )(in_hbm(gate_weight), y_own)
     anyspace = pl.BlockSpec(memory_space=pl.ANY)
@@ -735,14 +715,15 @@
 
     def add_z(got, each, name, dep=()):
         outs = [((each, wc), BF)] * n
-        out = small(functools.partial(sum_rows_kernel, m, n), name, outs, got, dep)
+        out = small(functools.partial(sum_rows_kernel, len(got), n), name, outs, got, dep)
         return [out[0]] + [trade(out[k], "dp", n, k) for k in range(1, n)]
 
-    keep_slot, send_slot_rows = project(n, ys, sel_slot, out_weight, "project_slot", loaded)
+    keep_slot, send_slot_rows, keep_own, send_own = project(
+        n, ys, sel_slot, sel_own, out_weight, loaded
+    )
     parts = add_core(keep_slot, send_slot_rows, pe, "core_slot")
     slot_z = send_z(parts)
-    keep_own, send_own = project(n, ys, sel_own, out_weight, "project_own", slot_z[1])
-    hid = add_z(slot_z, pe, "z_slot", (keep_own,))
+    hid = add_z(slot_z, pe, "z_slot")
     [normed] = small(
         functools.partial(norm_kernel, n),
         "norm",
@@ -753,7 +734,15 @@
     xs = []
     for piece in near:
         xs += [piece, trade(piece, "core", 2, 1)]
-    own_parts = add_core(keep_own, send_own, rm, "core_own", (near[1],))
+    size = m * n * rm // 2
+    halves = [((size, wc), F32), ((size, wc), BF)]
+    own_keep, own_send = small(
+        functools.partial(pair_rows_kernel, 2),
+        "core_own",
+        halves,
+        (keep_own, trade(send_own, "core", 2, 1)),
+        (near[1],),
+    )
     held = pl.pallas_call(
         hold_kernel,
         in_specs=[anyspace] * n,
@@ -762,7 +751,7 @@
         input_output_aliases={k: k for k in range(n - 1)},
         compiler_params=params(1),
         name="hold",
-    )(*kept[1:], normed)
+    )(*kept[1:], near[1])
     back = [kept[0]] + [trade(held[k - 1], "dp", n, k) for k in range(1, n)]
 
     half = dm // 2
@@ -782,15 +771,24 @@
         cost_estimate=cost(4 * cap * dm * width, 4 * dm * width),
         name="gate",
     )(me, *xs, share, gate_here, in_hbm(up_weight))
-    own_z = send_z(own_parts)
-    own = add_z(own_z, rm, "z_own", (act,))
-    deps = own_z[1:] + back[1:]
+    k = m // 2
+    while k > 1:
+        size //= 2
+        own_keep, own_send = small(
+            functools.partial(pair_rows_kernel, 2),
+            f"half{k}",
+            [((size, wc), F32), ((size, wc), BF)],
+            (own_keep, trade(own_send, "z", m, k)),
+        )
+        k //= 2
+    own_z = [own_keep, trade(own_send, "z", m, 1)]
+    deps = [own_send] + back[1:]
     send, keep = pl.pallas_call(
         functools.partial(down_kernel, m, len(deps)),
         in_specs=[sm, vm, pl.BlockSpec(memory_space=pltpu.HBM)] + [anyspace] * len(deps),
         out_specs=[vm] * 2,
         out_shape=[jax.ShapeDtypeStruct((cap, half), BF)] * 2,
-        scratch_shapes=[pltpu.VMEM((3, width, pc), BF), pltpu.SemaphoreType.DMA((3,))],
+        scratch_shapes=[pltpu.VMEM((6, width, pc // 2), BF), pltpu.SemaphoreType.DMA((6,))],
         compiler_params=params(14),
         cost_estimate=cost(2 * cap * dm * width, 2 * dm * width),
         name="down",
@@ -801,7 +799,18 @@
     cols = small(functools.partial(pair_cols_kernel, m), "core_out", outs, (keep, got))
     moved = [cols[0]] + [trade(cols[k], "z", m, k) for k in range(1, m)]
 
-    new_state, placed = place(n, per, rows, states, me, rr, back, cols[1])
+    own = add_z(own_z, rm, "z_own", (cols[1],))
+    share_rows = total // n
+    outs = [((share_rows, pc), F32)] + [((share_rows, pc), BF)] * (n - 1)
+    rows_out = small(
+        functools.partial(spread_kernel, n, m),
+        "spread",
+        outs,
+        (me, expand, *moved),
+        tuple(own[1:]),
+        [pltpu.VMEM((total, pc), F32)],
+    )
+    new_state, placed = place(n, per, rows, states, me, rr, back, rows_out[1])
     low = kept[0].shape[0] - per * states
     tail_at = per * states // low
     new_tail, placed = pl.pallas_call(
@@ -818,28 +827,18 @@
             jax.ShapeDtypeStruct((taps, rows, ch), F32),
             jax.ShapeDtypeStruct((8, 128), F32),
         ],
-        compiler_params=params(16),
-        cost_estimate=cost(1e5, 1 << 20),
+        compiler_params=params(8),
+        cost_estimate=cost(1e5, 1 << 12),
         name="tail",
     )(me, rr, x_input, *back, placed)
 
-    share_rows = total // n
-    outs = [((share_rows, pc), F32)] + [((share_rows, pc), BF)] * (n - 1)
-    rows_out = small(
-        functools.partial(spread_kernel, n, m),
-        "spread",
-        outs,
-        (me, expand, *moved),
-        (placed,),
-        [pltpu.VMEM((total, pc), F32)],
-    )
     mine = [rows_out[0]] + [trade(rows_out[k], "dp", n, k) for k in range(1, n)]
     deal_keep, deal_send = small(
         functools.partial(deal_kernel, n, m),
         "deal",
         [((m * rm, pc), BF)] * 2,
         (me, *mine),
-        (),
+        (placed,),
         [pltpu.VMEM((share_rows, pc), F32)],
     )
     pieces = small(

time: 160 us -> 148 us (0.925)
  Pallas kernels: 68.4 us -> 61 us
  starting transfers between devices: 48.1 us -> 44.6 us
    pallas_call x2, Pallas kernels: 13.8 us -> 7.65 us  [the longest x1 5.07 us: ssm(): pl.pallas_call(functools.partial(ssm_kernel, groups, per, steps), in_spec...]
    ppermute x41 -> x40, starting transfers between devices: 48.1 us -> 44.6 us  [trade(): return lax.ppermute(piece, axis, [(i, i ^ k) for i in range(size)])]
    unnamed x30 -> x24, local copies, waits for them, and re-layouts: 3.48 us -> 1.44 us
    pallas_call x2 -> x1, Pallas kernels: 6.69 us -> 5.81 us  [project(): pl.pallas_call(functools.partial(project_kernel, n), in_specs=[vm] * (n +...]
    ppermute x41 -> x40, waiting for transfers between devices: 38 us -> 37.9 us  [trade(): return lax.ppermute(piece, axis, [(i, i ^ k) for i in range(size)])]
    pallas_call x10 -> x11, Pallas kernels: 3.99 us -> 3.99 us  [small(): pl.pallas_call(run, in_specs=specs + [pl.BlockSpec(memory_space=pl.ANY)]...]
  transfers between devices with their start and end apart: 41 -> 40, of which waited for: 19 -> 21; matrix products, arithmetic and copies ran while one was open for 1% -> 1% of each run, Pallas kernels for 25% -> 24%
where the time goes in v3:
time: 148 us; the launch traced here: 147 us
  Pallas kernels  61 us (41%)
  starting transfers between devices  44.6 us (30%)
  waiting for transfers between devices  37.9 us (26%)
  local copies, waits for them, and re-layouts  2.91 us (2%)
    ppermute x40, starting transfers between devices, trade(): return lax.ppermute(piece, axis, [(i, i ^ k) for i in range(size)])  44.6 us
    ppermute x40, waiting for transfers between devices, trade(): return lax.ppermute(piece, axis, [(i, i ^ k) for i in range(size)])  37.9 us
    pallas_call x1, Pallas kernels, body(): pl.pallas_call(functools.partial(gate_kernel, m), in_specs=[sm] + [vm] *...  17.3 us
    pallas_call x1, Pallas kernels, body(): pl.pallas_call(functools.partial(down_kernel, m, len(deps)), in_specs=[sm...  9.61 us
    pallas_call x1, Pallas kernels, body(): pl.pallas_call(functools.partial(load_kernel, chunks), in_specs=[pl.Block...  8.33 us
    pallas_call x1, Pallas kernels, project(): pl.pallas_call(functools.partial(project_kernel, n), in_specs=[vm] * (n +...  5.81 us
    pallas_call x1, Pallas kernels, ssm(): pl.pallas_call(functools.partial(ssm_kernel, groups, per, steps), in_spec...  5.07 us
    pallas_call x1, Pallas kernels, place(): pl.pallas_call(functools.partial(place_kernel, n, states), grid_spec=pltp...  4.1 us
  transfers between devices with their start and end apart: 40, of which 21 were waited for; matrix products, arithmetic and copies ran while one was open for 1% of the time, Pallas kernels for 24%

profile of v3, /device:TPU:0, one launch (start us, length us, event | category | flops | bytes accessed | tf_op | source)
XLA Modules:
  0.0 147.5 jit_solution(8236247329894160062)
XLA Ops:
  1.4 1.6 %pack.1 = (bf16[8,12544]{1,0:T(8,128)(2,1)S(1)}, bf16[8,12544]{1,0:T(8,128)(2,1)S(1)}, bf16[8,12544]{1,0:T(8,128)(2,1)S(1)}, bf16[8,12544]{1,0:T(8,128)(2,1)S(1)}) custom-call(s32[3]{0:T(128)S(1)} %pad_add_fusion.me.refs_0_, s32[1,4,8]{2,1,0:T(4,128)S(1)} %copy-done.4, bf16[2,32,2048]{2,1,0:T(8,128)(2,1)} %x.3, bf16[2,32,2048]{2,1,0:T(8,128)(2,1)} %z.1, ...), custom_call_target="tpu_custom_call" | custom-call | flops 1000000 | bytes 2097152 | tf_op jit(solution)/shard_map/pack/pallas_call | solution.py:635
  3.0 3.0 %collective-permute-start = (bf16[8,12544]{1,0:T(8,128)(2,1)S(1)}, bf16[8,12544]{1,0:T(8,128)(2,1)S(1)}, u32[]{:S(2)}, u32[]{:S(2)}) collective-permute-start(bf16[8,12544]{1,0:T(8,128)(2,1)S(1)} %get-tuple-element.66), channel_id=1, source_target_pairs={{0,8},{8,0},{16,24},{24,16},{1,9},{9,1},{17,25},{25,17},{2,10},{10... | collective-permute-start | bytes 602120 | tf_op jit(solution)/shard_map/ppermute | solution.py:34
  6.0 1.5 %collective-permute-start.1 = (bf16[8,12544]{1,0:T(8,128)(2,1)S(1)}, bf16[8,12544]{1,0:T(8,128)(2,1)S(1)}, u32[]{:S(2)}, u32[]{:S(2)}) collective-permute-start(bf16[8,12544]{1,0:T(8,128)(2,1)S(1)} %get-tuple-element.67), channel_id=1, source_target_pairs={{0,16},{8,24},{16,0},{24,8},{1,17},{9,25},{17,1},{25,9},{2,18},{10... | collective-permute-start | bytes 602120 | tf_op jit(solution)/shard_map/ppermute | solution.py:34
  7.5 1.5 concatenate.3.refs_0_
  9.0 2.6 %fetch.1 = (f32[8,2048]{1,0:T(8,128)S(1)}, f32[16,2048]{1,0:T(8,128)S(1)}, f32[3,32,2048]{2,1,0:T(8,128)S(1)}, f32[32,16,2048]{2,1,0:T(8,128)S(1)}) custom-call(f32[8,2048]{1,0:T(8,128)} %concatenate.3.refs_0_, f32[16,2048]{1,0:T(8,128)} %refs_1_.1, f32[3,32,2048]{2,1,0:T(8,128)} %bitcast.23, f32[32,16,2048]{2,1,0:T(8,128)} %refs_3_.1, ...), custom_call_target="tpu_custom_call" | custom-call | flops 100000 | bytes 4096 | tf_op jit(solution)/shard_map/fetch/pallas_call | solution.py:653
  11.8 4.9 %collective-permute-done.1.refs_2_ = bf16[8,12544]{1,0:T(8,128)(2,1)S(1)} collective-permute-done((bf16[8,12544]{1,0:T(8,128)(2,1)S(1)}, bf16[8,12544]{1,0:T(8,128)(2,1)S(1)}, u32[]{:S(2)}, u32[]{:S(2)}) %collective-permute-start.1) | collective-permute-done | bytes 200736 | tf_op jit(solution)/shard_map/ppermute | solution.py:34
  17.5 5.1 %ssm.1 = (bf16[64,2048]{1,0:T(8,128)(2,1)S(1)}, f32[144,2048]{1,0:T(8,128)S(1)}, bf16[144,2048]{1,0:T(8,128)(2,1)S(1)}, bf16[144,2048]{1,0:T(8,128)(2,1)S(1)}, bf16[144,2048]{1,0:T(8,128)(2,1)S(1)}) custom-call(s32[3]{0:T(128)S(1)} %pad_add_fusion.me.refs_0_, s32[4,4,8]{2,1,0:T(4,128)S(1)} %copy-done.6, ...), custom_call_target="tpu_custom_call" | custom-call | flops 12000000 | bytes 12582912 | tf_op jit(solution)/shard_map/ssm/pallas_call | solution.py:158
  24.7 1.5 collective-permute-start.5
  26.2 8.3 %load.1 = (bf16[8192,1536]{1,0:T(8,128)(2,1)S(1)}, f32[8,128]{1,0:T(8,128)S(1)}) custom-call(bf16[8192,1536]{1,0:T(8,128)(2,1)} %w.1, bf16[64,2048]{1,0:T(8,128)(2,1)S(1)} %get-tuple-element.73.refs_0_), custom_call_target="tpu_custom_call" | custom-call | flops 100000 | bytes 4096 | tf_op jit(solution)/shard_map/load/pallas_call | solution.py:695
  36.4 5.8 %project.1 = (bf16[128,2048]{1,0:T(8,128)(2,1)S(1)}, bf16[128,2048]{1,0:T(8,128)(2,1)S(1)}, bf16[128,2048]{1,0:T(8,128)(2,1)S(1)}, bf16[128,2048]{1,0:T(8,128)(2,1)S(1)}) custom-call(bf16[64,2048]{1,0:T(8,128)(2,1)S(1)} %get-tuple-element.73.refs_0_, bf16[64,2048]{1,0:T(8,128)(2,1)S(1)} %collective-permute-done.3.refs_1_, ...), custom_call_target="tpu_custom_call" | custom-call | flops 100000 | bytes 4096 | tf_op jit(solution)/shard_map/project/pallas_call | solution.py:268
  42.8 1.4 collective-permute-done.7.refs_1_
  44.3 3.7 %collective-permute-start.10 = (bf16[32,2048]{1,0:T(8,128)(2,1)S(1)}, bf16[32,2048]{1,0:T(8,128)(2,1)S(1)}, u32[]{:S(2)}, u32[]{:S(2)}) collective-permute-start(bf16[32,2048]{1,0:T(8,128)(2,1)S(1)} %get-tuple-element.84), channel_id=1, source_target_pairs={{0,6},{2,4},{4,2},{6,0},{1,7},{3,5},{5,3},{7,1},{8,14},{10,12},{12... | collective-permute-start | bytes 393224 | tf_op jit(solution)/shard_map/ppermute | solution.py:34
  48.8 3.8 %collective-permute-done.10.refs_3_ = bf16[32,2048]{1,0:T(8,128)(2,1)S(1)} collective-permute-done((bf16[32,2048]{1,0:T(8,128)(2,1)S(1)}, bf16[32,2048]{1,0:T(8,128)(2,1)S(1)}, u32[]{:S(2)}, u32[]{:S(2)}) %collective-permute-start.10) | collective-permute-done | bytes 131104 | tf_op jit(solution)/shard_map/ppermute | solution.py:34
  52.6 3.1 %collective-permute-done.8.refs_1_ = bf16[32,2048]{1,0:T(8,128)(2,1)S(1)} collective-permute-done((bf16[32,2048]{1,0:T(8,128)(2,1)S(1)}, bf16[32,2048]{1,0:T(8,128)(2,1)S(1)}, u32[]{:S(2)}, u32[]{:S(2)}) %collective-permute-start.8) | collective-permute-done | bytes 131104 | tf_op jit(solution)/shard_map/ppermute | solution.py:34
  55.7 3.7 %collective-permute-done.9.refs_2_ = bf16[32,2048]{1,0:T(8,128)(2,1)S(1)} collective-permute-done((bf16[32,2048]{1,0:T(8,128)(2,1)S(1)}, bf16[32,2048]{1,0:T(8,128)(2,1)S(1)}, u32[]{:S(2)}, u32[]{:S(2)}) %collective-permute-start.9) | collective-permute-done | bytes 131104 | tf_op jit(solution)/shard_map/ppermute | solution.py:34
  61.3 1.7 %collective-permute-start.13 = (bf16[8,2048]{1,0:T(8,128)(2,1)S(1)}, bf16[8,2048]{1,0:T(8,128)(2,1)S(1)}, u32[]{:S(2)}, u32[]{:S(2)}) collective-permute-start(bf16[8,2048]{1,0:T(8,128)(2,1)S(1)} %get-tuple-element.88), channel_id=1, source_target_pairs={{0,24},{8,16},{16,8},{24,0},{1,25},{9,17},{17,9},{25,1},{2,26},{10... | collective-permute-start | bytes 98312 | tf_op jit(solution)/shard_map/ppermute | solution.py:34
  64.3 1.8 %collective-permute-done.13.refs_5_ = bf16[8,2048]{1,0:T(8,128)(2,1)S(1)} collective-permute-done((bf16[8,2048]{1,0:T(8,128)(2,1)S(1)}, bf16[8,2048]{1,0:T(8,128)(2,1)S(1)}, u32[]{:S(2)}, u32[]{:S(2)}) %collective-permute-start.13) | collective-permute-done | bytes 32800 | tf_op jit(solution)/shard_map/ppermute | solution.py:34
  66.9 3.0 %collective-permute-start.19 = (bf16[8,8192]{1,0:T(8,128)(2,1)S(1)}, bf16[8,8192]{1,0:T(8,128)(2,1)S(1)}, u32[]{:S(2)}, u32[]{:S(2)}) collective-permute-start(bf16[8,8192]{1,0:T(8,128)(2,1)S(1)} %norm.1.refs_0_), channel_id=1, source_target_pairs={{0,4},{2,6},{4,0},{6,2},{1,5},{3,7},{5,1},{7,3},{8,12},{10,14},{12... | collective-permute-start | bytes 393224 | tf_op jit(solution)/shard_map/ppermute | solution.py:34
  71.3 2.8 %collective-permute-done.14.refs_2_.refs_3_ = bf16[8,8192]{1,0:T(8,128)(2,1)S(1)} collective-permute-done((bf16[8,8192]{1,0:T(8,128)(2,1)S(1)}, bf16[8,8192]{1,0:T(8,128)(2,1)S(1)}, u32[]{:S(2)}, u32[]{:S(2)}) %collective-permute-start.14) | collective-permute-done | bytes 131104 | tf_op jit(solution)/shard_map/ppermute | solution.py:34
  82.2 17.3 %gate.1.act = bf16[64,1536]{1,0:T(8,128)(2,1)S(1)} custom-call(s32[3]{0:T(128)S(1)} %pad_add_fusion.me.refs_0_, bf16[8,8192]{1,0:T(8,128)(2,1)S(1)} %norm.1.refs_0_, bf16[8,8192]{1,0:T(8,128)(2,1)S(1)} %collective-permute-done.17.refs_1_, bf16[8,8192]{1,0:T(8,128)(2,1)S(1)} %collective-permute-done.14.refs_2_.refs_3_, ...), custom_call_target="tpu_custom_call" | custom-call | flops 3221225472 | bytes 50331648 | tf_op jit(solution)/shard_map/gate/pallas_call | solution.py:760
  99.7 9.6 %down.1 = (bf16[64,4096]{1,0:T(8,128)(2,1)S(1)}, bf16[64,4096]{1,0:T(8,128)(2,1)S(1)}) custom-call(s32[3]{0:T(128)S(1)} %pad_add_fusion.me.refs_0_, bf16[64,1536]{1,0:T(8,128)(2,1)S(1)} %gate.1.act, bf16[1536,8192]{1,0:T(8,128)(2,1)} %dw.1, bf16[32,2048]{1,0:T(8,128)(2,1)S(1)} %get-tuple-element.92.refs_0_, ...), custom_call_target="tpu_custom_call" | custom-call | flops 1610612736 | bytes 25165824 | tf_op jit(solution)/shard_map/down/pallas_call | solution.py:786
  112.5 1.5 collective-permute-start.31
  114.0 1.9 %collective-permute-start.32 = (bf16[64,1024]{1,0:T(8,128)(2,1)S(1)}, bf16[64,1024]{1,0:T(8,128)(2,1)S(1)}, u32[]{:S(2)}, u32[]{:S(2)}) collective-permute-start(bf16[64,1024]{1,0:T(8,128)(2,1)S(1)} %get-tuple-element.111), channel_id=1, source_target_pairs={{0,6},{2,4},{4,2},{6,0},{1,7},{3,5},{5,3},{7,1},{8,14},{10,12},{12... | collective-permute-start | bytes 393224 | tf_op jit(solution)/shard_map/ppermute | solution.py:34
  118.0 1.9 %collective-permute-done.27.refs_6_.refs_2_ = bf16[8,2048]{1,0:T(8,128)(2,1)S(1)} collective-permute-done((bf16[8,2048]{1,0:T(8,128)(2,1)S(1)}, bf16[8,2048]{1,0:T(8,128)(2,1)S(1)}, u32[]{:S(2)}, u32[]{:S(2)}) %collective-permute-start.27) | collective-permute-done | bytes 32800 | tf_op jit(solution)/shard_map/ppermute | solution.py:34
  119.9 1.4 collective-permute-start.29
  121.3 3.4 %collective-permute-done.29.refs_8_.refs_4_ = bf16[8,2048]{1,0:T(8,128)(2,1)S(1)} collective-permute-done((bf16[8,2048]{1,0:T(8,128)(2,1)S(1)}, bf16[8,2048]{1,0:T(8,128)(2,1)S(1)}, u32[]{:S(2)}, u32[]{:S(2)}) %collective-permute-start.29) | collective-permute-done | bytes 32800 | tf_op jit(solution)/shard_map/ppermute | solution.py:34
  128.4 1.5 %collective-permute-start.35 = (bf16[64,1024]{1,0:T(8,128)(2,1)S(1)}, bf16[64,1024]{1,0:T(8,128)(2,1)S(1)}, u32[]{:S(2)}, u32[]{:S(2)}) collective-permute-start(bf16[64,1024]{1,0:T(8,128)(2,1)S(1)} %get-tuple-element.115), channel_id=1, source_target_pairs={{0,24},{8,16},{16,8},{24,0},{1,25},{9,17},{17,9},{25,1},{2,26},{10... | collective-permute-start | bytes 393224 | tf_op jit(solution)/shard_map/ppermute | solution.py:34
  129.9 4.1 %place.1 = (f32[32,16,2048]{2,1,0:T(8,128)}, f32[8,128]{1,0:T(8,128)S(1)}) custom-call(s32[3]{0:T(128)S(1)} %pad_add_fusion.me.refs_0_, s32[1,4,8]{2,1,0:T(4,128)S(1)} %copy-done.5, f32[144,2048]{1,0:T(8,128)S(1)} %get-tuple-element.116.refs_0_, bf16[144,2048]{1,0:T(8,128)(2,1)S(1)} %collective-permute-done.23.refs_1_, ...), custom_call_target="tpu_custom_call" | custom-call | flops 100000 | bytes 4096 | tf_op jit(solution)/shard_map/place/pallas_call | solution.py:519
  134.0 1.5 %tail.1 = (f32[3,32,2048]{2,1,0:T(8,128)}, f32[8,128]{1,0:T(8,128)S(1)}) custom-call(s32[3]{0:T(128)S(1)} %pad_add_fusion.me.refs_0_, s32[1,4,8]{2,1,0:T(4,128)S(1)} %copy-done.5, bf16[2,32,2048]{2,1,0:T(8,128)(2,1)S(1)} %copy-done, f32[144,2048]{1,0:T(8,128)S(1)} %get-tuple-element.116.refs_0_, bf16[144,2048]{1,0:T(8,128)(2,1)S(1)} %collective-permute-done.23.refs_1_, ...), custom_call_target="tpu_custom_call" | custom-call | flops 100000 | bytes 4096 | tf_op jit(solution)/shard_map/tail/pallas_call | solution.py:816
  137.5 2.4 %collective-permute-start.37 = (bf16[8,2048]{1,0:T(8,128)(2,1)S(1)}, bf16[8,2048]{1,0:T(8,128)(2,1)S(1)}, u32[]{:S(2)}, u32[]{:S(2)}) collective-permute-start(bf16[8,2048]{1,0:T(8,128)(2,1)S(1)} %get-tuple-element.122), channel_id=1, source_target_pairs={{0,2},{2,0},{4,6},{6,4},{1,3},{3,1},{5,7},{7,5},{8,10},{10,8},{12,... | collective-permute-start | bytes 98312 | tf_op jit(solution)/shard_map/ppermute | solution.py:34
  140.5 1.9 %collective-permute-start.39 = (bf16[8,2048]{1,0:T(8,128)(2,1)S(1)}, bf16[8,2048]{1,0:T(8,128)(2,1)S(1)}, u32[]{:S(2)}, u32[]{:S(2)}) collective-permute-start(bf16[8,2048]{1,0:T(8,128)(2,1)S(1)} %get-tuple-element.124), channel_id=1, source_target_pairs={{0,6},{2,4},{4,2},{6,0},{1,7},{3,5},{5,3},{7,1},{8,14},{10,12},{12... | collective-permute-start | bytes 98312 | tf_op jit(solution)/shard_map/ppermute | solution.py:34
  142.4 2.9 %collective-permute-done.38.refs_7_ = bf16[8,2048]{1,0:T(8,128)(2,1)S(1)} collective-permute-done((bf16[8,2048]{1,0:T(8,128)(2,1)S(1)}, bf16[8,2048]{1,0:T(8,128)(2,1)S(1)}, u32[]{:S(2)}, u32[]{:S(2)}) %collective-permute-start.38) | collective-permute-done | bytes 32800 | tf_op jit(solution)/shard_map/ppermute | solution.py:34
  (98 shorter events, 34.5 us)
Async XLA Ops:
  3.0 8.8 %collective-permute-start = (bf16[8,12544]{1,0:T(8,128)(2,1)S(1)}, bf16[8,12544]{1,0:T(8,128)(2,1)S(1)}, u32[]{:S(2)}, u32[]{:S(2)}) collective-permute-start(bf16[8,12544]{1,0:T(8,128)(2,1)S(1)} %get-tuple-element.66), channel_id=1, source_target_pairs={{0,8},{8,0},{16,24},{24,16},{1,9},{9,1},{17,25},{25,17},{2,10},{10... | collective-permute-start | bytes 602120 | tf_op jit(solution)/shard_map/ppermute | solution.py:34
  6.0 10.8 %collective-permute-start.1 = (bf16[8,12544]{1,0:T(8,128)(2,1)S(1)}, bf16[8,12544]{1,0:T(8,128)(2,1)S(1)}, u32[]{:S(2)}, u32[]{:S(2)}) collective-permute-start(bf16[8,12544]{1,0:T(8,128)(2,1)S(1)} %get-tuple-element.67), channel_id=1, source_target_pairs={{0,16},{8,24},{16,0},{24,8},{1,17},{9,25},{17,1},{25,9},{2,18},{10... | collective-permute-start | bytes 602120 | tf_op jit(solution)/shard_map/ppermute | solution.py:34
  7.5 9.2 %collective-permute-start.2 = (bf16[8,12544]{1,0:T(8,128)(2,1)S(1)}, bf16[8,12544]{1,0:T(8,128)(2,1)S(1)}, u32[]{:S(2)}, u32[]{:S(2)}) collective-permute-start(bf16[8,12544]{1,0:T(8,128)(2,1)S(1)} %get-tuple-element.68), channel_id=1, source_target_pairs={{0,24},{8,16},{16,8},{24,0},{1,25},{9,17},{17,9},{25,1},{2,26},{10... | collective-permute-start | bytes 602120 | tf_op jit(solution)/shard_map/ppermute | solution.py:34
  22.6 13.0 %collective-permute-start.3 = (bf16[64,2048]{1,0:T(8,128)(2,1)S(1)}, bf16[64,2048]{1,0:T(8,128)(2,1)S(1)}, u32[]{:S(2)}, u32[]{:S(2)}) collective-permute-start(bf16[64,2048]{1,0:T(8,128)(2,1)S(1)} %get-tuple-element.73.refs_0_), channel_id=1, source_target_pairs={{0,8},{8,0},{16,24},{24,16},{1,9},{9,1},{17,25},{25,17},{2,10},{10... | collective-permute-start | bytes 786440 | tf_op jit(solution)/shard_map/ppermute | solution.py:34
  23.9 12.5 %collective-permute-start.4 = (bf16[64,2048]{1,0:T(8,128)(2,1)S(1)}, bf16[64,2048]{1,0:T(8,128)(2,1)S(1)}, u32[]{:S(2)}, u32[]{:S(2)}) collective-permute-start(bf16[64,2048]{1,0:T(8,128)(2,1)S(1)} %get-tuple-element.73.refs_0_), channel_id=1, source_target_pairs={{0,16},{8,24},{16,0},{24,8},{1,17},{9,25},{17,1},{25,9},{2,18},{10... | collective-permute-start | bytes 786440 | tf_op jit(solution)/shard_map/ppermute | solution.py:34
  24.7 11.7 %collective-permute-start.5 = (bf16[64,2048]{1,0:T(8,128)(2,1)S(1)}, bf16[64,2048]{1,0:T(8,128)(2,1)S(1)}, u32[]{:S(2)}, u32[]{:S(2)}) collective-permute-start(bf16[64,2048]{1,0:T(8,128)(2,1)S(1)} %get-tuple-element.73.refs_0_), channel_id=1, source_target_pairs={{0,24},{8,16},{16,8},{24,0},{1,25},{9,17},{17,9},{25,1},{2,26},{10... | collective-permute-start | bytes 786440 | tf_op jit(solution)/shard_map/ppermute | solution.py:34
  42.3 34.0 %collective-permute-start.6 = (bf16[128,2048]{1,0:T(8,128)(2,1)S(1)}, bf16[128,2048]{1,0:T(8,128)(2,1)S(1)}, u32[]{:S(2)}, u32[]{:S(2)}) collective-permute-start(bf16[128,2048]{1,0:T(8,128)(2,1)S(1)} %get-tuple-element.78), channel_id=1, source_target_pairs={{0,1},{1,0},{2,3},{3,2},{4,5},{5,4},{6,7},{7,6},{8,9},{9,8},{10,11... | collective-permute-start | bytes 1572872 | tf_op jit(solution)/shard_map/ppermute | solution.py:34
  44.3 8.2 %collective-permute-start.10 = (bf16[32,2048]{1,0:T(8,128)(2,1)S(1)}, bf16[32,2048]{1,0:T(8,128)(2,1)S(1)}, u32[]{:S(2)}, u32[]{:S(2)}) collective-permute-start(bf16[32,2048]{1,0:T(8,128)(2,1)S(1)} %get-tuple-element.84), channel_id=1, source_target_pairs={{0,6},{2,4},{4,2},{6,0},{1,7},{3,5},{5,3},{7,1},{8,14},{10,12},{12... | collective-permute-start | bytes 393224 | tf_op jit(solution)/shard_map/ppermute | solution.py:34
  48.0 7.7 %collective-permute-start.8 = (bf16[32,2048]{1,0:T(8,128)(2,1)S(1)}, bf16[32,2048]{1,0:T(8,128)(2,1)S(1)}, u32[]{:S(2)}, u32[]{:S(2)}) collective-permute-start(bf16[32,2048]{1,0:T(8,128)(2,1)S(1)} %get-tuple-element.82), channel_id=1, source_target_pairs={{0,2},{2,0},{4,6},{6,4},{1,3},{3,1},{5,7},{7,5},{8,10},{10,8},{12,... | collective-permute-start | bytes 393224 | tf_op jit(solution)/shard_map/ppermute | solution.py:34
  48.0 11.4 %collective-permute-start.9 = (bf16[32,2048]{1,0:T(8,128)(2,1)S(1)}, bf16[32,2048]{1,0:T(8,128)(2,1)S(1)}, u32[]{:S(2)}, u32[]{:S(2)}) collective-permute-start(bf16[32,2048]{1,0:T(8,128)(2,1)S(1)} %get-tuple-element.83), channel_id=1, source_target_pairs={{0,4},{2,6},{4,0},{6,2},{1,5},{3,7},{5,1},{7,3},{8,12},{10,14},{12... | collective-permute-start | bytes 393224 | tf_op jit(solution)/shard_map/ppermute | solution.py:34
  59.5 4.1 %collective-permute-start.11 = (bf16[8,2048]{1,0:T(8,128)(2,1)S(1)}, bf16[8,2048]{1,0:T(8,128)(2,1)S(1)}, u32[]{:S(2)}, u32[]{:S(2)}) collective-permute-start(bf16[8,2048]{1,0:T(8,128)(2,1)S(1)} %get-tuple-element.86), channel_id=1, source_target_pairs={{0,8},{8,0},{16,24},{24,16},{1,9},{9,1},{17,25},{25,17},{2,10},{10... | collective-permute-start | bytes 98312 | tf_op jit(solution)/shard_map/ppermute | solution.py:34
  60.1 4.2 %collective-permute-start.12 = (bf16[8,2048]{1,0:T(8,128)(2,1)S(1)}, bf16[8,2048]{1,0:T(8,128)(2,1)S(1)}, u32[]{:S(2)}, u32[]{:S(2)}) collective-permute-start(bf16[8,2048]{1,0:T(8,128)(2,1)S(1)} %get-tuple-element.87), channel_id=1, source_target_pairs={{0,16},{8,24},{16,0},{24,8},{1,17},{9,25},{17,1},{25,9},{2,18},{10... | collective-permute-start | bytes 98312 | tf_op jit(solution)/shard_map/ppermute | solution.py:34
  61.3 4.8 %collective-permute-start.13 = (bf16[8,2048]{1,0:T(8,128)(2,1)S(1)}, bf16[8,2048]{1,0:T(8,128)(2,1)S(1)}, u32[]{:S(2)}, u32[]{:S(2)}) collective-permute-start(bf16[8,2048]{1,0:T(8,128)(2,1)S(1)} %get-tuple-element.88), channel_id=1, source_target_pairs={{0,24},{8,16},{16,8},{24,0},{1,25},{9,17},{17,9},{25,1},{2,26},{10... | collective-permute-start | bytes 98312 | tf_op jit(solution)/shard_map/ppermute | solution.py:34
  66.8 7.2 %collective-permute-start.14 = (bf16[8,8192]{1,0:T(8,128)(2,1)S(1)}, bf16[8,8192]{1,0:T(8,128)(2,1)S(1)}, u32[]{:S(2)}, u32[]{:S(2)}) collective-permute-start(bf16[8,8192]{1,0:T(8,128)(2,1)S(1)} %norm.1.refs_0_), channel_id=1, source_target_pairs={{0,2},{2,0},{4,6},{6,4},{1,3},{3,1},{5,7},{7,5},{8,10},{10,8},{12,... | collective-permute-start | bytes 393224 | tf_op jit(solution)/shard_map/ppermute | solution.py:34
  66.9 11.3 %collective-permute-start.19 = (bf16[8,8192]{1,0:T(8,128)(2,1)S(1)}, bf16[8,8192]{1,0:T(8,128)(2,1)S(1)}, u32[]{:S(2)}, u32[]{:S(2)}) collective-permute-start(bf16[8,8192]{1,0:T(8,128)(2,1)S(1)} %norm.1.refs_0_), channel_id=1, source_target_pairs={{0,4},{2,6},{4,0},{6,2},{1,5},{3,7},{5,1},{7,3},{8,12},{10,14},{12... | collective-permute-start | bytes 393224 | tf_op jit(solution)/shard_map/ppermute | solution.py:34
  69.9 8.3 %collective-permute-start.21 = (bf16[8,8192]{1,0:T(8,128)(2,1)S(1)}, bf16[8,8192]{1,0:T(8,128)(2,1)S(1)}, u32[]{:S(2)}, u32[]{:S(2)}) collective-permute-start(bf16[8,8192]{1,0:T(8,128)(2,1)S(1)} %norm.1.refs_0_), channel_id=1, source_target_pairs={{0,6},{2,4},{4,2},{6,0},{1,7},{3,5},{5,3},{7,1},{8,14},{10,12},{12... | collective-permute-start | bytes 393224 | tf_op jit(solution)/shard_map/ppermute | solution.py:34
  74.1 25.6 %collective-permute-start.23 = (bf16[144,2048]{1,0:T(8,128)(2,1)S(1)}, bf16[144,2048]{1,0:T(8,128)(2,1)S(1)}, u32[]{:S(2)}, u32[]{:S(2)}) collective-permute-start(bf16[144,2048]{1,0:T(8,128)(2,1)S(1)} %get-tuple-element.98), channel_id=1, source_target_pairs={{0,8},{8,0},{16,24},{24,16},{1,9},{9,1},{17,25},{25,17},{2,10},{10... | collective-permute-start | bytes 1769480 | tf_op jit(solution)/shard_map/ppermute | solution.py:34
  75.1 24.6 %collective-permute-start.24 = (bf16[144,2048]{1,0:T(8,128)(2,1)S(1)}, bf16[144,2048]{1,0:T(8,128)(2,1)S(1)}, u32[]{:S(2)}, u32[]{:S(2)}) collective-permute-start(bf16[144,2048]{1,0:T(8,128)(2,1)S(1)} %get-tuple-element.99), channel_id=1, source_target_pairs={{0,16},{8,24},{16,0},{24,8},{1,17},{9,25},{17,1},{25,9},{2,18},{10... | collective-permute-start | bytes 1769480 | tf_op jit(solution)/shard_map/ppermute | solution.py:34
  76.3 23.3 %collective-permute-start.25 = (bf16[144,2048]{1,0:T(8,128)(2,1)S(1)}, bf16[144,2048]{1,0:T(8,128)(2,1)S(1)}, u32[]{:S(2)}, u32[]{:S(2)}) collective-permute-start(bf16[144,2048]{1,0:T(8,128)(2,1)S(1)} %get-tuple-element.100), channel_id=1, source_target_pairs={{0,24},{8,16},{16,8},{24,0},{1,25},{9,17},{17,9},{25,1},{2,26},{10... | collective-permute-start | bytes 1769480 | tf_op jit(solution)/shard_map/ppermute | solution.py:34
  80.9 18.7 %collective-permute-start.15 = (bf16[64,2048]{1,0:T(8,128)(2,1)S(1)}, bf16[64,2048]{1,0:T(8,128)(2,1)S(1)}, u32[]{:S(2)}, u32[]{:S(2)}) collective-permute-start(bf16[64,2048]{1,0:T(8,128)(2,1)S(1)} %get-tuple-element.90), channel_id=1, source_target_pairs={{0,4},{2,6},{4,0},{6,2},{1,5},{3,7},{5,1},{7,3},{8,12},{10,14},{12... | collective-permute-start | bytes 786440 | tf_op jit(solution)/shard_map/ppermute | solution.py:34
  109.5 6.4 %collective-permute-start.16 = (bf16[32,2048]{1,0:T(8,128)(2,1)S(1)}, bf16[32,2048]{1,0:T(8,128)(2,1)S(1)}, u32[]{:S(2)}, u32[]{:S(2)}) collective-permute-start(bf16[32,2048]{1,0:T(8,128)(2,1)S(1)} %get-tuple-element.92.refs_0_), channel_id=1, source_target_pairs={{0,2},{2,0},{4,6},{6,4},{1,3},{3,1},{5,7},{7,5},{8,10},{10,8},{12,... | collective-permute-start | bytes 393224 | tf_op jit(solution)/shard_map/ppermute | solution.py:34
  111.4 13.3 %collective-permute-start.30 = (bf16[64,1024]{1,0:T(8,128)(2,1)S(1)}, bf16[64,1024]{1,0:T(8,128)(2,1)S(1)}, u32[]{:S(2)}, u32[]{:S(2)}) collective-permute-start(bf16[64,1024]{1,0:T(8,128)(2,1)S(1)} %get-tuple-element.103.refs_2_), channel_id=1, source_target_pairs={{0,2},{2,0},{4,6},{6,4},{1,3},{3,1},{5,7},{7,5},{8,10},{10,8},{12,... | collective-permute-start | bytes 393224 | tf_op jit(solution)/shard_map/ppermute | solution.py:34
  112.5 12.9 %collective-permute-start.31 = (bf16[64,1024]{1,0:T(8,128)(2,1)S(1)}, bf16[64,1024]{1,0:T(8,128)(2,1)S(1)}, u32[]{:S(2)}, u32[]{:S(2)}) collective-permute-start(bf16[64,1024]{1,0:T(8,128)(2,1)S(1)} %get-tuple-element.110), channel_id=1, source_target_pairs={{0,4},{2,6},{4,0},{6,2},{1,5},{3,7},{5,1},{7,3},{8,12},{10,14},{12... | collective-permute-start | bytes 393224 | tf_op jit(solution)/shard_map/ppermute | solution.py:34
  114.0 11.4 %collective-permute-start.32 = (bf16[64,1024]{1,0:T(8,128)(2,1)S(1)}, bf16[64,1024]{1,0:T(8,128)(2,1)S(1)}, u32[]{:S(2)}, u32[]{:S(2)}) collective-permute-start(bf16[64,1024]{1,0:T(8,128)(2,1)S(1)} %get-tuple-element.111), channel_id=1, source_target_pairs={{0,6},{2,4},{4,2},{6,0},{1,7},{3,5},{5,3},{7,1},{8,14},{10,12},{12... | collective-permute-start | bytes 393224 | tf_op jit(solution)/shard_map/ppermute | solution.py:34
  116.9 4.5 %collective-permute-start.28 = (bf16[8,2048]{1,0:T(8,128)(2,1)S(1)}, bf16[8,2048]{1,0:T(8,128)(2,1)S(1)}, u32[]{:S(2)}, u32[]{:S(2)}) collective-permute-start(bf16[8,2048]{1,0:T(8,128)(2,1)S(1)} %get-tuple-element.106), channel_id=1, source_target_pairs={{0,16},{8,24},{16,0},{24,8},{1,17},{9,25},{17,1},{25,9},{2,18},{10... | collective-permute-start | bytes 98312 | tf_op jit(solution)/shard_map/ppermute | solution.py:34
  119.9 4.8 %collective-permute-start.29 = (bf16[8,2048]{1,0:T(8,128)(2,1)S(1)}, bf16[8,2048]{1,0:T(8,128)(2,1)S(1)}, u32[]{:S(2)}, u32[]{:S(2)}) collective-permute-start(bf16[8,2048]{1,0:T(8,128)(2,1)S(1)} %get-tuple-element.107), channel_id=1, source_target_pairs={{0,24},{8,16},{16,8},{24,0},{1,25},{9,17},{17,9},{25,1},{2,26},{10... | collective-permute-start | bytes 98312 | tf_op jit(solution)/shard_map/ppermute | solution.py:34
  126.4 9.2 %collective-permute-start.33 = (bf16[64,1024]{1,0:T(8,128)(2,1)S(1)}, bf16[64,1024]{1,0:T(8,128)(2,1)S(1)}, u32[]{:S(2)}, u32[]{:S(2)}) collective-permute-start(bf16[64,1024]{1,0:T(8,128)(2,1)S(1)} %get-tuple-element.113.refs_4_), channel_id=1, source_target_pairs={{0,8},{8,0},{16,24},{24,16},{1,9},{9,1},{17,25},{25,17},{2,10},{10... | collective-permute-start | bytes 393224 | tf_op jit(solution)/shard_map/ppermute | solution.py:34
  127.3 8.3 %collective-permute-start.34 = (bf16[64,1024]{1,0:T(8,128)(2,1)S(1)}, bf16[64,1024]{1,0:T(8,128)(2,1)S(1)}, u32[]{:S(2)}, u32[]{:S(2)}) collective-permute-start(bf16[64,1024]{1,0:T(8,128)(2,1)S(1)} %get-tuple-element.114), channel_id=1, source_target_pairs={{0,16},{8,24},{16,0},{24,8},{1,17},{9,25},{17,1},{25,9},{2,18},{10... | collective-permute-start | bytes 393224 | tf_op jit(solution)/shard_map/ppermute | solution.py:34
  128.4 7.2 %collective-permute-start.35 = (bf16[64,1024]{1,0:T(8,128)(2,1)S(1)}, bf16[64,1024]{1,0:T(8,128)(2,1)S(1)}, u32[]{:S(2)}, u32[]{:S(2)}) collective-permute-start(bf16[64,1024]{1,0:T(8,128)(2,1)S(1)} %get-tuple-element.115), channel_id=1, source_target_pairs={{0,24},{8,16},{16,8},{24,0},{1,25},{9,17},{17,9},{25,1},{2,26},{10... | collective-permute-start | bytes 393224 | tf_op jit(solution)/shard_map/ppermute | solution.py:34
  137.5 4.8 %collective-permute-start.37 = (bf16[8,2048]{1,0:T(8,128)(2,1)S(1)}, bf16[8,2048]{1,0:T(8,128)(2,1)S(1)}, u32[]{:S(2)}, u32[]{:S(2)}) collective-permute-start(bf16[8,2048]{1,0:T(8,128)(2,1)S(1)} %get-tuple-element.122), channel_id=1, source_target_pairs={{0,2},{2,0},{4,6},{6,4},{1,3},{3,1},{5,7},{7,5},{8,10},{10,8},{12,... | collective-permute-start | bytes 98312 | tf_op jit(solution)/shard_map/ppermute | solution.py:34
  139.9 5.4 %collective-permute-start.38 = (bf16[8,2048]{1,0:T(8,128)(2,1)S(1)}, bf16[8,2048]{1,0:T(8,128)(2,1)S(1)}, u32[]{:S(2)}, u32[]{:S(2)}) collective-permute-start(bf16[8,2048]{1,0:T(8,128)(2,1)S(1)} %get-tuple-element.123), channel_id=1, source_target_pairs={{0,4},{2,6},{4,0},{6,2},{1,5},{3,7},{5,1},{7,3},{8,12},{10,14},{12... | collective-permute-start | bytes 98312 | tf_op jit(solution)/shard_map/ppermute | solution.py:34
  140.5 5.7 %collective-permute-start.39 = (bf16[8,2048]{1,0:T(8,128)(2,1)S(1)}, bf16[8,2048]{1,0:T(8,128)(2,1)S(1)}, u32[]{:S(2)}, u32[]{:S(2)}) collective-permute-start(bf16[8,2048]{1,0:T(8,128)(2,1)S(1)} %get-tuple-element.124), channel_id=1, source_target_pairs={{0,6},{2,4},{4,2},{6,0},{1,7},{3,5},{5,3},{7,1},{8,14},{10,12},{12... | collective-permute-start | bytes 98312 | tf_op jit(solution)/shard_map/ppermute | solution.py:34
  (20 other events, 193.4 us)

commit v4 on v3

--- a/solution.py
+++ b/solution.py
@@ -72,7 +72,9 @@
         outs[k][:, at + 128 : at + 256] = lo[k * per : (k + 1) * per]
 
 
-def ssm_kernel(groups, per, steps, me, ss, *refs):
+def ssm_kernel(first, groups, per, steps, me, ss, *refs):
+    if first:
+        y_first, refs = refs[0], refs[1:]
     loads = refs[:groups]
     par, decay, conv, state, y_out = refs[groups : groups + 5]
     st_outs = refs[groups + 5 : 2 * groups + 5]
@@ -82,6 +84,10 @@
     cb = y_scr.shape[2]
     lb = min(256, cb)
     low = st_outs[0].shape[0] - per * states
+    done = 0
+    if first:
+        done = y_first.shape[0]
+        y_out[:done, :] = y_first[...]
     at = 3 * steps * ch
     masks = []
     for q in range(groups):
@@ -96,7 +102,7 @@
         base = pl.multiple_of(g * cb, cb)
         wide = pl.ds(base, cb)
         for q in range(groups):
-            slots = [ss[me[0], me[0] ^ q, i] for i in range(per)]
+            slots = [ss[me[0], me[0] ^ (q + first), i] for i in range(per)]
 
             def load(a):
                 return loads[q][:, pl.ds(pl.multiple_of(a * ch + base, cb), cb)].astype(F32)
@@ -142,11 +148,11 @@
                         )
                     st_outs[q][i * states : (i + 1) * states, there] = st.astype(st_outs[q].dtype)
             for t in range(steps):
-                row = (q * steps + t) * per
+                row = done + (q * steps + t) * per
                 y_out[row : row + per, wide] = ((y_scr[t] + skips[t]) * gates[t]).astype(BF)
 
 
-def ssm(per, steps, me, ss, payloads, par, decay, conv, state):
+def ssm(first, per, steps, me, ss, payloads, par, decay, conv, state):
     groups = len(payloads)
     states, ch = decay.shape
     cb = ch // 4
@@ -155,13 +161,14 @@
     vm = pl.BlockSpec(memory_space=pltpu.VMEM)
     sm = pl.BlockSpec(memory_space=pltpu.SMEM)
     args = list(payloads) + [par, decay, conv, state]
+    groups -= first
     return pl.pallas_call(
-        functools.partial(ssm_kernel, groups, per, steps),
+        functools.partial(ssm_kernel, first, groups, per, steps),
         in_specs=[sm, sm] + [vm] * len(args),
         out_specs=[vm] * (1 + groups),
-        out_shape=[jax.ShapeDtypeStruct((groups * steps * per, ch), BF)]
+        out_shape=[jax.ShapeDtypeStruct(((first + groups) * steps * per, ch), BF)]
         + [
-            jax.ShapeDtypeStruct((per * states + low, ch), BF if q else F32)
+            jax.ShapeDtypeStruct((per * states + low, ch), BF if first else F32)
             for q in range(groups)
         ],
         scratch_shapes=[
@@ -172,7 +179,7 @@
         ],
         compiler_params=params(4),
         cost_estimate=cost(3e6 * groups, groups * 3 << 20),
-        name="ssm",
+        name=f"ssm{first}",
     )(me, ss, *args)
 
 
@@ -660,7 +667,9 @@
         cost_estimate=cost(1e5, 1 << 12),
         name="fetch",
     )(*[in_hbm(a) for a in fixed], payload[0])
-    y_own, *kept = ssm(per, steps, me, ss, payload, *fixed)
+    y_first, own_kept = ssm(0, per, steps, me, ss, payload[:1], *fixed)
+    y_own, *kept = ssm(1, per, steps, me, ss, [y_first] + payload[1:], *fixed)
+    kept = [own_kept] + kept
     ys = [y_own] + [trade(y_own, "dp", n, k) for k in range(1, n)]
 
     n_slot, n_own = 2 * m * n * pe, 2 * m * n * rm
@@ -800,20 +809,9 @@
     moved = [cols[0]] + [trade(cols[k], "z", m, k) for k in range(1, m)]
 
     own = add_z(own_z, rm, "z_own", (cols[1],))
-    share_rows = total // n
-    outs = [((share_rows, pc), F32)] + [((share_rows, pc), BF)] * (n - 1)
-    rows_out = small(
-        functools.partial(spread_kernel, n, m),
-        "spread",
-        outs,
-        (me, expand, *moved),
-        tuple(own[1:]),
-        [pltpu.VMEM((total, pc), F32)],
-    )
-    new_state, placed = place(n, per, rows, states, me, rr, back, rows_out[1])
     low = kept[0].shape[0] - per * states
     tail_at = per * states // low
-    new_tail, placed = pl.pallas_call(
+    new_tail, tailed = pl.pallas_call(
         functools.partial(tail_kernel, n, per, taps),
         grid=(1,),
         in_specs=[sm, sm, pl.BlockSpec(x_input.shape, lambda g: (0, 0, 0))]
@@ -830,7 +828,18 @@
         compiler_params=params(8),
         cost_estimate=cost(1e5, 1 << 12),
         name="tail",
-    )(me, rr, x_input, *back, placed)
+    )(me, rr, x_input, *back, cols[1])
+    share_rows = total // n
+    outs = [((share_rows, pc), F32)] + [((share_rows, pc), BF)] * (n - 1)
+    rows_out = small(
+        functools.partial(spread_kernel, n, m),
+        "spread",
+        outs,
+        (me, expand, *moved),
+        (tailed, *own[1:]),
+        [pltpu.VMEM((total, pc), F32)],
+    )
+    new_state, placed = place(n, per, rows, states, me, rr, back, rows_out[1])
 
     mine = [rows_out[0]] + [trade(rows_out[k], "dp", n, k) for k in range(1, n)]
     deal_keep, deal_send = small(

time: 148 us -> 145 us (0.980)
  waiting for transfers between devices: 37.9 us -> 34.6 us
    ppermute x40, waiting for transfers between devices: 37.9 us -> 34.6 us  [trade(): return lax.ppermute(piece, axis, [(i, i ^ k) for i in range(size)])]
    pallas_call x1 -> x2, Pallas kernels: 5.07 us -> 5.97 us  [ssm(): pl.pallas_call(functools.partial(ssm_kernel, first, groups, per, steps),...]
  transfers between devices with their start and end apart: 40 -> 40, of which waited for: 21 -> 21; matrix products, arithmetic and copies ran while one was open for 1% -> 1% of each run, Pallas kernels for 24% -> 26%
where the time goes in v4:
time: 145 us
  Pallas kernels  61.9 us (43%)
  starting transfers between devices  44.6 us (31%)
  waiting for transfers between devices  34.6 us (24%)
  local copies, waits for them, and re-layouts  2.9 us (2%)
    ppermute x40, starting transfers between devices, trade(): return lax.ppermute(piece, axis, [(i, i ^ k) for i in range(size)])  44.6 us
    ppermute x40, waiting for transfers between devices, trade(): return lax.ppermute(piece, axis, [(i, i ^ k) for i in range(size)])  34.6 us
    pallas_call x1, Pallas kernels, body(): pl.pallas_call(functools.partial(gate_kernel, m), in_specs=[sm] + [vm] *...  17.3 us
    pallas_call x1, Pallas kernels, body(): pl.pallas_call(functools.partial(down_kernel, m, len(deps)), in_specs=[sm...  9.61 us
    pallas_call x1, Pallas kernels, body(): pl.pallas_call(functools.partial(load_kernel, chunks), in_specs=[pl.Block...  8.33 us
    pallas_call x2, Pallas kernels, ssm(): pl.pallas_call(functools.partial(ssm_kernel, first, groups, per, steps),...  5.97 us
    pallas_call x1, Pallas kernels, project(): pl.pallas_call(functools.partial(project_kernel, n), in_specs=[vm] * (n +...  5.81 us
    pallas_call x1, Pallas kernels, place(): pl.pallas_call(functools.partial(place_kernel, n, states), grid_spec=pltp...  4.1 us
  transfers between devices with their start and end apart: 40, of which 21 were waited for; matrix products, arithmetic and copies ran while one was open for 1% of the time, Pallas kernels for 26%

profile of v4, /device:TPU:0, one launch (start us, length us, event | category | flops | bytes accessed | tf_op | source)
XLA Modules:
  0.0 145.0 jit_solution(6361485656516328473)
XLA Ops:
  1.4 1.6 %pack.1 = (bf16[8,12544]{1,0:T(8,128)(2,1)S(1)}, bf16[8,12544]{1,0:T(8,128)(2,1)S(1)}, bf16[8,12544]{1,0:T(8,128)(2,1)S(1)}, bf16[8,12544]{1,0:T(8,128)(2,1)S(1)}) custom-call(s32[3]{0:T(128)S(1)} %pad_add_fusion.me.refs_0_, s32[1,4,8]{2,1,0:T(4,128)S(1)} %copy-done.5, bf16[2,32,2048]{2,1,0:T(8,128)(2,1)} %x.3, bf16[2,32,2048]{2,1,0:T(8,128)(2,1)} %z.1, ...), custom_call_target="tpu_custom_call" | custom-call | flops 1000000 | bytes 2097152 | tf_op jit(solution)/shard_map/pack/pallas_call | solution.py:642
  3.0 3.0 %collective-permute-start = (bf16[8,12544]{1,0:T(8,128)(2,1)S(1)}, bf16[8,12544]{1,0:T(8,128)(2,1)S(1)}, u32[]{:S(2)}, u32[]{:S(2)}) collective-permute-start(bf16[8,12544]{1,0:T(8,128)(2,1)S(1)} %get-tuple-element.72), channel_id=1, source_target_pairs={{0,8},{8,0},{16,24},{24,16},{1,9},{9,1},{17,25},{25,17},{2,10},{10... | collective-permute-start | bytes 602120 | tf_op jit(solution)/shard_map/ppermute | solution.py:34
  6.0 1.5 %collective-permute-start.1 = (bf16[8,12544]{1,0:T(8,128)(2,1)S(1)}, bf16[8,12544]{1,0:T(8,128)(2,1)S(1)}, u32[]{:S(2)}, u32[]{:S(2)}) collective-permute-start(bf16[8,12544]{1,0:T(8,128)(2,1)S(1)} %get-tuple-element.73), channel_id=1, source_target_pairs={{0,16},{8,24},{16,0},{24,8},{1,17},{9,25},{17,1},{25,9},{2,18},{10... | collective-permute-start | bytes 602120 | tf_op jit(solution)/shard_map/ppermute | solution.py:34
  7.5 1.5 %concatenate.3.refs_0_ = f32[8,2048]{1,0:T(8,128)} concatenate(f32[4,2048]{1,0:T(4,128)} %param.33, f32[1,2048]{1,0:T(1,128)} %bitcast.26, f32[1,2048]{1,0:T(1,128)} %bitcast.27, f32[1,2048]{1,0:T(1,128)} %bitcast.28, f32[1,2048]{1,0:T(1,128)S(1)} %broadcast_in_dim.15), dimensions={0} | concatenate | bytes 131072 | tf_op jit(solution)/shard_map/concatenate | solution.py:654
  9.0 2.6 %fetch.1 = (f32[8,2048]{1,0:T(8,128)S(1)}, f32[16,2048]{1,0:T(8,128)S(1)}, f32[3,32,2048]{2,1,0:T(8,128)S(1)}, f32[32,16,2048]{2,1,0:T(8,128)S(1)}) custom-call(f32[8,2048]{1,0:T(8,128)} %concatenate.3.refs_0_, f32[16,2048]{1,0:T(8,128)} %refs_1_.1, f32[3,32,2048]{2,1,0:T(8,128)} %bitcast.23, f32[32,16,2048]{2,1,0:T(8,128)} %refs_3_.1, ...), custom_call_target="tpu_custom_call" | custom-call | flops 100000 | bytes 4096 | tf_op jit(solution)/shard_map/fetch/pallas_call | solution.py:660
  12.3 1.9 %ssm0.1 = (bf16[16,2048]{1,0:T(8,128)(2,1)S(1)}, f32[144,2048]{1,0:T(8,128)S(1)}) custom-call(s32[3]{0:T(128)S(1)} %pad_add_fusion.me.refs_0_, s32[4,4,8]{2,1,0:T(4,128)S(1)} %copy-done.3, bf16[8,12544]{1,0:T(8,128)(2,1)S(1)} %get-tuple-element.66.refs_4_.refs_0_, f32[8,2048]{1,0:T(8,128)S(1)} %get-tuple-element.67.refs_1_.refs_4_, ...), custom_call_target="tpu_custom_call" | custom-call | flops 3000000 | bytes 3145728 | tf_op jit(solution)/shard_map/ssm0/pallas_call | solution.py:165
  14.2 2.5 %collective-permute-done.1.refs_2_ = bf16[8,12544]{1,0:T(8,128)(2,1)S(1)} collective-permute-done((bf16[8,12544]{1,0:T(8,128)(2,1)S(1)}, bf16[8,12544]{1,0:T(8,128)(2,1)S(1)}, u32[]{:S(2)}, u32[]{:S(2)}) %collective-permute-start.1) | collective-permute-done | bytes 200736 | tf_op jit(solution)/shard_map/ppermute | solution.py:34
  16.8 4.0 %ssm1.1 = (bf16[64,2048]{1,0:T(8,128)(2,1)S(1)}, bf16[144,2048]{1,0:T(8,128)(2,1)S(1)}, bf16[144,2048]{1,0:T(8,128)(2,1)S(1)}, bf16[144,2048]{1,0:T(8,128)(2,1)S(1)}) custom-call(s32[3]{0:T(128)S(1)} %pad_add_fusion.me.refs_0_, s32[4,4,8]{2,1,0:T(4,128)S(1)} %copy-done.3, bf16[16,2048]{1,0:T(8,128)(2,1)S(1)} %get-tuple-element.71.refs_0_, ...), custom_call_target="tpu_custom_call" | custom-call | flops 9000000 | bytes 9437184 | tf_op jit(solution)/shard_map/ssm1/pallas_call | solution.py:165
  23.0 1.5 %collective-permute-start.5 = (bf16[64,2048]{1,0:T(8,128)(2,1)S(1)}, bf16[64,2048]{1,0:T(8,128)(2,1)S(1)}, u32[]{:S(2)}, u32[]{:S(2)}) collective-permute-start(bf16[64,2048]{1,0:T(8,128)(2,1)S(1)} %get-tuple-element.75.refs_0_), channel_id=1, source_target_pairs={{0,24},{8,16},{16,8},{24,0},{1,25},{9,17},{17,9},{25,1},{2,26},{10... | collective-permute-start | bytes 786440 | tf_op jit(solution)/shard_map/ppermute | solution.py:34
  24.4 8.3 %load.1 = (bf16[8192,1536]{1,0:T(8,128)(2,1)S(1)}, f32[8,128]{1,0:T(8,128)S(1)}) custom-call(bf16[8192,1536]{1,0:T(8,128)(2,1)} %w.1, bf16[64,2048]{1,0:T(8,128)(2,1)S(1)} %get-tuple-element.75.refs_0_), custom_call_target="tpu_custom_call" | custom-call | flops 100000 | bytes 4096 | tf_op jit(solution)/shard_map/load/pallas_call | solution.py:704
  34.7 5.8 %project.1 = (bf16[128,2048]{1,0:T(8,128)(2,1)S(1)}, bf16[128,2048]{1,0:T(8,128)(2,1)S(1)}, bf16[128,2048]{1,0:T(8,128)(2,1)S(1)}, bf16[128,2048]{1,0:T(8,128)(2,1)S(1)}) custom-call(bf16[64,2048]{1,0:T(8,128)(2,1)S(1)} %get-tuple-element.75.refs_0_, bf16[64,2048]{1,0:T(8,128)(2,1)S(1)} %collective-permute-done.3.refs_1_, ...), custom_call_target="tpu_custom_call" | custom-call | flops 100000 | bytes 4096 | tf_op jit(solution)/shard_map/project/pallas_call | solution.py:275
  42.6 3.7 %collective-permute-start.10 = (bf16[32,2048]{1,0:T(8,128)(2,1)S(1)}, bf16[32,2048]{1,0:T(8,128)(2,1)S(1)}, u32[]{:S(2)}, u32[]{:S(2)}) collective-permute-start(bf16[32,2048]{1,0:T(8,128)(2,1)S(1)} %get-tuple-element.86), channel_id=1, source_target_pairs={{0,6},{2,4},{4,2},{6,0},{1,7},{3,5},{5,3},{7,1},{8,14},{10,12},{12... | collective-permute-start | bytes 393224 | tf_op jit(solution)/shard_map/ppermute | solution.py:34
  47.1 3.8 %collective-permute-done.10.refs_3_ = bf16[32,2048]{1,0:T(8,128)(2,1)S(1)} collective-permute-done((bf16[32,2048]{1,0:T(8,128)(2,1)S(1)}, bf16[32,2048]{1,0:T(8,128)(2,1)S(1)}, u32[]{:S(2)}, u32[]{:S(2)}) %collective-permute-start.10) | collective-permute-done | bytes 131104 | tf_op jit(solution)/shard_map/ppermute | solution.py:34
  50.8 3.1 %collective-permute-done.8.refs_1_ = bf16[32,2048]{1,0:T(8,128)(2,1)S(1)} collective-permute-done((bf16[32,2048]{1,0:T(8,128)(2,1)S(1)}, bf16[32,2048]{1,0:T(8,128)(2,1)S(1)}, u32[]{:S(2)}, u32[]{:S(2)}) %collective-permute-start.8) | collective-permute-done | bytes 131104 | tf_op jit(solution)/shard_map/ppermute | solution.py:34
  53.9 3.7 %collective-permute-done.9.refs_2_ = bf16[32,2048]{1,0:T(8,128)(2,1)S(1)} collective-permute-done((bf16[32,2048]{1,0:T(8,128)(2,1)S(1)}, bf16[32,2048]{1,0:T(8,128)(2,1)S(1)}, u32[]{:S(2)}, u32[]{:S(2)}) %collective-permute-start.9) | collective-permute-done | bytes 131104 | tf_op jit(solution)/shard_map/ppermute | solution.py:34
  59.6 1.7 %collective-permute-start.13 = (bf16[8,2048]{1,0:T(8,128)(2,1)S(1)}, bf16[8,2048]{1,0:T(8,128)(2,1)S(1)}, u32[]{:S(2)}, u32[]{:S(2)}) collective-permute-start(bf16[8,2048]{1,0:T(8,128)(2,1)S(1)} %get-tuple-element.90), channel_id=1, source_target_pairs={{0,24},{8,16},{16,8},{24,0},{1,25},{9,17},{17,9},{25,1},{2,26},{10... | collective-permute-start | bytes 98312 | tf_op jit(solution)/shard_map/ppermute | solution.py:34
  62.6 1.8 %collective-permute-done.13.refs_5_ = bf16[8,2048]{1,0:T(8,128)(2,1)S(1)} collective-permute-done((bf16[8,2048]{1,0:T(8,128)(2,1)S(1)}, bf16[8,2048]{1,0:T(8,128)(2,1)S(1)}, u32[]{:S(2)}, u32[]{:S(2)}) %collective-permute-start.13) | collective-permute-done | bytes 32800 | tf_op jit(solution)/shard_map/ppermute | solution.py:34
  65.2 3.0 %collective-permute-start.19 = (bf16[8,8192]{1,0:T(8,128)(2,1)S(1)}, bf16[8,8192]{1,0:T(8,128)(2,1)S(1)}, u32[]{:S(2)}, u32[]{:S(2)}) collective-permute-start(bf16[8,8192]{1,0:T(8,128)(2,1)S(1)} %norm.1.refs_0_), channel_id=1, source_target_pairs={{0,4},{2,6},{4,0},{6,2},{1,5},{3,7},{5,1},{7,3},{8,12},{10,14},{12... | collective-permute-start | bytes 393224 | tf_op jit(solution)/shard_map/ppermute | solution.py:34
  69.5 2.8 %collective-permute-done.14.refs_2_.refs_3_ = bf16[8,8192]{1,0:T(8,128)(2,1)S(1)} collective-permute-done((bf16[8,8192]{1,0:T(8,128)(2,1)S(1)}, bf16[8,8192]{1,0:T(8,128)(2,1)S(1)}, u32[]{:S(2)}, u32[]{:S(2)}) %collective-permute-start.14) | collective-permute-done | bytes 131104 | tf_op jit(solution)/shard_map/ppermute | solution.py:34
  80.5 17.3 %gate.1.act = bf16[64,1536]{1,0:T(8,128)(2,1)S(1)} custom-call(s32[3]{0:T(128)S(1)} %pad_add_fusion.me.refs_0_, bf16[8,8192]{1,0:T(8,128)(2,1)S(1)} %norm.1.refs_0_, bf16[8,8192]{1,0:T(8,128)(2,1)S(1)} %collective-permute-done.17.refs_1_, bf16[8,8192]{1,0:T(8,128)(2,1)S(1)} %collective-permute-done.14.refs_2_.refs_3_, ...), custom_call_target="tpu_custom_call" | custom-call | flops 3221225472 | bytes 50331648 | tf_op jit(solution)/shard_map/gate/pallas_call | solution.py:769
  98.0 9.6 %down.1 = (bf16[64,4096]{1,0:T(8,128)(2,1)S(1)}, bf16[64,4096]{1,0:T(8,128)(2,1)S(1)}) custom-call(s32[3]{0:T(128)S(1)} %pad_add_fusion.me.refs_0_, bf16[64,1536]{1,0:T(8,128)(2,1)S(1)} %gate.1.act, bf16[1536,8192]{1,0:T(8,128)(2,1)} %dw.1, bf16[32,2048]{1,0:T(8,128)(2,1)S(1)} %get-tuple-element.94.refs_0_, ...), custom_call_target="tpu_custom_call" | custom-call | flops 1610612736 | bytes 25165824 | tf_op jit(solution)/shard_map/down/pallas_call | solution.py:795
  110.8 1.5 %collective-permute-start.31 = (bf16[64,1024]{1,0:T(8,128)(2,1)S(1)}, bf16[64,1024]{1,0:T(8,128)(2,1)S(1)}, u32[]{:S(2)}, u32[]{:S(2)}) collective-permute-start(bf16[64,1024]{1,0:T(8,128)(2,1)S(1)} %get-tuple-element.112), channel_id=1, source_target_pairs={{0,4},{2,6},{4,0},{6,2},{1,5},{3,7},{5,1},{7,3},{8,12},{10,14},{12... | collective-permute-start | bytes 393224 | tf_op jit(solution)/shard_map/ppermute | solution.py:34
  112.3 1.9 %collective-permute-start.32 = (bf16[64,1024]{1,0:T(8,128)(2,1)S(1)}, bf16[64,1024]{1,0:T(8,128)(2,1)S(1)}, u32[]{:S(2)}, u32[]{:S(2)}) collective-permute-start(bf16[64,1024]{1,0:T(8,128)(2,1)S(1)} %get-tuple-element.113), channel_id=1, source_target_pairs={{0,6},{2,4},{4,2},{6,0},{1,7},{3,5},{5,3},{7,1},{8,14},{10,12},{12... | collective-permute-start | bytes 393224 | tf_op jit(solution)/shard_map/ppermute | solution.py:34
  116.2 1.9 %collective-permute-done.27.refs_7_.refs_2_ = bf16[8,2048]{1,0:T(8,128)(2,1)S(1)} collective-permute-done((bf16[8,2048]{1,0:T(8,128)(2,1)S(1)}, bf16[8,2048]{1,0:T(8,128)(2,1)S(1)}, u32[]{:S(2)}, u32[]{:S(2)}) %collective-permute-start.27) | collective-permute-done | bytes 32800 | tf_op jit(solution)/shard_map/ppermute | solution.py:34
  118.2 1.4 collective-permute-start.29
  119.6 1.5 %tail.1 = (f32[3,32,2048]{2,1,0:T(8,128)}, f32[8,128]{1,0:T(8,128)S(1)}) custom-call(s32[3]{0:T(128)S(1)} %pad_add_fusion.me.refs_0_, s32[1,4,8]{2,1,0:T(4,128)S(1)} %copy-done.6, bf16[2,32,2048]{2,1,0:T(8,128)(2,1)S(1)} %copy-done, f32[144,2048]{1,0:T(8,128)S(1)} %get-tuple-element.114.refs_0_, bf16[144,2048]{1,0:T(8,128)(2,1)S(1)} %collective-permute-done.23.refs_1_, ...), custom_call_target="tpu_custom_call" | custom-call | flops 100000 | bytes 4096 | tf_op jit(solution)/shard_map/tail/pallas_call | solution.py:814
  121.1 1.8 %collective-permute-done.29.refs_9_.refs_4_ = bf16[8,2048]{1,0:T(8,128)(2,1)S(1)} collective-permute-done((bf16[8,2048]{1,0:T(8,128)(2,1)S(1)}, bf16[8,2048]{1,0:T(8,128)(2,1)S(1)}, u32[]{:S(2)}, u32[]{:S(2)}) %collective-permute-start.29) | collective-permute-done | bytes 32800 | tf_op jit(solution)/shard_map/ppermute | solution.py:34
  126.7 1.5 %collective-permute-start.35 = (bf16[64,1024]{1,0:T(8,128)(2,1)S(1)}, bf16[64,1024]{1,0:T(8,128)(2,1)S(1)}, u32[]{:S(2)}, u32[]{:S(2)}) collective-permute-start(bf16[64,1024]{1,0:T(8,128)(2,1)S(1)} %get-tuple-element.119), channel_id=1, source_target_pairs={{0,24},{8,16},{16,8},{24,0},{1,25},{9,17},{17,9},{25,1},{2,26},{10... | collective-permute-start | bytes 393224 | tf_op jit(solution)/shard_map/ppermute | solution.py:34
  128.2 4.1 %place.1 = (f32[32,16,2048]{2,1,0:T(8,128)}, f32[8,128]{1,0:T(8,128)S(1)}) custom-call(s32[3]{0:T(128)S(1)} %pad_add_fusion.me.refs_0_, s32[1,4,8]{2,1,0:T(4,128)S(1)} %copy-done.6, f32[144,2048]{1,0:T(8,128)S(1)} %get-tuple-element.114.refs_0_, bf16[144,2048]{1,0:T(8,128)(2,1)S(1)} %collective-permute-done.23.refs_1_, ...), custom_call_target="tpu_custom_call" | custom-call | flops 100000 | bytes 4096 | tf_op jit(solution)/shard_map/place/pallas_call | solution.py:526
  135.1 2.4 %collective-permute-start.37 = (bf16[8,2048]{1,0:T(8,128)(2,1)S(1)}, bf16[8,2048]{1,0:T(8,128)(2,1)S(1)}, u32[]{:S(2)}, u32[]{:S(2)}) collective-permute-start(bf16[8,2048]{1,0:T(8,128)(2,1)S(1)} %get-tuple-element.124), channel_id=1, source_target_pairs={{0,2},{2,0},{4,6},{6,4},{1,3},{3,1},{5,7},{7,5},{8,10},{10,8},{12,... | collective-permute-start | bytes 98312 | tf_op jit(solution)/shard_map/ppermute | solution.py:34
  138.1 1.8 %collective-permute-start.39 = (bf16[8,2048]{1,0:T(8,128)(2,1)S(1)}, bf16[8,2048]{1,0:T(8,128)(2,1)S(1)}, u32[]{:S(2)}, u32[]{:S(2)}) collective-permute-start(bf16[8,2048]{1,0:T(8,128)(2,1)S(1)} %get-tuple-element.126), channel_id=1, source_target_pairs={{0,6},{2,4},{4,2},{6,0},{1,7},{3,5},{5,3},{7,1},{8,14},{10,12},{12... | collective-permute-start | bytes 98312 | tf_op jit(solution)/shard_map/ppermute | solution.py:34
  139.9 2.9 %collective-permute-done.38.refs_7_ = bf16[8,2048]{1,0:T(8,128)(2,1)S(1)} collective-permute-done((bf16[8,2048]{1,0:T(8,128)(2,1)S(1)}, bf16[8,2048]{1,0:T(8,128)(2,1)S(1)}, u32[]{:S(2)}, u32[]{:S(2)}) %collective-permute-start.38) | collective-permute-done | bytes 32800 | tf_op jit(solution)/shard_map/ppermute | solution.py:34
  (99 shorter events, 36.5 us)
Async XLA Ops:
  3.0 11.2 %collective-permute-start = (bf16[8,12544]{1,0:T(8,128)(2,1)S(1)}, bf16[8,12544]{1,0:T(8,128)(2,1)S(1)}, u32[]{:S(2)}, u32[]{:S(2)}) collective-permute-start(bf16[8,12544]{1,0:T(8,128)(2,1)S(1)} %get-tuple-element.72), channel_id=1, source_target_pairs={{0,8},{8,0},{16,24},{24,16},{1,9},{9,1},{17,25},{25,17},{2,10},{10... | collective-permute-start | bytes 602120 | tf_op jit(solution)/shard_map/ppermute | solution.py:34
  6.0 10.8 %collective-permute-start.1 = (bf16[8,12544]{1,0:T(8,128)(2,1)S(1)}, bf16[8,12544]{1,0:T(8,128)(2,1)S(1)}, u32[]{:S(2)}, u32[]{:S(2)}) collective-permute-start(bf16[8,12544]{1,0:T(8,128)(2,1)S(1)} %get-tuple-element.73), channel_id=1, source_target_pairs={{0,16},{8,24},{16,0},{24,8},{1,17},{9,25},{17,1},{25,9},{2,18},{10... | collective-permute-start | bytes 602120 | tf_op jit(solution)/shard_map/ppermute | solution.py:34
  7.5 9.2 %collective-permute-start.2 = (bf16[8,12544]{1,0:T(8,128)(2,1)S(1)}, bf16[8,12544]{1,0:T(8,128)(2,1)S(1)}, u32[]{:S(2)}, u32[]{:S(2)}) collective-permute-start(bf16[8,12544]{1,0:T(8,128)(2,1)S(1)} %get-tuple-element.74), channel_id=1, source_target_pairs={{0,24},{8,16},{16,8},{24,0},{1,25},{9,17},{17,9},{25,1},{2,26},{10... | collective-permute-start | bytes 602120 | tf_op jit(solution)/shard_map/ppermute | solution.py:34
  20.9 13.0 %collective-permute-start.3 = (bf16[64,2048]{1,0:T(8,128)(2,1)S(1)}, bf16[64,2048]{1,0:T(8,128)(2,1)S(1)}, u32[]{:S(2)}, u32[]{:S(2)}) collective-permute-start(bf16[64,2048]{1,0:T(8,128)(2,1)S(1)} %get-tuple-element.75.refs_0_), channel_id=1, source_target_pairs={{0,8},{8,0},{16,24},{24,16},{1,9},{9,1},{17,25},{25,17},{2,10},{10... | collective-permute-start | bytes 786440 | tf_op jit(solution)/shard_map/ppermute | solution.py:34
  22.2 12.5 %collective-permute-start.4 = (bf16[64,2048]{1,0:T(8,128)(2,1)S(1)}, bf16[64,2048]{1,0:T(8,128)(2,1)S(1)}, u32[]{:S(2)}, u32[]{:S(2)}) collective-permute-start(bf16[64,2048]{1,0:T(8,128)(2,1)S(1)} %get-tuple-element.75.refs_0_), channel_id=1, source_target_pairs={{0,16},{8,24},{16,0},{24,8},{1,17},{9,25},{17,1},{25,9},{2,18},{10... | collective-permute-start | bytes 786440 | tf_op jit(solution)/shard_map/ppermute | solution.py:34
  23.0 11.7 %collective-permute-start.5 = (bf16[64,2048]{1,0:T(8,128)(2,1)S(1)}, bf16[64,2048]{1,0:T(8,128)(2,1)S(1)}, u32[]{:S(2)}, u32[]{:S(2)}) collective-permute-start(bf16[64,2048]{1,0:T(8,128)(2,1)S(1)} %get-tuple-element.75.refs_0_), channel_id=1, source_target_pairs={{0,24},{8,16},{16,8},{24,0},{1,25},{9,17},{17,9},{25,1},{2,26},{10... | collective-permute-start | bytes 786440 | tf_op jit(solution)/shard_map/ppermute | solution.py:34
  40.6 34.0 %collective-permute-start.6 = (bf16[128,2048]{1,0:T(8,128)(2,1)S(1)}, bf16[128,2048]{1,0:T(8,128)(2,1)S(1)}, u32[]{:S(2)}, u32[]{:S(2)}) collective-permute-start(bf16[128,2048]{1,0:T(8,128)(2,1)S(1)} %get-tuple-element.80), channel_id=1, source_target_pairs={{0,1},{1,0},{2,3},{3,2},{4,5},{5,4},{6,7},{7,6},{8,9},{9,8},{10,11... | collective-permute-start | bytes 1572872 | tf_op jit(solution)/shard_map/ppermute | solution.py:34
  42.6 8.2 %collective-permute-start.10 = (bf16[32,2048]{1,0:T(8,128)(2,1)S(1)}, bf16[32,2048]{1,0:T(8,128)(2,1)S(1)}, u32[]{:S(2)}, u32[]{:S(2)}) collective-permute-start(bf16[32,2048]{1,0:T(8,128)(2,1)S(1)} %get-tuple-element.86), channel_id=1, source_target_pairs={{0,6},{2,4},{4,2},{6,0},{1,7},{3,5},{5,3},{7,1},{8,14},{10,12},{12... | collective-permute-start | bytes 393224 | tf_op jit(solution)/shard_map/ppermute | solution.py:34
  46.3 7.7 %collective-permute-start.8 = (bf16[32,2048]{1,0:T(8,128)(2,1)S(1)}, bf16[32,2048]{1,0:T(8,128)(2,1)S(1)}, u32[]{:S(2)}, u32[]{:S(2)}) collective-permute-start(bf16[32,2048]{1,0:T(8,128)(2,1)S(1)} %get-tuple-element.84), channel_id=1, source_target_pairs={{0,2},{2,0},{4,6},{6,4},{1,3},{3,1},{5,7},{7,5},{8,10},{10,8},{12,... | collective-permute-start | bytes 393224 | tf_op jit(solution)/shard_map/ppermute | solution.py:34
  46.3 11.4 %collective-permute-start.9 = (bf16[32,2048]{1,0:T(8,128)(2,1)S(1)}, bf16[32,2048]{1,0:T(8,128)(2,1)S(1)}, u32[]{:S(2)}, u32[]{:S(2)}) collective-permute-start(bf16[32,2048]{1,0:T(8,128)(2,1)S(1)} %get-tuple-element.85), channel_id=1, source_target_pairs={{0,4},{2,6},{4,0},{6,2},{1,5},{3,7},{5,1},{7,3},{8,12},{10,14},{12... | collective-permute-start | bytes 393224 | tf_op jit(solution)/shard_map/ppermute | solution.py:34
  57.8 4.1 %collective-permute-start.11 = (bf16[8,2048]{1,0:T(8,128)(2,1)S(1)}, bf16[8,2048]{1,0:T(8,128)(2,1)S(1)}, u32[]{:S(2)}, u32[]{:S(2)}) collective-permute-start(bf16[8,2048]{1,0:T(8,128)(2,1)S(1)} %get-tuple-element.88), channel_id=1, source_target_pairs={{0,8},{8,0},{16,24},{24,16},{1,9},{9,1},{17,25},{25,17},{2,10},{10... | collective-permute-start | bytes 98312 | tf_op jit(solution)/shard_map/ppermute | solution.py:34
  58.4 4.2 %collective-permute-start.12 = (bf16[8,2048]{1,0:T(8,128)(2,1)S(1)}, bf16[8,2048]{1,0:T(8,128)(2,1)S(1)}, u32[]{:S(2)}, u32[]{:S(2)}) collective-permute-start(bf16[8,2048]{1,0:T(8,128)(2,1)S(1)} %get-tuple-element.89), channel_id=1, source_target_pairs={{0,16},{8,24},{16,0},{24,8},{1,17},{9,25},{17,1},{25,9},{2,18},{10... | collective-permute-start | bytes 98312 | tf_op jit(solution)/shard_map/ppermute | solution.py:34
  59.6 4.8 %collective-permute-start.13 = (bf16[8,2048]{1,0:T(8,128)(2,1)S(1)}, bf16[8,2048]{1,0:T(8,128)(2,1)S(1)}, u32[]{:S(2)}, u32[]{:S(2)}) collective-permute-start(bf16[8,2048]{1,0:T(8,128)(2,1)S(1)} %get-tuple-element.90), channel_id=1, source_target_pairs={{0,24},{8,16},{16,8},{24,0},{1,25},{9,17},{17,9},{25,1},{2,26},{10... | collective-permute-start | bytes 98312 | tf_op jit(solution)/shard_map/ppermute | solution.py:34
  65.1 7.2 %collective-permute-start.14 = (bf16[8,8192]{1,0:T(8,128)(2,1)S(1)}, bf16[8,8192]{1,0:T(8,128)(2,1)S(1)}, u32[]{:S(2)}, u32[]{:S(2)}) collective-permute-start(bf16[8,8192]{1,0:T(8,128)(2,1)S(1)} %norm.1.refs_0_), channel_id=1, source_target_pairs={{0,2},{2,0},{4,6},{6,4},{1,3},{3,1},{5,7},{7,5},{8,10},{10,8},{12,... | collective-permute-start | bytes 393224 | tf_op jit(solution)/shard_map/ppermute | solution.py:34
  65.2 11.3 %collective-permute-start.19 = (bf16[8,8192]{1,0:T(8,128)(2,1)S(1)}, bf16[8,8192]{1,0:T(8,128)(2,1)S(1)}, u32[]{:S(2)}, u32[]{:S(2)}) collective-permute-start(bf16[8,8192]{1,0:T(8,128)(2,1)S(1)} %norm.1.refs_0_), channel_id=1, source_target_pairs={{0,4},{2,6},{4,0},{6,2},{1,5},{3,7},{5,1},{7,3},{8,12},{10,14},{12... | collective-permute-start | bytes 393224 | tf_op jit(solution)/shard_map/ppermute | solution.py:34
  68.2 8.3 %collective-permute-start.21 = (bf16[8,8192]{1,0:T(8,128)(2,1)S(1)}, bf16[8,8192]{1,0:T(8,128)(2,1)S(1)}, u32[]{:S(2)}, u32[]{:S(2)}) collective-permute-start(bf16[8,8192]{1,0:T(8,128)(2,1)S(1)} %norm.1.refs_0_), channel_id=1, source_target_pairs={{0,6},{2,4},{4,2},{6,0},{1,7},{3,5},{5,3},{7,1},{8,14},{10,12},{12... | collective-permute-start | bytes 393224 | tf_op jit(solution)/shard_map/ppermute | solution.py:34
  72.3 25.6 %collective-permute-start.23 = (bf16[144,2048]{1,0:T(8,128)(2,1)S(1)}, bf16[144,2048]{1,0:T(8,128)(2,1)S(1)}, u32[]{:S(2)}, u32[]{:S(2)}) collective-permute-start(bf16[144,2048]{1,0:T(8,128)(2,1)S(1)} %get-tuple-element.100), channel_id=1, source_target_pairs={{0,8},{8,0},{16,24},{24,16},{1,9},{9,1},{17,25},{25,17},{2,10},{10... | collective-permute-start | bytes 1769480 | tf_op jit(solution)/shard_map/ppermute | solution.py:34
  73.4 24.6 %collective-permute-start.24 = (bf16[144,2048]{1,0:T(8,128)(2,1)S(1)}, bf16[144,2048]{1,0:T(8,128)(2,1)S(1)}, u32[]{:S(2)}, u32[]{:S(2)}) collective-permute-start(bf16[144,2048]{1,0:T(8,128)(2,1)S(1)} %get-tuple-element.101), channel_id=1, source_target_pairs={{0,16},{8,24},{16,0},{24,8},{1,17},{9,25},{17,1},{25,9},{2,18},{10... | collective-permute-start | bytes 1769480 | tf_op jit(solution)/shard_map/ppermute | solution.py:34
  74.6 23.3 %collective-permute-start.25 = (bf16[144,2048]{1,0:T(8,128)(2,1)S(1)}, bf16[144,2048]{1,0:T(8,128)(2,1)S(1)}, u32[]{:S(2)}, u32[]{:S(2)}) collective-permute-start(bf16[144,2048]{1,0:T(8,128)(2,1)S(1)} %get-tuple-element.102), channel_id=1, source_target_pairs={{0,24},{8,16},{16,8},{24,0},{1,25},{9,17},{17,9},{25,1},{2,26},{10... | collective-permute-start | bytes 1769480 | tf_op jit(solution)/shard_map/ppermute | solution.py:34
  79.1 18.7 %collective-permute-start.15 = (bf16[64,2048]{1,0:T(8,128)(2,1)S(1)}, bf16[64,2048]{1,0:T(8,128)(2,1)S(1)}, u32[]{:S(2)}, u32[]{:S(2)}) collective-permute-start(bf16[64,2048]{1,0:T(8,128)(2,1)S(1)} %get-tuple-element.92), channel_id=1, source_target_pairs={{0,4},{2,6},{4,0},{6,2},{1,5},{3,7},{5,1},{7,3},{8,12},{10,14},{12... | collective-permute-start | bytes 786440 | tf_op jit(solution)/shard_map/ppermute | solution.py:34
  107.7 6.4 %collective-permute-start.16 = (bf16[32,2048]{1,0:T(8,128)(2,1)S(1)}, bf16[32,2048]{1,0:T(8,128)(2,1)S(1)}, u32[]{:S(2)}, u32[]{:S(2)}) collective-permute-start(bf16[32,2048]{1,0:T(8,128)(2,1)S(1)} %get-tuple-element.94.refs_0_), channel_id=1, source_target_pairs={{0,2},{2,0},{4,6},{6,4},{1,3},{3,1},{5,7},{7,5},{8,10},{10,8},{12,... | collective-permute-start | bytes 393224 | tf_op jit(solution)/shard_map/ppermute | solution.py:34
  109.7 13.3 %collective-permute-start.30 = (bf16[64,1024]{1,0:T(8,128)(2,1)S(1)}, bf16[64,1024]{1,0:T(8,128)(2,1)S(1)}, u32[]{:S(2)}, u32[]{:S(2)}) collective-permute-start(bf16[64,1024]{1,0:T(8,128)(2,1)S(1)} %get-tuple-element.105.refs_2_.refs_4_), channel_id=1, source_target_pairs={{0,2},{2,0},{4,6},{6,4},{1,3},{3,1},{5,7},{7,5},{8,10},{10,8},{12,... | collective-permute-start | bytes 393224 | tf_op jit(solution)/shard_map/ppermute | solution.py:34
  110.8 12.9 %collective-permute-start.31 = (bf16[64,1024]{1,0:T(8,128)(2,1)S(1)}, bf16[64,1024]{1,0:T(8,128)(2,1)S(1)}, u32[]{:S(2)}, u32[]{:S(2)}) collective-permute-start(bf16[64,1024]{1,0:T(8,128)(2,1)S(1)} %get-tuple-element.112), channel_id=1, source_target_pairs={{0,4},{2,6},{4,0},{6,2},{1,5},{3,7},{5,1},{7,3},{8,12},{10,14},{12... | collective-permute-start | bytes 393224 | tf_op jit(solution)/shard_map/ppermute | solution.py:34
  112.3 11.4 %collective-permute-start.32 = (bf16[64,1024]{1,0:T(8,128)(2,1)S(1)}, bf16[64,1024]{1,0:T(8,128)(2,1)S(1)}, u32[]{:S(2)}, u32[]{:S(2)}) collective-permute-start(bf16[64,1024]{1,0:T(8,128)(2,1)S(1)} %get-tuple-element.113), channel_id=1, source_target_pairs={{0,6},{2,4},{4,2},{6,0},{1,7},{3,5},{5,3},{7,1},{8,14},{10,12},{12... | collective-permute-start | bytes 393224 | tf_op jit(solution)/shard_map/ppermute | solution.py:34
  115.1 6.0 %collective-permute-start.28 = (bf16[8,2048]{1,0:T(8,128)(2,1)S(1)}, bf16[8,2048]{1,0:T(8,128)(2,1)S(1)}, u32[]{:S(2)}, u32[]{:S(2)}) collective-permute-start(bf16[8,2048]{1,0:T(8,128)(2,1)S(1)} %get-tuple-element.108), channel_id=1, source_target_pairs={{0,16},{8,24},{16,0},{24,8},{1,17},{9,25},{17,1},{25,9},{2,18},{10... | collective-permute-start | bytes 98312 | tf_op jit(solution)/shard_map/ppermute | solution.py:34
  118.2 4.8 %collective-permute-start.29 = (bf16[8,2048]{1,0:T(8,128)(2,1)S(1)}, bf16[8,2048]{1,0:T(8,128)(2,1)S(1)}, u32[]{:S(2)}, u32[]{:S(2)}) collective-permute-start(bf16[8,2048]{1,0:T(8,128)(2,1)S(1)} %get-tuple-element.109), channel_id=1, source_target_pairs={{0,24},{8,16},{16,8},{24,0},{1,25},{9,17},{17,9},{25,1},{2,26},{10... | collective-permute-start | bytes 98312 | tf_op jit(solution)/shard_map/ppermute | solution.py:34
  124.6 7.7 %collective-permute-start.33 = (bf16[64,1024]{1,0:T(8,128)(2,1)S(1)}, bf16[64,1024]{1,0:T(8,128)(2,1)S(1)}, u32[]{:S(2)}, u32[]{:S(2)}) collective-permute-start(bf16[64,1024]{1,0:T(8,128)(2,1)S(1)} %get-tuple-element.117.refs_4_), channel_id=1, source_target_pairs={{0,8},{8,0},{16,24},{24,16},{1,9},{9,1},{17,25},{25,17},{2,10},{10... | collective-permute-start | bytes 393224 | tf_op jit(solution)/shard_map/ppermute | solution.py:34
  125.6 7.5 %collective-permute-start.34 = (bf16[64,1024]{1,0:T(8,128)(2,1)S(1)}, bf16[64,1024]{1,0:T(8,128)(2,1)S(1)}, u32[]{:S(2)}, u32[]{:S(2)}) collective-permute-start(bf16[64,1024]{1,0:T(8,128)(2,1)S(1)} %get-tuple-element.118), channel_id=1, source_target_pairs={{0,16},{8,24},{16,0},{24,8},{1,17},{9,25},{17,1},{25,9},{2,18},{10... | collective-permute-start | bytes 393224 | tf_op jit(solution)/shard_map/ppermute | solution.py:34
  126.7 6.4 %collective-permute-start.35 = (bf16[64,1024]{1,0:T(8,128)(2,1)S(1)}, bf16[64,1024]{1,0:T(8,128)(2,1)S(1)}, u32[]{:S(2)}, u32[]{:S(2)}) collective-permute-start(bf16[64,1024]{1,0:T(8,128)(2,1)S(1)} %get-tuple-element.119), channel_id=1, source_target_pairs={{0,24},{8,16},{16,8},{24,0},{1,25},{9,17},{17,9},{25,1},{2,26},{10... | collective-permute-start | bytes 393224 | tf_op jit(solution)/shard_map/ppermute | solution.py:34
  135.1 4.8 %collective-permute-start.37 = (bf16[8,2048]{1,0:T(8,128)(2,1)S(1)}, bf16[8,2048]{1,0:T(8,128)(2,1)S(1)}, u32[]{:S(2)}, u32[]{:S(2)}) collective-permute-start(bf16[8,2048]{1,0:T(8,128)(2,1)S(1)} %get-tuple-element.124), channel_id=1, source_target_pairs={{0,2},{2,0},{4,6},{6,4},{1,3},{3,1},{5,7},{7,5},{8,10},{10,8},{12,... | collective-permute-start | bytes 98312 | tf_op jit(solution)/shard_map/ppermute | solution.py:34
  137.4 5.4 %collective-permute-start.38 = (bf16[8,2048]{1,0:T(8,128)(2,1)S(1)}, bf16[8,2048]{1,0:T(8,128)(2,1)S(1)}, u32[]{:S(2)}, u32[]{:S(2)}) collective-permute-start(bf16[8,2048]{1,0:T(8,128)(2,1)S(1)} %get-tuple-element.125), channel_id=1, source_target_pairs={{0,4},{2,6},{4,0},{6,2},{1,5},{3,7},{5,1},{7,3},{8,12},{10,14},{12... | collective-permute-start | bytes 98312 | tf_op jit(solution)/shard_map/ppermute | solution.py:34
  138.1 5.7 %collective-permute-start.39 = (bf16[8,2048]{1,0:T(8,128)(2,1)S(1)}, bf16[8,2048]{1,0:T(8,128)(2,1)S(1)}, u32[]{:S(2)}, u32[]{:S(2)}) collective-permute-start(bf16[8,2048]{1,0:T(8,128)(2,1)S(1)} %get-tuple-element.126), channel_id=1, source_target_pairs={{0,6},{2,4},{4,2},{6,0},{1,7},{3,5},{5,3},{7,1},{8,14},{10,12},{12... | collective-permute-start | bytes 98312 | tf_op jit(solution)/shard_map/ppermute | solution.py:34
  (20 other events, 170.4 us)

commit v5 on v4

--- a/solution.py
+++ b/solution.py
@@ -255,7 +255,7 @@
         got = jnp.dot(sel[...], y_all[...], preferred_element_type=F32).astype(BF)
         y_sel[at : at + got.shape[0], :] = got
         at += got.shape[0]
-    wb = min(512, w.shape[1])
+    wb = min(1024, w.shape[1])
 
     @pl.loop(0, w.shape[1] // wb)
     def _(g):

time: 145 us -> 145 us (level)
  no operation moved by 1% of the time
where the time goes in v5:
time: 145 us
  Pallas kernels  61.6 us (42%)
  starting transfers between devices  44.6 us (31%)
  waiting for transfers between devices  34.6 us (24%)
  local copies, waits for them, and re-layouts  2.9 us (2%)
    ppermute x40, starting transfers between devices, trade(): return lax.ppermute(piece, axis, [(i, i ^ k) for i in range(size)])  44.6 us
    ppermute x40, waiting for transfers between devices, trade(): return lax.ppermute(piece, axis, [(i, i ^ k) for i in range(size)])  34.6 us
    pallas_call x1, Pallas kernels, body(): pl.pallas_call(functools.partial(gate_kernel, m), in_specs=[sm] + [vm] *...  17.3 us
    pallas_call x1, Pallas kernels, body(): pl.pallas_call(functools.partial(down_kernel, m, len(deps)), in_specs=[sm...  9.61 us
    pallas_call x1, Pallas kernels, body(): pl.pallas_call(functools.partial(load_kernel, chunks), in_specs=[pl.Block...  8.33 us
    pallas_call x2, Pallas kernels, ssm(): pl.pallas_call(functools.partial(ssm_kernel, first, groups, per, steps),...  5.96 us
    pallas_call x1, Pallas kernels, project(): pl.pallas_call(functools.partial(project_kernel, n), in_specs=[vm] * (n +...  5.44 us
    pallas_call x1, Pallas kernels, place(): pl.pallas_call(functools.partial(place_kernel, n, states), grid_spec=pltp...  4.1 us
  transfers between devices with their start and end apart: 40, of which 21 were waited for; matrix products, arithmetic and copies ran while one was open for 1% of the time, Pallas kernels for 26%

profile of v5, /device:TPU:0, one launch (start us, length us, event | category | flops | bytes accessed | tf_op | source)
XLA Modules:
  0.0 144.7 jit_solution(16262430440286962821)
XLA Ops:
  1.4 1.6 %pack.1 = (bf16[8,12544]{1,0:T(8,128)(2,1)S(1)}, bf16[8,12544]{1,0:T(8,128)(2,1)S(1)}, bf16[8,12544]{1,0:T(8,128)(2,1)S(1)}, bf16[8,12544]{1,0:T(8,128)(2,1)S(1)}) custom-call(s32[3]{0:T(128)S(1)} %pad_add_fusion.me.refs_0_, s32[1,4,8]{2,1,0:T(4,128)S(1)} %copy-done.5, bf16[2,32,2048]{2,1,0:T(8,128)(2,1)} %x.3, bf16[2,32,2048]{2,1,0:T(8,128)(2,1)} %z.1, ...), custom_call_target="tpu_custom_call" | custom-call | flops 1000000 | bytes 2097152 | tf_op jit(solution)/shard_map/pack/pallas_call | solution.py:642
  3.0 3.0 %collective-permute-start = (bf16[8,12544]{1,0:T(8,128)(2,1)S(1)}, bf16[8,12544]{1,0:T(8,128)(2,1)S(1)}, u32[]{:S(2)}, u32[]{:S(2)}) collective-permute-start(bf16[8,12544]{1,0:T(8,128)(2,1)S(1)} %get-tuple-element.72), channel_id=1, source_target_pairs={{0,8},{8,0},{16,24},{24,16},{1,9},{9,1},{17,25},{25,17},{2,10},{10... | collective-permute-start | bytes 602120 | tf_op jit(solution)/shard_map/ppermute | solution.py:34
  6.0 1.5 %collective-permute-start.1 = (bf16[8,12544]{1,0:T(8,128)(2,1)S(1)}, bf16[8,12544]{1,0:T(8,128)(2,1)S(1)}, u32[]{:S(2)}, u32[]{:S(2)}) collective-permute-start(bf16[8,12544]{1,0:T(8,128)(2,1)S(1)} %get-tuple-element.73), channel_id=1, source_target_pairs={{0,16},{8,24},{16,0},{24,8},{1,17},{9,25},{17,1},{25,9},{2,18},{10... | collective-permute-start | bytes 602120 | tf_op jit(solution)/shard_map/ppermute | solution.py:34
  7.5 1.5 %concatenate.3.refs_0_ = f32[8,2048]{1,0:T(8,128)} concatenate(f32[4,2048]{1,0:T(4,128)} %param.33, f32[1,2048]{1,0:T(1,128)} %bitcast.26, f32[1,2048]{1,0:T(1,128)} %bitcast.27, f32[1,2048]{1,0:T(1,128)} %bitcast.28, f32[1,2048]{1,0:T(1,128)S(1)} %broadcast_in_dim.15), dimensions={0} | concatenate | bytes 131072 | tf_op jit(solution)/shard_map/concatenate | solution.py:654
  9.0 2.6 %fetch.1 = (f32[8,2048]{1,0:T(8,128)S(1)}, f32[16,2048]{1,0:T(8,128)S(1)}, f32[3,32,2048]{2,1,0:T(8,128)S(1)}, f32[32,16,2048]{2,1,0:T(8,128)S(1)}) custom-call(f32[8,2048]{1,0:T(8,128)} %concatenate.3.refs_0_, f32[16,2048]{1,0:T(8,128)} %refs_1_.1, f32[3,32,2048]{2,1,0:T(8,128)} %bitcast.23, f32[32,16,2048]{2,1,0:T(8,128)} %refs_3_.1, ...), custom_call_target="tpu_custom_call" | custom-call | flops 100000 | bytes 4096 | tf_op jit(solution)/shard_map/fetch/pallas_call | solution.py:660
  12.3 1.9 %ssm0.1 = (bf16[16,2048]{1,0:T(8,128)(2,1)S(1)}, f32[144,2048]{1,0:T(8,128)S(1)}) custom-call(s32[3]{0:T(128)S(1)} %pad_add_fusion.me.refs_0_, s32[4,4,8]{2,1,0:T(4,128)S(1)} %copy-done.3, bf16[8,12544]{1,0:T(8,128)(2,1)S(1)} %get-tuple-element.66.refs_4_.refs_0_, f32[8,2048]{1,0:T(8,128)S(1)} %get-tuple-element.67.refs_1_.refs_4_, ...), custom_call_target="tpu_custom_call" | custom-call | flops 3000000 | bytes 3145728 | tf_op jit(solution)/shard_map/ssm0/pallas_call | solution.py:165
  14.2 2.5 %collective-permute-done.1.refs_2_ = bf16[8,12544]{1,0:T(8,128)(2,1)S(1)} collective-permute-done((bf16[8,12544]{1,0:T(8,128)(2,1)S(1)}, bf16[8,12544]{1,0:T(8,128)(2,1)S(1)}, u32[]{:S(2)}, u32[]{:S(2)}) %collective-permute-start.1) | collective-permute-done | bytes 200736 | tf_op jit(solution)/shard_map/ppermute | solution.py:34
  16.8 4.0 %ssm1.1 = (bf16[64,2048]{1,0:T(8,128)(2,1)S(1)}, bf16[144,2048]{1,0:T(8,128)(2,1)S(1)}, bf16[144,2048]{1,0:T(8,128)(2,1)S(1)}, bf16[144,2048]{1,0:T(8,128)(2,1)S(1)}) custom-call(s32[3]{0:T(128)S(1)} %pad_add_fusion.me.refs_0_, s32[4,4,8]{2,1,0:T(4,128)S(1)} %copy-done.3, bf16[16,2048]{1,0:T(8,128)(2,1)S(1)} %get-tuple-element.71.refs_0_, ...), custom_call_target="tpu_custom_call" | custom-call | flops 9000000 | bytes 9437184 | tf_op jit(solution)/shard_map/ssm1/pallas_call | solution.py:165
  23.0 1.4 %collective-permute-start.5 = (bf16[64,2048]{1,0:T(8,128)(2,1)S(1)}, bf16[64,2048]{1,0:T(8,128)(2,1)S(1)}, u32[]{:S(2)}, u32[]{:S(2)}) collective-permute-start(bf16[64,2048]{1,0:T(8,128)(2,1)S(1)} %get-tuple-element.75.refs_0_), channel_id=1, source_target_pairs={{0,24},{8,16},{16,8},{24,0},{1,25},{9,17},{17,9},{25,1},{2,26},{10... | collective-permute-start | bytes 786440 | tf_op jit(solution)/shard_map/ppermute | solution.py:34
  24.4 8.3 %load.1 = (bf16[8192,1536]{1,0:T(8,128)(2,1)S(1)}, f32[8,128]{1,0:T(8,128)S(1)}) custom-call(bf16[8192,1536]{1,0:T(8,128)(2,1)} %w.1, bf16[64,2048]{1,0:T(8,128)(2,1)S(1)} %get-tuple-element.75.refs_0_), custom_call_target="tpu_custom_call" | custom-call | flops 100000 | bytes 4096 | tf_op jit(solution)/shard_map/load/pallas_call | solution.py:704
  34.7 5.4 %project.1 = (bf16[128,2048]{1,0:T(8,128)(2,1)S(1)}, bf16[128,2048]{1,0:T(8,128)(2,1)S(1)}, bf16[128,2048]{1,0:T(8,128)(2,1)S(1)}, bf16[128,2048]{1,0:T(8,128)(2,1)S(1)}) custom-call(bf16[64,2048]{1,0:T(8,128)(2,1)S(1)} %get-tuple-element.75.refs_0_, bf16[64,2048]{1,0:T(8,128)(2,1)S(1)} %collective-permute-done.3.refs_1_, ...), custom_call_target="tpu_custom_call" | custom-call | flops 100000 | bytes 4096 | tf_op jit(solution)/shard_map/project/pallas_call | solution.py:275
  42.2 3.7 %collective-permute-start.10 = (bf16[32,2048]{1,0:T(8,128)(2,1)S(1)}, bf16[32,2048]{1,0:T(8,128)(2,1)S(1)}, u32[]{:S(2)}, u32[]{:S(2)}) collective-permute-start(bf16[32,2048]{1,0:T(8,128)(2,1)S(1)} %get-tuple-element.86), channel_id=1, source_target_pairs={{0,6},{2,4},{4,2},{6,0},{1,7},{3,5},{5,3},{7,1},{8,14},{10,12},{12... | collective-permute-start | bytes 393224 | tf_op jit(solution)/shard_map/ppermute | solution.py:34
  46.7 3.8 %collective-permute-done.10.refs_3_ = bf16[32,2048]{1,0:T(8,128)(2,1)S(1)} collective-permute-done((bf16[32,2048]{1,0:T(8,128)(2,1)S(1)}, bf16[32,2048]{1,0:T(8,128)(2,1)S(1)}, u32[]{:S(2)}, u32[]{:S(2)}) %collective-permute-start.10) | collective-permute-done | bytes 131104 | tf_op jit(solution)/shard_map/ppermute | solution.py:34
  50.5 3.1 %collective-permute-done.8.refs_1_ = bf16[32,2048]{1,0:T(8,128)(2,1)S(1)} collective-permute-done((bf16[32,2048]{1,0:T(8,128)(2,1)S(1)}, bf16[32,2048]{1,0:T(8,128)(2,1)S(1)}, u32[]{:S(2)}, u32[]{:S(2)}) %collective-permute-start.8) | collective-permute-done | bytes 131104 | tf_op jit(solution)/shard_map/ppermute | solution.py:34
  53.6 3.7 %collective-permute-done.9.refs_2_ = bf16[32,2048]{1,0:T(8,128)(2,1)S(1)} collective-permute-done((bf16[32,2048]{1,0:T(8,128)(2,1)S(1)}, bf16[32,2048]{1,0:T(8,128)(2,1)S(1)}, u32[]{:S(2)}, u32[]{:S(2)}) %collective-permute-start.9) | collective-permute-done | bytes 131104 | tf_op jit(solution)/shard_map/ppermute | solution.py:34
  59.2 1.7 %collective-permute-start.13 = (bf16[8,2048]{1,0:T(8,128)(2,1)S(1)}, bf16[8,2048]{1,0:T(8,128)(2,1)S(1)}, u32[]{:S(2)}, u32[]{:S(2)}) collective-permute-start(bf16[8,2048]{1,0:T(8,128)(2,1)S(1)} %get-tuple-element.90), channel_id=1, source_target_pairs={{0,24},{8,16},{16,8},{24,0},{1,25},{9,17},{17,9},{25,1},{2,26},{10... | collective-permute-start | bytes 98312 | tf_op jit(solution)/shard_map/ppermute | solution.py:34
  62.2 1.8 %collective-permute-done.13.refs_5_ = bf16[8,2048]{1,0:T(8,128)(2,1)S(1)} collective-permute-done((bf16[8,2048]{1,0:T(8,128)(2,1)S(1)}, bf16[8,2048]{1,0:T(8,128)(2,1)S(1)}, u32[]{:S(2)}, u32[]{:S(2)}) %collective-permute-start.13) | collective-permute-done | bytes 32800 | tf_op jit(solution)/shard_map/ppermute | solution.py:34
  64.8 3.0 %collective-permute-start.19 = (bf16[8,8192]{1,0:T(8,128)(2,1)S(1)}, bf16[8,8192]{1,0:T(8,128)(2,1)S(1)}, u32[]{:S(2)}, u32[]{:S(2)}) collective-permute-start(bf16[8,8192]{1,0:T(8,128)(2,1)S(1)} %norm.1.refs_0_), channel_id=1, source_target_pairs={{0,4},{2,6},{4,0},{6,2},{1,5},{3,7},{5,1},{7,3},{8,12},{10,14},{12... | collective-permute-start | bytes 393224 | tf_op jit(solution)/shard_map/ppermute | solution.py:34
  69.2 2.8 %collective-permute-done.14.refs_2_.refs_3_ = bf16[8,8192]{1,0:T(8,128)(2,1)S(1)} collective-permute-done((bf16[8,8192]{1,0:T(8,128)(2,1)S(1)}, bf16[8,8192]{1,0:T(8,128)(2,1)S(1)}, u32[]{:S(2)}, u32[]{:S(2)}) %collective-permute-start.14) | collective-permute-done | bytes 131104 | tf_op jit(solution)/shard_map/ppermute | solution.py:34
  80.1 17.3 %gate.1.act = bf16[64,1536]{1,0:T(8,128)(2,1)S(1)} custom-call(s32[3]{0:T(128)S(1)} %pad_add_fusion.me.refs_0_, bf16[8,8192]{1,0:T(8,128)(2,1)S(1)} %norm.1.refs_0_, bf16[8,8192]{1,0:T(8,128)(2,1)S(1)} %collective-permute-done.17.refs_1_, bf16[8,8192]{1,0:T(8,128)(2,1)S(1)} %collective-permute-done.14.refs_2_.refs_3_, ...), custom_call_target="tpu_custom_call" | custom-call | flops 3221225472 | bytes 50331648 | tf_op jit(solution)/shard_map/gate/pallas_call | solution.py:769
  97.6 9.6 %down.1 = (bf16[64,4096]{1,0:T(8,128)(2,1)S(1)}, bf16[64,4096]{1,0:T(8,128)(2,1)S(1)}) custom-call(s32[3]{0:T(128)S(1)} %pad_add_fusion.me.refs_0_, bf16[64,1536]{1,0:T(8,128)(2,1)S(1)} %gate.1.act, bf16[1536,8192]{1,0:T(8,128)(2,1)} %dw.1, bf16[32,2048]{1,0:T(8,128)(2,1)S(1)} %get-tuple-element.94.refs_0_, ...), custom_call_target="tpu_custom_call" | custom-call | flops 1610612736 | bytes 25165824 | tf_op jit(solution)/shard_map/down/pallas_call | solution.py:795
  110.4 1.5 %collective-permute-start.31 = (bf16[64,1024]{1,0:T(8,128)(2,1)S(1)}, bf16[64,1024]{1,0:T(8,128)(2,1)S(1)}, u32[]{:S(2)}, u32[]{:S(2)}) collective-permute-start(bf16[64,1024]{1,0:T(8,128)(2,1)S(1)} %get-tuple-element.112), channel_id=1, source_target_pairs={{0,4},{2,6},{4,0},{6,2},{1,5},{3,7},{5,1},{7,3},{8,12},{10,14},{12... | collective-permute-start | bytes 393224 | tf_op jit(solution)/shard_map/ppermute | solution.py:34
  111.9 1.9 %collective-permute-start.32 = (bf16[64,1024]{1,0:T(8,128)(2,1)S(1)}, bf16[64,1024]{1,0:T(8,128)(2,1)S(1)}, u32[]{:S(2)}, u32[]{:S(2)}) collective-permute-start(bf16[64,1024]{1,0:T(8,128)(2,1)S(1)} %get-tuple-element.113), channel_id=1, source_target_pairs={{0,6},{2,4},{4,2},{6,0},{1,7},{3,5},{5,3},{7,1},{8,14},{10,12},{12... | collective-permute-start | bytes 393224 | tf_op jit(solution)/shard_map/ppermute | solution.py:34
  115.9 1.9 %collective-permute-done.27.refs_7_.refs_2_ = bf16[8,2048]{1,0:T(8,128)(2,1)S(1)} collective-permute-done((bf16[8,2048]{1,0:T(8,128)(2,1)S(1)}, bf16[8,2048]{1,0:T(8,128)(2,1)S(1)}, u32[]{:S(2)}, u32[]{:S(2)}) %collective-permute-start.27) | collective-permute-done | bytes 32800 | tf_op jit(solution)/shard_map/ppermute | solution.py:34
  117.8 1.5 %collective-permute-start.29 = (bf16[8,2048]{1,0:T(8,128)(2,1)S(1)}, bf16[8,2048]{1,0:T(8,128)(2,1)S(1)}, u32[]{:S(2)}, u32[]{:S(2)}) collective-permute-start(bf16[8,2048]{1,0:T(8,128)(2,1)S(1)} %get-tuple-element.109), channel_id=1, source_target_pairs={{0,24},{8,16},{16,8},{24,0},{1,25},{9,17},{17,9},{25,1},{2,26},{10... | collective-permute-start | bytes 98312 | tf_op jit(solution)/shard_map/ppermute | solution.py:34
  119.3 1.5 %tail.1 = (f32[3,32,2048]{2,1,0:T(8,128)}, f32[8,128]{1,0:T(8,128)S(1)}) custom-call(s32[3]{0:T(128)S(1)} %pad_add_fusion.me.refs_0_, s32[1,4,8]{2,1,0:T(4,128)S(1)} %copy-done.6, bf16[2,32,2048]{2,1,0:T(8,128)(2,1)S(1)} %copy-done, f32[144,2048]{1,0:T(8,128)S(1)} %get-tuple-element.114.refs_0_, bf16[144,2048]{1,0:T(8,128)(2,1)S(1)} %collective-permute-done.23.refs_1_, ...), custom_call_target="tpu_custom_call" | custom-call | flops 100000 | bytes 4096 | tf_op jit(solution)/shard_map/tail/pallas_call | solution.py:814
  120.8 1.8 %collective-permute-done.29.refs_9_.refs_4_ = bf16[8,2048]{1,0:T(8,128)(2,1)S(1)} collective-permute-done((bf16[8,2048]{1,0:T(8,128)(2,1)S(1)}, bf16[8,2048]{1,0:T(8,128)(2,1)S(1)}, u32[]{:S(2)}, u32[]{:S(2)}) %collective-permute-start.29) | collective-permute-done | bytes 32800 | tf_op jit(solution)/shard_map/ppermute | solution.py:34
  126.4 1.5 %collective-permute-start.35 = (bf16[64,1024]{1,0:T(8,128)(2,1)S(1)}, bf16[64,1024]{1,0:T(8,128)(2,1)S(1)}, u32[]{:S(2)}, u32[]{:S(2)}) collective-permute-start(bf16[64,1024]{1,0:T(8,128)(2,1)S(1)} %get-tuple-element.119), channel_id=1, source_target_pairs={{0,24},{8,16},{16,8},{24,0},{1,25},{9,17},{17,9},{25,1},{2,26},{10... | collective-permute-start | bytes 393224 | tf_op jit(solution)/shard_map/ppermute | solution.py:34
  127.8 4.1 %place.1 = (f32[32,16,2048]{2,1,0:T(8,128)}, f32[8,128]{1,0:T(8,128)S(1)}) custom-call(s32[3]{0:T(128)S(1)} %pad_add_fusion.me.refs_0_, s32[1,4,8]{2,1,0:T(4,128)S(1)} %copy-done.6, f32[144,2048]{1,0:T(8,128)S(1)} %get-tuple-element.114.refs_0_, bf16[144,2048]{1,0:T(8,128)(2,1)S(1)} %collective-permute-done.23.refs_1_, ...), custom_call_target="tpu_custom_call" | custom-call | flops 100000 | bytes 4096 | tf_op jit(solution)/shard_map/place/pallas_call | solution.py:526
  134.7 2.3 %collective-permute-start.37 = (bf16[8,2048]{1,0:T(8,128)(2,1)S(1)}, bf16[8,2048]{1,0:T(8,128)(2,1)S(1)}, u32[]{:S(2)}, u32[]{:S(2)}) collective-permute-start(bf16[8,2048]{1,0:T(8,128)(2,1)S(1)} %get-tuple-element.124), channel_id=1, source_target_pairs={{0,2},{2,0},{4,6},{6,4},{1,3},{3,1},{5,7},{7,5},{8,10},{10,8},{12,... | collective-permute-start | bytes 98312 | tf_op jit(solution)/shard_map/ppermute | solution.py:34
  137.7 1.8 %collective-permute-start.39 = (bf16[8,2048]{1,0:T(8,128)(2,1)S(1)}, bf16[8,2048]{1,0:T(8,128)(2,1)S(1)}, u32[]{:S(2)}, u32[]{:S(2)}) collective-permute-start(bf16[8,2048]{1,0:T(8,128)(2,1)S(1)} %get-tuple-element.126), channel_id=1, source_target_pairs={{0,6},{2,4},{4,2},{6,0},{1,7},{3,5},{5,3},{7,1},{8,14},{10,12},{12... | collective-permute-start | bytes 98312 | tf_op jit(solution)/shard_map/ppermute | solution.py:34
  139.5 2.9 %collective-permute-done.38.refs_7_ = bf16[8,2048]{1,0:T(8,128)(2,1)S(1)} collective-permute-done((bf16[8,2048]{1,0:T(8,128)(2,1)S(1)}, bf16[8,2048]{1,0:T(8,128)(2,1)S(1)}, u32[]{:S(2)}, u32[]{:S(2)}) %collective-permute-start.38) | collective-permute-done | bytes 32800 | tf_op jit(solution)/shard_map/ppermute | solution.py:34
  (99 shorter events, 36.6 us)
Async XLA Ops:
  3.0 11.2 %collective-permute-start = (bf16[8,12544]{1,0:T(8,128)(2,1)S(1)}, bf16[8,12544]{1,0:T(8,128)(2,1)S(1)}, u32[]{:S(2)}, u32[]{:S(2)}) collective-permute-start(bf16[8,12544]{1,0:T(8,128)(2,1)S(1)} %get-tuple-element.72), channel_id=1, source_target_pairs={{0,8},{8,0},{16,24},{24,16},{1,9},{9,1},{17,25},{25,17},{2,10},{10... | collective-permute-start | bytes 602120 | tf_op jit(solution)/shard_map/ppermute | solution.py:34
  6.0 10.8 %collective-permute-start.1 = (bf16[8,12544]{1,0:T(8,128)(2,1)S(1)}, bf16[8,12544]{1,0:T(8,128)(2,1)S(1)}, u32[]{:S(2)}, u32[]{:S(2)}) collective-permute-start(bf16[8,12544]{1,0:T(8,128)(2,1)S(1)} %get-tuple-element.73), channel_id=1, source_target_pairs={{0,16},{8,24},{16,0},{24,8},{1,17},{9,25},{17,1},{25,9},{2,18},{10... | collective-permute-start | bytes 602120 | tf_op jit(solution)/shard_map/ppermute | solution.py:34
  7.5 9.2 %collective-permute-start.2 = (bf16[8,12544]{1,0:T(8,128)(2,1)S(1)}, bf16[8,12544]{1,0:T(8,128)(2,1)S(1)}, u32[]{:S(2)}, u32[]{:S(2)}) collective-permute-start(bf16[8,12544]{1,0:T(8,128)(2,1)S(1)} %get-tuple-element.74), channel_id=1, source_target_pairs={{0,24},{8,16},{16,8},{24,0},{1,25},{9,17},{17,9},{25,1},{2,26},{10... | collective-permute-start | bytes 602120 | tf_op jit(solution)/shard_map/ppermute | solution.py:34
  20.9 13.0 %collective-permute-start.3 = (bf16[64,2048]{1,0:T(8,128)(2,1)S(1)}, bf16[64,2048]{1,0:T(8,128)(2,1)S(1)}, u32[]{:S(2)}, u32[]{:S(2)}) collective-permute-start(bf16[64,2048]{1,0:T(8,128)(2,1)S(1)} %get-tuple-element.75.refs_0_), channel_id=1, source_target_pairs={{0,8},{8,0},{16,24},{24,16},{1,9},{9,1},{17,25},{25,17},{2,10},{10... | collective-permute-start | bytes 786440 | tf_op jit(solution)/shard_map/ppermute | solution.py:34
  22.2 12.5 %collective-permute-start.4 = (bf16[64,2048]{1,0:T(8,128)(2,1)S(1)}, bf16[64,2048]{1,0:T(8,128)(2,1)S(1)}, u32[]{:S(2)}, u32[]{:S(2)}) collective-permute-start(bf16[64,2048]{1,0:T(8,128)(2,1)S(1)} %get-tuple-element.75.refs_0_), channel_id=1, source_target_pairs={{0,16},{8,24},{16,0},{24,8},{1,17},{9,25},{17,1},{25,9},{2,18},{10... | collective-permute-start | bytes 786440 | tf_op jit(solution)/shard_map/ppermute | solution.py:34
  23.0 11.7 %collective-permute-start.5 = (bf16[64,2048]{1,0:T(8,128)(2,1)S(1)}, bf16[64,2048]{1,0:T(8,128)(2,1)S(1)}, u32[]{:S(2)}, u32[]{:S(2)}) collective-permute-start(bf16[64,2048]{1,0:T(8,128)(2,1)S(1)} %get-tuple-element.75.refs_0_), channel_id=1, source_target_pairs={{0,24},{8,16},{16,8},{24,0},{1,25},{9,17},{17,9},{25,1},{2,26},{10... | collective-permute-start | bytes 786440 | tf_op jit(solution)/shard_map/ppermute | solution.py:34
  40.2 34.0 %collective-permute-start.6 = (bf16[128,2048]{1,0:T(8,128)(2,1)S(1)}, bf16[128,2048]{1,0:T(8,128)(2,1)S(1)}, u32[]{:S(2)}, u32[]{:S(2)}) collective-permute-start(bf16[128,2048]{1,0:T(8,128)(2,1)S(1)} %get-tuple-element.80), channel_id=1, source_target_pairs={{0,1},{1,0},{2,3},{3,2},{4,5},{5,4},{6,7},{7,6},{8,9},{9,8},{10,11... | collective-permute-start | bytes 1572872 | tf_op jit(solution)/shard_map/ppermute | solution.py:34
  42.2 8.2 %collective-permute-start.10 = (bf16[32,2048]{1,0:T(8,128)(2,1)S(1)}, bf16[32,2048]{1,0:T(8,128)(2,1)S(1)}, u32[]{:S(2)}, u32[]{:S(2)}) collective-permute-start(bf16[32,2048]{1,0:T(8,128)(2,1)S(1)} %get-tuple-element.86), channel_id=1, source_target_pairs={{0,6},{2,4},{4,2},{6,0},{1,7},{3,5},{5,3},{7,1},{8,14},{10,12},{12... | collective-permute-start | bytes 393224 | tf_op jit(solution)/shard_map/ppermute | solution.py:34
  45.9 7.7 %collective-permute-start.8 = (bf16[32,2048]{1,0:T(8,128)(2,1)S(1)}, bf16[32,2048]{1,0:T(8,128)(2,1)S(1)}, u32[]{:S(2)}, u32[]{:S(2)}) collective-permute-start(bf16[32,2048]{1,0:T(8,128)(2,1)S(1)} %get-tuple-element.84), channel_id=1, source_target_pairs={{0,2},{2,0},{4,6},{6,4},{1,3},{3,1},{5,7},{7,5},{8,10},{10,8},{12,... | collective-permute-start | bytes 393224 | tf_op jit(solution)/shard_map/ppermute | solution.py:34
  45.9 11.4 %collective-permute-start.9 = (bf16[32,2048]{1,0:T(8,128)(2,1)S(1)}, bf16[32,2048]{1,0:T(8,128)(2,1)S(1)}, u32[]{:S(2)}, u32[]{:S(2)}) collective-permute-start(bf16[32,2048]{1,0:T(8,128)(2,1)S(1)} %get-tuple-element.85), channel_id=1, source_target_pairs={{0,4},{2,6},{4,0},{6,2},{1,5},{3,7},{5,1},{7,3},{8,12},{10,14},{12... | collective-permute-start | bytes 393224 | tf_op jit(solution)/shard_map/ppermute | solution.py:34
  57.4 4.1 %collective-permute-start.11 = (bf16[8,2048]{1,0:T(8,128)(2,1)S(1)}, bf16[8,2048]{1,0:T(8,128)(2,1)S(1)}, u32[]{:S(2)}, u32[]{:S(2)}) collective-permute-start(bf16[8,2048]{1,0:T(8,128)(2,1)S(1)} %get-tuple-element.88), channel_id=1, source_target_pairs={{0,8},{8,0},{16,24},{24,16},{1,9},{9,1},{17,25},{25,17},{2,10},{10... | collective-permute-start | bytes 98312 | tf_op jit(solution)/shard_map/ppermute | solution.py:34
  58.0 4.2 %collective-permute-start.12 = (bf16[8,2048]{1,0:T(8,128)(2,1)S(1)}, bf16[8,2048]{1,0:T(8,128)(2,1)S(1)}, u32[]{:S(2)}, u32[]{:S(2)}) collective-permute-start(bf16[8,2048]{1,0:T(8,128)(2,1)S(1)} %get-tuple-element.89), channel_id=1, source_target_pairs={{0,16},{8,24},{16,0},{24,8},{1,17},{9,25},{17,1},{25,9},{2,18},{10... | collective-permute-start | bytes 98312 | tf_op jit(solution)/shard_map/ppermute | solution.py:34
  59.2 4.8 %collective-permute-start.13 = (bf16[8,2048]{1,0:T(8,128)(2,1)S(1)}, bf16[8,2048]{1,0:T(8,128)(2,1)S(1)}, u32[]{:S(2)}, u32[]{:S(2)}) collective-permute-start(bf16[8,2048]{1,0:T(8,128)(2,1)S(1)} %get-tuple-element.90), channel_id=1, source_target_pairs={{0,24},{8,16},{16,8},{24,0},{1,25},{9,17},{17,9},{25,1},{2,26},{10... | collective-permute-start | bytes 98312 | tf_op jit(solution)/shard_map/ppermute | solution.py:34
  64.7 7.2 %collective-permute-start.14 = (bf16[8,8192]{1,0:T(8,128)(2,1)S(1)}, bf16[8,8192]{1,0:T(8,128)(2,1)S(1)}, u32[]{:S(2)}, u32[]{:S(2)}) collective-permute-start(bf16[8,8192]{1,0:T(8,128)(2,1)S(1)} %norm.1.refs_0_), channel_id=1, source_target_pairs={{0,2},{2,0},{4,6},{6,4},{1,3},{3,1},{5,7},{7,5},{8,10},{10,8},{12,... | collective-permute-start | bytes 393224 | tf_op jit(solution)/shard_map/ppermute | solution.py:34
  64.8 11.3 %collective-permute-start.19 = (bf16[8,8192]{1,0:T(8,128)(2,1)S(1)}, bf16[8,8192]{1,0:T(8,128)(2,1)S(1)}, u32[]{:S(2)}, u32[]{:S(2)}) collective-permute-start(bf16[8,8192]{1,0:T(8,128)(2,1)S(1)} %norm.1.refs_0_), channel_id=1, source_target_pairs={{0,4},{2,6},{4,0},{6,2},{1,5},{3,7},{5,1},{7,3},{8,12},{10,14},{12... | collective-permute-start | bytes 393224 | tf_op jit(solution)/shard_map/ppermute | solution.py:34
  67.8 8.3 %collective-permute-start.21 = (bf16[8,8192]{1,0:T(8,128)(2,1)S(1)}, bf16[8,8192]{1,0:T(8,128)(2,1)S(1)}, u32[]{:S(2)}, u32[]{:S(2)}) collective-permute-start(bf16[8,8192]{1,0:T(8,128)(2,1)S(1)} %norm.1.refs_0_), channel_id=1, source_target_pairs={{0,6},{2,4},{4,2},{6,0},{1,7},{3,5},{5,3},{7,1},{8,14},{10,12},{12... | collective-permute-start | bytes 393224 | tf_op jit(solution)/shard_map/ppermute | solution.py:34
  71.9 25.6 %collective-permute-start.23 = (bf16[144,2048]{1,0:T(8,128)(2,1)S(1)}, bf16[144,2048]{1,0:T(8,128)(2,1)S(1)}, u32[]{:S(2)}, u32[]{:S(2)}) collective-permute-start(bf16[144,2048]{1,0:T(8,128)(2,1)S(1)} %get-tuple-element.100), channel_id=1, source_target_pairs={{0,8},{8,0},{16,24},{24,16},{1,9},{9,1},{17,25},{25,17},{2,10},{10... | collective-permute-start | bytes 1769480 | tf_op jit(solution)/shard_map/ppermute | solution.py:34
  73.0 24.6 %collective-permute-start.24 = (bf16[144,2048]{1,0:T(8,128)(2,1)S(1)}, bf16[144,2048]{1,0:T(8,128)(2,1)S(1)}, u32[]{:S(2)}, u32[]{:S(2)}) collective-permute-start(bf16[144,2048]{1,0:T(8,128)(2,1)S(1)} %get-tuple-element.101), channel_id=1, source_target_pairs={{0,16},{8,24},{16,0},{24,8},{1,17},{9,25},{17,1},{25,9},{2,18},{10... | collective-permute-start | bytes 1769480 | tf_op jit(solution)/shard_map/ppermute | solution.py:34
  74.3 23.3 %collective-permute-start.25 = (bf16[144,2048]{1,0:T(8,128)(2,1)S(1)}, bf16[144,2048]{1,0:T(8,128)(2,1)S(1)}, u32[]{:S(2)}, u32[]{:S(2)}) collective-permute-start(bf16[144,2048]{1,0:T(8,128)(2,1)S(1)} %get-tuple-element.102), channel_id=1, source_target_pairs={{0,24},{8,16},{16,8},{24,0},{1,25},{9,17},{17,9},{25,1},{2,26},{10... | collective-permute-start | bytes 1769480 | tf_op jit(solution)/shard_map/ppermute | solution.py:34
  78.7 18.7 %collective-permute-start.15 = (bf16[64,2048]{1,0:T(8,128)(2,1)S(1)}, bf16[64,2048]{1,0:T(8,128)(2,1)S(1)}, u32[]{:S(2)}, u32[]{:S(2)}) collective-permute-start(bf16[64,2048]{1,0:T(8,128)(2,1)S(1)} %get-tuple-element.92), channel_id=1, source_target_pairs={{0,4},{2,6},{4,0},{6,2},{1,5},{3,7},{5,1},{7,3},{8,12},{10,14},{12... | collective-permute-start | bytes 786440 | tf_op jit(solution)/shard_map/ppermute | solution.py:34
  107.4 6.4 %collective-permute-start.16 = (bf16[32,2048]{1,0:T(8,128)(2,1)S(1)}, bf16[32,2048]{1,0:T(8,128)(2,1)S(1)}, u32[]{:S(2)}, u32[]{:S(2)}) collective-permute-start(bf16[32,2048]{1,0:T(8,128)(2,1)S(1)} %get-tuple-element.94.refs_0_), channel_id=1, source_target_pairs={{0,2},{2,0},{4,6},{6,4},{1,3},{3,1},{5,7},{7,5},{8,10},{10,8},{12,... | collective-permute-start | bytes 393224 | tf_op jit(solution)/shard_map/ppermute | solution.py:34
  109.3 13.3 %collective-permute-start.30 = (bf16[64,1024]{1,0:T(8,128)(2,1)S(1)}, bf16[64,1024]{1,0:T(8,128)(2,1)S(1)}, u32[]{:S(2)}, u32[]{:S(2)}) collective-permute-start(bf16[64,1024]{1,0:T(8,128)(2,1)S(1)} %get-tuple-element.105.refs_2_.refs_4_), channel_id=1, source_target_pairs={{0,2},{2,0},{4,6},{6,4},{1,3},{3,1},{5,7},{7,5},{8,10},{10,8},{12,... | collective-permute-start | bytes 393224 | tf_op jit(solution)/shard_map/ppermute | solution.py:34
  110.4 12.9 %collective-permute-start.31 = (bf16[64,1024]{1,0:T(8,128)(2,1)S(1)}, bf16[64,1024]{1,0:T(8,128)(2,1)S(1)}, u32[]{:S(2)}, u32[]{:S(2)}) collective-permute-start(bf16[64,1024]{1,0:T(8,128)(2,1)S(1)} %get-tuple-element.112), channel_id=1, source_target_pairs={{0,4},{2,6},{4,0},{6,2},{1,5},{3,7},{5,1},{7,3},{8,12},{10,14},{12... | collective-permute-start | bytes 393224 | tf_op jit(solution)/shard_map/ppermute | solution.py:34
  111.9 11.4 %collective-permute-start.32 = (bf16[64,1024]{1,0:T(8,128)(2,1)S(1)}, bf16[64,1024]{1,0:T(8,128)(2,1)S(1)}, u32[]{:S(2)}, u32[]{:S(2)}) collective-permute-start(bf16[64,1024]{1,0:T(8,128)(2,1)S(1)} %get-tuple-element.113), channel_id=1, source_target_pairs={{0,6},{2,4},{4,2},{6,0},{1,7},{3,5},{5,3},{7,1},{8,14},{10,12},{12... | collective-permute-start | bytes 393224 | tf_op jit(solution)/shard_map/ppermute | solution.py:34
  114.8 6.0 %collective-permute-start.28 = (bf16[8,2048]{1,0:T(8,128)(2,1)S(1)}, bf16[8,2048]{1,0:T(8,128)(2,1)S(1)}, u32[]{:S(2)}, u32[]{:S(2)}) collective-permute-start(bf16[8,2048]{1,0:T(8,128)(2,1)S(1)} %get-tuple-element.108), channel_id=1, source_target_pairs={{0,16},{8,24},{16,0},{24,8},{1,17},{9,25},{17,1},{25,9},{2,18},{10... | collective-permute-start | bytes 98312 | tf_op jit(solution)/shard_map/ppermute | solution.py:34
  117.8 4.8 %collective-permute-start.29 = (bf16[8,2048]{1,0:T(8,128)(2,1)S(1)}, bf16[8,2048]{1,0:T(8,128)(2,1)S(1)}, u32[]{:S(2)}, u32[]{:S(2)}) collective-permute-start(bf16[8,2048]{1,0:T(8,128)(2,1)S(1)} %get-tuple-element.109), channel_id=1, source_target_pairs={{0,24},{8,16},{16,8},{24,0},{1,25},{9,17},{17,9},{25,1},{2,26},{10... | collective-permute-start | bytes 98312 | tf_op jit(solution)/shard_map/ppermute | solution.py:34
  124.3 7.7 %collective-permute-start.33 = (bf16[64,1024]{1,0:T(8,128)(2,1)S(1)}, bf16[64,1024]{1,0:T(8,128)(2,1)S(1)}, u32[]{:S(2)}, u32[]{:S(2)}) collective-permute-start(bf16[64,1024]{1,0:T(8,128)(2,1)S(1)} %get-tuple-element.117.refs_4_), channel_id=1, source_target_pairs={{0,8},{8,0},{16,24},{24,16},{1,9},{9,1},{17,25},{25,17},{2,10},{10... | collective-permute-start | bytes 393224 | tf_op jit(solution)/shard_map/ppermute | solution.py:34
  125.2 7.5 %collective-permute-start.34 = (bf16[64,1024]{1,0:T(8,128)(2,1)S(1)}, bf16[64,1024]{1,0:T(8,128)(2,1)S(1)}, u32[]{:S(2)}, u32[]{:S(2)}) collective-permute-start(bf16[64,1024]{1,0:T(8,128)(2,1)S(1)} %get-tuple-element.118), channel_id=1, source_target_pairs={{0,16},{8,24},{16,0},{24,8},{1,17},{9,25},{17,1},{25,9},{2,18},{10... | collective-permute-start | bytes 393224 | tf_op jit(solution)/shard_map/ppermute | solution.py:34
  126.4 6.4 %collective-permute-start.35 = (bf16[64,1024]{1,0:T(8,128)(2,1)S(1)}, bf16[64,1024]{1,0:T(8,128)(2,1)S(1)}, u32[]{:S(2)}, u32[]{:S(2)}) collective-permute-start(bf16[64,1024]{1,0:T(8,128)(2,1)S(1)} %get-tuple-element.119), channel_id=1, source_target_pairs={{0,24},{8,16},{16,8},{24,0},{1,25},{9,17},{17,9},{25,1},{2,26},{10... | collective-permute-start | bytes 393224 | tf_op jit(solution)/shard_map/ppermute | solution.py:34
  134.7 4.8 %collective-permute-start.37 = (bf16[8,2048]{1,0:T(8,128)(2,1)S(1)}, bf16[8,2048]{1,0:T(8,128)(2,1)S(1)}, u32[]{:S(2)}, u32[]{:S(2)}) collective-permute-start(bf16[8,2048]{1,0:T(8,128)(2,1)S(1)} %get-tuple-element.124), channel_id=1, source_target_pairs={{0,2},{2,0},{4,6},{6,4},{1,3},{3,1},{5,7},{7,5},{8,10},{10,8},{12,... | collective-permute-start | bytes 98312 | tf_op jit(solution)/shard_map/ppermute | solution.py:34
  137.0 5.4 %collective-permute-start.38 = (bf16[8,2048]{1,0:T(8,128)(2,1)S(1)}, bf16[8,2048]{1,0:T(8,128)(2,1)S(1)}, u32[]{:S(2)}, u32[]{:S(2)}) collective-permute-start(bf16[8,2048]{1,0:T(8,128)(2,1)S(1)} %get-tuple-element.125), channel_id=1, source_target_pairs={{0,4},{2,6},{4,0},{6,2},{1,5},{3,7},{5,1},{7,3},{8,12},{10,14},{12... | collective-permute-start | bytes 98312 | tf_op jit(solution)/shard_map/ppermute | solution.py:34
  137.7 5.7 %collective-permute-start.39 = (bf16[8,2048]{1,0:T(8,128)(2,1)S(1)}, bf16[8,2048]{1,0:T(8,128)(2,1)S(1)}, u32[]{:S(2)}, u32[]{:S(2)}) collective-permute-start(bf16[8,2048]{1,0:T(8,128)(2,1)S(1)} %get-tuple-element.126), channel_id=1, source_target_pairs={{0,6},{2,4},{4,2},{6,0},{1,7},{3,5},{5,3},{7,1},{8,14},{10,12},{12... | collective-permute-start | bytes 98312 | tf_op jit(solution)/shard_map/ppermute | solution.py:34
  (20 other events, 170.2 us)
